TPU v7x, 32 devices: a whole 2x2x4 slice. The times are simulated.
32 devices in a mesh: lat: 4 (over y, core), lon: 8 (over z, x).
Axes of the slice: x: 2, y: 2, z: 4, core: 2. Of those that a mesh axis runs over, the one named last changes fastest.
Arguments:
- ensemble: bfloat16 [8, 4, 16, 384, 128], P(None, None, 'lat', 'lon'), may hold values from -5 to 5
- vert_loc: float32 [128, 128], replicated, may hold values from -0.5 to 0.5
- static_vert: float32 [128, 128], replicated, may hold values from -0.5 to 0.5
- inst_vert: float32 [16, 128], replicated, may hold values from -0.5 to 0.5
- inst_err: float32 [16], replicated, may hold values from 0.5 to 2
- obs_dest: int32 [8192, 1], P(('lat', 'lon')), may hold values from 0 to 31; in each aligned block of 256 rows (0 to 255, 256 to 511, ...) at most 16 rows name the same one
- obs_patch: int32 [8192], P(('lat', 'lon')), may hold values from 0 to 47
- obs_window: int32 [8192], P(('lat', 'lon')), may hold values from 0 to 3
- obs_inst: int32 [8192], P(('lat', 'lon')), may hold values from 0 to 15
- obs_hweight: float32 [4, 8192], P(None, ('lat', 'lon')), may hold values from 0 to 0.5
- innovation: float32 [8192], P(('lat', 'lon')), may hold values from -6 to 6
- obs_count: int32 [32], P(('lat', 'lon')), may hold values from 128 to 256, as said below
Outputs:
- static_control: float32 [16, 384, 128], P('lat', 'lon')
- member_control: float32 [8, 16, 384, 128], P(None, 'lat', 'lon')
- obs_equivalent: float32 [8192], P(('lat', 'lon'))
Inputs may be any that keep to these rules, and one draw needn't show every extreme that they name: `obs_dest`: index of the tile in lat+lon order (lat slowest) that holds the row's patch; within the rows of one shard no tile is named more than 16 times. `obs_patch`: patch p of a tile covers its latitude rows 2 (p // 24) and the next, and its longitude columns 2 (p % 24) and the next. `obs_count`: some shard uses all 256 rows in every draw; rows at or past a shard's count are unused.
All inputs are finite; a program needn't handle non-finite values.
Results may differ from a plain program's by a relative error of at most 0.0003.
Values sent between devices are 32-bit elements; how exact they have to be, the bound alone decides.
No kernel may reach another device: no remote copies, remote signals or barrier semaphores. Data moves between devices by JAX's collectives and lax.ppermute only.
A program may use at most 64 MiB of HBM per device.

v0:
```python
import functools

import jax
import jax.numpy as jnp
from jax import lax
from jax.experimental import pallas as pl
from jax.experimental.pallas import tpu as pltpu
from jax.sharding import PartitionSpec as P

SMOOTH = 0.15
CENTER = 1.0 - 4.0 * SMOOTH
BETA_STATIC = 0.5
BETA_ENSEMBLE = 0.85
HALO = 4
LANES = 128
HIGHEST = lax.Precision.HIGHEST
F32 = jnp.float32

ANY = pl.BlockSpec(memory_space=pl.ANY)
VMEM = pl.BlockSpec(memory_space=pltpu.VMEM)
SMEM = pl.BlockSpec(memory_space=pltpu.SMEM)
PARAMS = pltpu.CompilerParams(vmem_limit_bytes=48 * 1024 * 1024)


def dot(left, right, dims=((1,), (0,))):
    return lax.dot_general(
        left, right, (dims, ((), ())), precision=HIGHEST, preferred_element_type=F32
    )


def iota(shape, dim):
    return lax.broadcasted_iota(jnp.int32, shape, dim)


def pack_kernel(
    slots, patches, dest_col, dest, patch, window, inst, hweight, innov, count, send, lane, feat
):
    owners = send.shape[0]
    rows = dest.shape[1]
    me = lax.axis_index("lat") * lax.axis_size("lon") + lax.axis_index("lon")
    base = lax.rem(me, LANES // slots) * slots
    destination = dest[...]
    earlier = (dest_col[...] == destination) & (iota((rows, rows), 0) < iota((rows, rows), 1))
    ranking = jnp.sum(jnp.where(earlier, 1.0, 0.0), axis=0, keepdims=True).astype(jnp.int32)
    position = ranking + base
    lane[...] = position
    active = (iota((1, rows), 1) < count[0]).astype(F32)
    feat[...] = jnp.zeros_like(feat)
    feat[0:1] = (window[...] * patches + patch[...]).astype(F32)
    feat[1:2] = inst[...].astype(F32)
    feat[2:6] = hweight[...] * active
    feat[6:7] = innov[...]
    chosen = iota((owners, 8, rows), 0) == destination.reshape(1, 1, rows)
    spread_out = jnp.where(chosen, feat[...][None], 0.0).reshape(owners * 8, rows)
    at_lane = (iota((LANES, rows), 0) == position).astype(F32)
    send[...] = dot(spread_out, at_lane, ((1,), (1,))).reshape(owners, 8, LANES)


def prepare_kernel(vert_loc, static_vert, squares):
    squares[0] = BETA_ENSEMBLE**2 * dot(vert_loc[...], vert_loc[...], ((0,), (0,)))
    squares[1] = BETA_STATIC**2 * dot(static_vert[...], static_vert[...], ((0,), (0,)))


def fill_weights(feat, weights, windows, rows_lat, rows_lon):
    slots = feat.shape[1]
    cell = feat[0:1].astype(jnp.int32)
    half = iota((rows_lon, slots), 0) >> 1
    odd = (iota((rows_lon, slots), 0) & 1) == 1
    corner = [jnp.where(odd, feat[3 + 2 * q : 4 + 2 * q], feat[2 + 2 * q : 3 + 2 * q]) for q in range(2)]
    per_window = rows_lat // 2 * (rows_lon // 2)
    for t in range(windows):
        for a in range(rows_lat):
            first = t * per_window + a // 2 * (rows_lon // 2)
            row = (t * rows_lat + a) * rows_lon
            weights[row : row + rows_lon] = jnp.where(half == cell - first, corner[a % 2], 0.0)


def adjoint_fields(amount, weights, ivert, ens, grad, fields, edge_a, edge_b):
    members, windows, rows_lat, rows_lon, levels = ens.shape
    block = rows_lat * rows_lon
    scaled = ivert[...] * amount
    for t in range(windows):
        rows = slice(t * block, (t + 1) * block)
        grad[rows] = dot(weights[rows], scaled, ((1,), (1,)))
    even = lax.rem(lax.axis_index("lon"), 2) == 0
    upper = iota((8, levels), 0) >= 4

    def put(k, a, value):
        fields[k, a] = value
        east = jnp.where(upper, value[rows_lon - 8 :], 0.0)
        west = jnp.where(upper, 0.0, value[:8])
        edge_a[k, a] = jnp.where(even, east, west)
        edge_b[k, a] = jnp.where(even, west, east)

    for a in range(rows_lat):
        parts = [grad[
            (t * rows_lat + a) * rows_lon : (t * rows_lat + a + 1) * rows_lon
        ] for t in range(windows)]
        for k in range(members):
            total = ens[k, 0, a].astype(F32) * parts[0]
            for t in range(1, windows):
                total = total + ens[k, t, a].astype(F32) * parts[t]
            put(k, a, total)
        total = parts[0]
        for t in range(1, windows):
            total = total + parts[t]
        put(members, a, total)


def first_kernel(
    slots,
    recv,
    inst_vert,
    inst_err,
    ens_hbm,
    feat,
    ivert,
    fields,
    edge_a,
    edge_b,
    ens,
    weights,
    grad,
    sem,
):
    copy = pltpu.make_async_copy(ens_hbm, ens, sem)
    copy.start()
    members, windows, rows_lat, rows_lon, levels = ens.shape
    owners = recv.shape[0]
    per = LANES // slots
    for g in range(owners // per):
        feat[:, g * LANES : (g + 1) * LANES] = jnp.sum(recv[g * per : (g + 1) * per], axis=0)
    instruments = inst_vert.shape[0]
    total = feat.shape[1]
    onehot = (iota((instruments, total), 0) == feat[1:2].astype(jnp.int32)).astype(F32)
    ivert[...] = dot(inst_vert[...].T, onehot)
    inverse = jnp.broadcast_to(1.0 / (inst_err[...] * inst_err[...]), (8, instruments))
    rinv = dot(inverse, onehot)[0:1]
    feat[6:7] = feat[6:7] * rinv
    feat[7:8] = rinv
    fill_weights(feat, weights, windows, rows_lat, rows_lon)
    copy.wait()
    adjoint_fields(feat[6:7], weights, ivert, ens, grad, fields, edge_a, edge_b)


def halo_copies(own, lat_a, lat_b, cross, corner_a, corner_b, field, sems):
    rows_lat, rows_lon = own.shape[1:3]
    odd = lax.rem(lax.axis_index("lat"), 2)
    south = HALO + rows_lat
    row_a = south * (1 - odd)
    row_b = south * odd
    far_a = (rows_lat - HALO) * odd
    far_b = (rows_lat - HALO) * (1 - odd)
    main = pl.ds(0, rows_lon)
    side = pl.ds(rows_lon, 8)
    mid = pl.ds(HALO, rows_lat)
    plan = (
        (own, field.at[:, mid, main]),
        (cross, field.at[:, mid, side]),
        (lat_a.at[:, pl.ds(far_a, HALO)], field.at[:, pl.ds(row_a, HALO), main]),
        (lat_b.at[:, pl.ds(far_b, HALO)], field.at[:, pl.ds(row_b, HALO), main]),
        (corner_a.at[:, pl.ds(far_a, HALO)], field.at[:, pl.ds(row_a, HALO), side]),
        (corner_b.at[:, pl.ds(far_b, HALO)], field.at[:, pl.ds(row_b, HALO), side]),
    )
    return [pltpu.make_async_copy(s, d, sems.at[n]) for n, (s, d) in enumerate(plan)]


def smooth_power(field, powers, out, order):
    count, rows, width, levels = field.shape
    rows_lat = rows - 2 * HALO
    rows_lon = width - 8
    lat = lax.axis_index("lat")
    north = (lat > 0).astype(F32)
    south = (lat < lax.axis_size("lat") - 1).astype(F32)
    factor = {2: (2.0, 1.0), 4: (4.0, 6.0, 4.0, 1.0)}[order]

    def one(k, carry):
        for c in range(width // 8):
            cols = slice(8 * c, 8 * c + 8)
            low = HALO - order
            line = {i: field[k, i, cols] for i in range(low, rows - low)}
            for m in range(1, order + 1):
                fresh = {}
                for i in range(low + m, rows - low - m):
                    value = line[i - 1] + line[i + 1]
                    if i < HALO:
                        value = value * north
                    if i >= HALO + rows_lat:
                        value = value * south
                    fresh[i] = value
                line = fresh
                for i in range(rows_lat):
                    powers[m - 1, i, cols] = line[HALO + i]
        for i in range(rows_lat):
            value = field[k, HALO + i]
            for m in range(1, order + 1):
                ring = pltpu.roll(value, 1, 0) + pltpu.roll(value, width - 1, 0)
                value = CENTER * value + SMOOTH * ring
                value = value + (factor[m - 1] * SMOOTH**m) * powers[m - 1, i]
            out[k, i] = value[:rows_lon]
        return carry

    lax.fori_loop(0, count, one, 0)


def observe(field, powers, smooth, mixed, squares, ivert, weights, ens, ens_copy):
    members, windows, rows_lat, rows_lon, levels = ens.shape
    block = rows_lat * rows_lon
    smooth_power(field, powers, smooth, 4)
    shape = (rows_lat, rows_lon, levels)
    for k in range(members + 1):
        square = squares[0] if k < members else squares[1]
        mixed[k] = dot(smooth[k].reshape(block, levels), square).reshape(shape)
    ens_copy.wait()
    slots = weights.shape[1]
    image = jnp.zeros((8, slots), F32)
    for t in range(windows):
        lines = []
        for a in range(rows_lat):
            total = mixed[members, a]
            for k in range(members):
                total = total + ens[k, t, a].astype(F32) * mixed[k, a]
            lines.append(total)
        increment = jnp.stack(lines).reshape(block, levels)
        seen = dot(increment, ivert[...]) * weights[t * block : (t + 1) * block]
        image = image + jnp.sum(seen.reshape(block // 8, 8, slots), axis=0)
    return jnp.sum(image, axis=0, keepdims=True)


def middle_kernel(
    own, lat_a, lat_b, cross, corner_a, corner_b, ens_hbm, feat, ivert, squares,
    image, fields, edge_a, edge_b,
    ens, field, powers, smooth, mixed, weights, grad, sem, sems,
):
    copies = halo_copies(own, lat_a, lat_b, cross, corner_a, corner_b, field, sems)
    for copy in copies:
        copy.start()
    ens_copy = pltpu.make_async_copy(ens_hbm, ens, sem)
    ens_copy.start()
    members, windows, rows_lat, rows_lon, levels = ens.shape
    fill_weights(feat, weights, windows, rows_lat, rows_lon)
    for copy in copies:
        copy.wait()
    seen = observe(field, powers, smooth, mixed, squares, ivert, weights, ens, ens_copy)
    scaled = seen * feat[7:8]
    image[...] = jnp.zeros_like(image)
    image[0:1] = seen
    image[1:2] = scaled
    adjoint_fields(scaled, weights, ivert, ens, grad, fields, edge_a, edge_b)


def last_kernel(
    slots,
    own, lat_a, lat_b, cross, corner_a, corner_b, ens_hbm, feat, ivert, squares, image,
    send,
    ens, field, powers, smooth, mixed, weights, terms, sem, sems,
):
    copies = halo_copies(own, lat_a, lat_b, cross, corner_a, corner_b, field, sems)
    for copy in copies:
        copy.start()
    ens_copy = pltpu.make_async_copy(ens_hbm, ens, sem)
    ens_copy.start()
    members, windows, rows_lat, rows_lon, levels = ens.shape
    fill_weights(feat, weights, windows, rows_lat, rows_lon)
    for copy in copies:
        copy.wait()
    second = observe(field, powers, smooth, mixed, squares, ivert, weights, ens, ens_copy)
    start = feat[6:7]
    rinv = feat[7:8]
    first = image[0:1]
    scaled = image[1:2]
    norm = jnp.sum(start * first, axis=1, keepdims=True)
    curve = norm + jnp.sum(first * scaled, axis=1, keepdims=True)
    guess = jnp.where(curve > 0.0, norm / jnp.where(curve > 0.0, curve, 1.0), 1.0)
    guess = jnp.clip(guess, 0.0, 1.0)
    ahead = start + scaled
    ahead_image = first + second
    rest = start - guess * ahead
    rest_image = first - guess * ahead_image
    products = (
        start * first,
        first * scaled,
        rest * rest_image,
        rest * ahead_image + ahead * rest_image,
        ahead * ahead_image,
        rest_image * rinv * rest_image,
        2.0 * rest_image * rinv * ahead_image,
        ahead_image * rinv * ahead_image,
        2.0 * rest_image * scaled,
        2.0 * ahead_image * scaled,
        start * rest_image + rest * first,
        start * ahead_image + ahead * first,
    )
    terms[...] = jnp.zeros_like(terms)
    for n, value in enumerate(products):
        terms[n : n + 1] = value
    sums = jnp.sum(terms[...], axis=1, keepdims=True)
    square = (16, LANES)
    line = jnp.sum(
        jnp.where(iota(square, 0) == iota(square, 1), sums, 0.0), axis=0, keepdims=True
    )
    owners = send.shape[0]
    per = LANES // slots
    row = iota((8, LANES), 0)
    for g in range(owners // per):
        lanes = slice(g * LANES, (g + 1) * LANES)
        block = jnp.where(row == 0, first[:, lanes], 0.0)
        block = jnp.where(row == 1, second[:, lanes], block)
        block = jnp.where(row == 2, line, block)
        block = jnp.where(row == 3, guess, block)
        send[g * per : (g + 1) * per] = jnp.broadcast_to(block[None], (per, 8, LANES))


def control_kernel(
    own, lat_a, lat_b, cross, corner_a, corner_b, vert_loc, static_vert,
    control,
    field, powers, smooth, sems,
):
    copies = halo_copies(own, lat_a, lat_b, cross, corner_a, corner_b, field, sems)
    for copy in copies:
        copy.start()
    for copy in copies:
        copy.wait()
    smooth_power(field, powers, smooth, 2)
    count, rows_lat, rows_lon, levels = smooth.shape
    for k in range(count):
        scale, matrix = (BETA_ENSEMBLE, vert_loc) if k < count - 1 else (BETA_STATIC, static_vert)
        value = dot(smooth[k].reshape(rows_lat * rows_lon, levels), matrix[...], ((1,), (1,)))
        control[k] = (scale * value).reshape(rows_lat, rows_lon, levels)


def final_kernel(recv, dest, lane, early, late, static, member, equivalent):
    owners = recv.shape[0]
    rows = dest.shape[1]
    blocks = recv[...]
    line = blocks[:, 2:3]
    sums = jnp.sum(line, axis=0)

    def pick(values, n):
        return values[:, n : n + 1]

    norm = pick(sums, 0)
    step = norm / (norm + pick(sums, 1))
    off = blocks[:, 3:4] - step[None]
    linear = jnp.sum(off * line, axis=0)
    square = jnp.sum(off * off * line, axis=0)
    norm_next = jnp.maximum(pick(sums, 2) + pick(linear, 3) + pick(square, 4), 0.0)
    beta = norm_next / norm
    bend = pick(sums, 5) + pick(linear, 6) + pick(square, 7)
    bend = bend + beta * (pick(sums, 8) + pick(linear, 9)) + beta * beta * pick(sums, 1)
    length = norm_next + beta * (pick(sums, 10) + pick(linear, 11)) + beta * beta * norm
    curve = length + bend
    step_next = jnp.where(curve > 0.0, norm_next / jnp.where(curve > 0.0, curve, 1.0), 0.0)
    step_next = jnp.minimum(step_next, 1.0)
    near = step + step_next * ((1.0 - step) + beta)
    far = -step_next * step
    members = member.shape[0]
    for k in range(members):
        member[k] = near[None] * early[k] + far[None] * late[k]
    static[...] = near[None] * early[members] + far[None] * late[members]
    kind = iota((owners, 8, rows), 1)
    factor = jnp.where(kind == 0, near[None], jnp.where(kind == 1, far[None], 0.0))
    chosen = iota((owners, 8, rows), 0) == dest[...].reshape(1, 1, rows)
    picked = jnp.where(chosen, factor, 0.0).reshape(owners * 8, rows)
    table = dot(blocks.reshape(owners * 8, LANES), picked, ((0,), (0,)))
    equivalent[...] = jnp.sum(
        jnp.where(iota((LANES, rows), 0) == lane[...], table, 0.0), axis=0, keepdims=True
    )


def shape(*dims):
    return jax.ShapeDtypeStruct(dims, F32)


def swaps(count, ring):
    inner = [(i, i ^ 1) for i in range(count)]
    outer = []
    for i in range(1, count - 1, 2):
        outer += [(i, i + 1), (i + 1, i)]
    if ring:
        outer += [(count - 1, 0), (0, count - 1)]
    return inner, outer


def body(
    ensemble,
    vert_loc,
    static_vert,
    inst_vert,
    inst_err,
    obs_dest,
    obs_patch,
    obs_window,
    obs_inst,
    obs_hweight,
    innovation,
    obs_count,
):
    members, windows, rows_lat, rows_lon, levels = ensemble.shape
    lat_count = lax.axis_size("lat")
    lon_count = lax.axis_size("lon")
    owners = lat_count * lon_count
    rows = innovation.shape[0]
    slots = 2 * rows // owners
    total = owners * slots
    patches = rows_lat // 2 * (rows_lon // 2)
    count = members + 1
    width = rows_lon + 8
    lat_inner, lat_outer = swaps(lat_count, False)
    lon_inner, lon_outer = swaps(lon_count, True)
    tile = shape(count, rows_lat, rows_lon, levels)
    edge = shape(count, rows_lat, 8, levels)

    def line(values):
        return values.reshape(1, rows)

    dest = line(obs_dest)
    send, lane = pl.pallas_call(
        functools.partial(pack_kernel, slots, patches),
        out_shape=(shape(owners, 8, LANES), jax.ShapeDtypeStruct((1, rows), jnp.int32)),
        in_specs=[VMEM] * 7 + [SMEM],
        out_specs=(VMEM, VMEM),
        scratch_shapes=[pltpu.VMEM((8, rows), F32)],
        compiler_params=PARAMS,
        name="pack",
    )(
        obs_dest,
        dest,
        line(obs_patch),
        line(obs_window),
        line(obs_inst),
        obs_hweight,
        line(innovation),
        obs_count,
    )
    squares = pl.pallas_call(
        prepare_kernel,
        out_shape=shape(2, levels, levels),
        compiler_params=PARAMS,
        name="prepare",
    )(vert_loc, static_vert)

    def exchange(blocks):
        return lax.all_to_all(blocks, ("lat", "lon"), split_axis=0, concat_axis=0, tiled=True)

    recv = exchange(send)
    ens_scratch = pltpu.VMEM(ensemble.shape, ensemble.dtype)
    field_scratch = pltpu.VMEM((count, rows_lat + 2 * HALO, width, levels), F32)
    tile_scratch = pltpu.VMEM(tile.shape, F32)
    weight_scratch = pltpu.VMEM((windows * rows_lat * rows_lon, total), F32)
    grad_scratch = pltpu.VMEM((windows * rows_lat * rows_lon, levels), F32)

    def powers(order):
        return pltpu.VMEM((order, rows_lat, width, levels), F32)

    feat, ivert, fields, edge_a, edge_b = pl.pallas_call(
        functools.partial(first_kernel, slots),
        out_shape=(shape(8, total), shape(levels, total), tile, edge, edge),
        in_specs=[VMEM, VMEM, VMEM, ANY],
        out_specs=(VMEM,) * 5,
        scratch_shapes=[ens_scratch, weight_scratch, grad_scratch, pltpu.SemaphoreType.DMA],
        compiler_params=PARAMS,
        name="first",
    )(recv, inst_vert, inst_err.reshape(1, -1), ensemble)

    def halo(fields, edge_a, edge_b):
        lat_b = lax.ppermute(fields, "lat", lat_outer)
        side_a = lax.ppermute(edge_a, "lon", lon_inner)
        side_b = lax.ppermute(edge_b, "lon", lon_outer)
        lat_a = lax.ppermute(fields, "lat", lat_inner)
        cross = side_a + side_b
        corner_b = lax.ppermute(cross, "lat", lat_outer)
        corner_a = lax.ppermute(cross, "lat", lat_inner)
        return (fields, lat_a, lat_b, cross, corner_a, corner_b)

    def control(parts):
        return pl.pallas_call(
            control_kernel,
            out_shape=tile,
            in_specs=[ANY] * 6 + [VMEM] * 2,
            out_specs=VMEM,
            scratch_shapes=[
                field_scratch,
                powers(2),
                tile_scratch,
                pltpu.SemaphoreType.DMA((6,)),
            ],
            compiler_params=PARAMS,
            name="control",
        )(*parts, vert_loc, static_vert)

    parts = halo(fields, edge_a, edge_b)
    work = [ens_scratch, field_scratch, powers(4), tile_scratch, tile_scratch, weight_scratch]
    sems = [pltpu.SemaphoreType.DMA, pltpu.SemaphoreType.DMA((6,))]
    image, fields, edge_a, edge_b = pl.pallas_call(
        middle_kernel,
        out_shape=(shape(8, total), tile, edge, edge),
        in_specs=[ANY] * 7 + [VMEM] * 3,
        out_specs=(VMEM,) * 4,
        scratch_shapes=work + [grad_scratch] + sems,
        compiler_params=PARAMS,
        name="middle",
    )(*parts, ensemble, feat, ivert, squares)
    early = control(parts)
    parts = halo(fields, edge_a, edge_b)
    send = pl.pallas_call(
        functools.partial(last_kernel, slots),
        out_shape=shape(owners, 8, LANES),
        in_specs=[ANY] * 7 + [VMEM] * 4,
        out_specs=VMEM,
        scratch_shapes=work + [pltpu.VMEM((16, total), F32)] + sems,
        compiler_params=PARAMS,
        name="last",
    )(*parts, ensemble, feat, ivert, squares, image)
    late = control(parts)
    recv = exchange(send)
    static, member, equivalent = pl.pallas_call(
        final_kernel,
        out_shape=(
            shape(rows_lat, rows_lon, levels),
            shape(members, rows_lat, rows_lon, levels),
            shape(1, rows),
        ),
        compiler_params=PARAMS,
        name="final",
    )(recv, dest, lane, early, late)
    return static, member, equivalent.reshape(rows)


def solution(mesh):
    return jax.shard_map(
        body,
        mesh=mesh,
        in_specs=(
            P(None, None, "lat", "lon", None),
            P(),
            P(),
            P(),
            P(),
            P(("lat", "lon"), None),
            P(("lat", "lon")),
            P(("lat", "lon")),
            P(("lat", "lon")),
            P(None, ("lat", "lon")),
            P(("lat", "lon")),
            P(("lat", "lon")),
        ),
        out_specs=(P("lat", "lon", None), P(None, "lat", "lon", None), P(("lat", "lon"))),
        check_vma=False,
    )
```

profile of v0, /device:TPU:0, one launch (start us, length us, event | category | flops | bytes accessed | tf_op | source)
XLA Modules:
  0.0 96.0 jit_solution(4252037395361471042)
XLA Ops:
  0.6 0.0 copy-start.14
  0.6 0.0 copy-start.12
  1.3 0.8 copy.15.dest_col
  2.1 0.0 copy-start.25
  2.2 0.7 copy-done.25
  2.8 0.7 copy-done.28
  3.5 0.7 copy-done.29
  4.2 0.7 copy-done.30
  4.9 0.7 copy-done.31
  5.6 0.7 copy-done.32
  6.2 0.5 pack.1
  6.7 14.9 %all_to_all.10.recv = f32[32,8,128]{2,1,0:T(8,128)S(1)} all-to-all(f32[32,8,128]{2,1,0:T(8,128)S(1)} %get-tuple-element.17), channel_id=1, replica_groups=mesh['lat'=4,'lon'=8] {'lat','lon'}, dimensions={0} | all-to-all | bytes 262144 | tf_op jit(solution)/shard_map/all_to_all | solution.py:444
  21.7 1.4 %copy-done = bf16[8,4,4,48,128]{4,3,2,1,0:T(8,128)(2,1)S(1)} copy-done((bf16[8,4,4,48,128]{4,3,2,1,0:T(8,128)(2,1)S(1)}, bf16[8,4,4,48,128]{4,3,2,1,0:T(8,128)(2,1)}, u32[]{:S(2)}) %copy-start) | copy-done | bytes 1572888
  23.1 0.7 copy-done.27
  23.8 0.7 copy-done.33
  24.4 2.3 %first.1 = (f32[8,512]{1,0:T(8,128)S(1)}, f32[128,512]{1,0:T(8,128)S(1)}, f32[9,4,48,128]{3,2,1,0:T(8,128)S(1)}, f32[9,4,8,128]{3,2,1,0:T(8,128)S(1)}, f32[9,4,8,128]{3,2,1,0:T(8,128)S(1)}) custom-call(f32[32,8,128]{2,1,0:T(8,128)S(1)} %all_to_all.10.recv, f32[16,128]{1,0:T(8,128)S(1)} %copy-done.27, f32[1,16]{1,0:T(1,128)S(1)} %bitcast.13, ...), custom_call_target="tpu_custom_call" | custom-call | tf_op jit(solution)/shard_map/first/pallas_call | solution.py:456
  26.7 0.7 collective-permute-start.1
  27.4 2.3 %collective-permute-start = (f32[9,4,48,128]{3,2,1,0:T(8,128)S(1)}, f32[9,4,48,128]{3,2,1,0:T(8,128)S(1)}, u32[]{:S(2)}, u32[]{:S(2)}) collective-permute-start(f32[9,4,48,128]{3,2,1,0:T(8,128)S(1)} %get-tuple-element.18.own), channel_id=1, source_target_pairs={{0,8},{8,0},{16,24},{24,16},{1,9},{9,1},{17,25},{25,17},{2,10},{10... | collective-permute-start | bytes 2654216 | tf_op jit(solution)/shard_map/ppermute | solution.py:470
  29.8 0.9 collective-permute-start.2
  30.7 2.1 %collective-permute-start.3 = (f32[9,4,8,128]{3,2,1,0:T(8,128)S(1)}, f32[9,4,8,128]{3,2,1,0:T(8,128)S(1)}, u32[]{:S(2)}, u32[]{:S(2)}) collective-permute-start(f32[9,4,8,128]{3,2,1,0:T(8,128)S(1)} %get-tuple-element.20), channel_id=1, source_target_pairs={{1,2},{2,1},{3,4},{4,3},{5,6},{6,5},{7,0},{0,7},{9,10},{10,9},{11,... | collective-permute-start | bytes 442376 | tf_op jit(solution)/shard_map/ppermute | solution.py:469
  32.8 4.4 %collective-permute-done.2 = f32[9,4,8,128]{3,2,1,0:T(8,128)S(1)} collective-permute-done((f32[9,4,8,128]{3,2,1,0:T(8,128)S(1)}, f32[9,4,8,128]{3,2,1,0:T(8,128)S(1)}, u32[]{:S(2)}, u32[]{:S(2)}) %collective-permute-start.2) | collective-permute-done | bytes 147488 | tf_op jit(solution)/shard_map/ppermute | solution.py:468
  37.2 1.7 %collective-permute-done.3 = f32[9,4,8,128]{3,2,1,0:T(8,128)S(1)} collective-permute-done((f32[9,4,8,128]{3,2,1,0:T(8,128)S(1)}, f32[9,4,8,128]{3,2,1,0:T(8,128)S(1)}, u32[]{:S(2)}, u32[]{:S(2)}) %collective-permute-start.3) | collective-permute-done | bytes 147488 | tf_op jit(solution)/shard_map/ppermute | solution.py:469
  38.9 0.0 copy-start.8
  39.0 0.7 collective-permute-start.5
  39.6 2.7 %collective-permute-start.4 = (f32[9,4,8,128]{3,2,1,0:T(8,128)S(1)}, f32[9,4,8,128]{3,2,1,0:T(8,128)S(1)}, u32[]{:S(2)}, u32[]{:S(2)}) collective-permute-start(f32[9,4,8,128]{3,2,1,0:T(8,128)S(1)} %add.6.cross), channel_id=1, source_target_pairs={{0,8},{8,0},{16,24},{24,16},{1,9},{9,1},{17,25},{25,17},{2,10},{10... | collective-permute-start | bytes 442376 | tf_op jit(solution)/shard_map/ppermute | solution.py:473
  42.4 0.3 prepare.1.squares
  42.7 0.0 collective-permute-done.5.corner_b
  42.7 0.7 collective-permute-done.4.corner_a
  43.4 0.0 collective-permute-done.1.lat_b
  43.4 0.0 collective-permute-done.lat_a
  43.4 6.3 %middle.1 = (f32[8,512]{1,0:T(8,128)S(1)}, f32[9,4,48,128]{3,2,1,0:T(8,128)S(1)}, f32[9,4,8,128]{3,2,1,0:T(8,128)S(1)}, f32[9,4,8,128]{3,2,1,0:T(8,128)S(1)}) custom-call(f32[9,4,48,128]{3,2,1,0:T(8,128)S(1)} %get-tuple-element.18.own, f32[9,4,48,128]{3,2,1,0:T(8,128)S(1)} %collective-permute-done.lat_a, f32[9,4,48,128]{3,2,1,0:T(8,128)S(1)} %collective-permute-done.1.lat_b, ...), custom_call_target="tpu_custom_call" | custom-call | tf_op jit(solution)/shard_map/middle/pallas_call | solution.py:495
  49.7 0.7 collective-permute-start.7
  50.4 4.7 %collective-permute-start.6 = (f32[9,4,48,128]{3,2,1,0:T(8,128)S(1)}, f32[9,4,48,128]{3,2,1,0:T(8,128)S(1)}, u32[]{:S(2)}, u32[]{:S(2)}) collective-permute-start(f32[9,4,48,128]{3,2,1,0:T(8,128)S(1)} %get-tuple-element.23.own), channel_id=1, source_target_pairs={{0,8},{8,0},{16,24},{24,16},{1,9},{9,1},{17,25},{25,17},{2,10},{10... | collective-permute-start | bytes 2654216 | tf_op jit(solution)/shard_map/ppermute | solution.py:470
  55.2 0.7 collective-permute-start.8
  55.9 1.3 %collective-permute-start.9 = (f32[9,4,8,128]{3,2,1,0:T(8,128)S(1)}, f32[9,4,8,128]{3,2,1,0:T(8,128)S(1)}, u32[]{:S(2)}, u32[]{:S(2)}) collective-permute-start(f32[9,4,8,128]{3,2,1,0:T(8,128)S(1)} %get-tuple-element.25), channel_id=1, source_target_pairs={{1,2},{2,1},{3,4},{4,3},{5,6},{6,5},{7,0},{0,7},{9,10},{10,9},{11,... | collective-permute-start | bytes 442376 | tf_op jit(solution)/shard_map/ppermute | solution.py:469
  57.2 5.2 %collective-permute-done.8 = f32[9,4,8,128]{3,2,1,0:T(8,128)S(1)} collective-permute-done((f32[9,4,8,128]{3,2,1,0:T(8,128)S(1)}, f32[9,4,8,128]{3,2,1,0:T(8,128)S(1)}, u32[]{:S(2)}, u32[]{:S(2)}) %collective-permute-start.8) | collective-permute-done | bytes 147488 | tf_op jit(solution)/shard_map/ppermute | solution.py:468
  62.4 1.7 %collective-permute-done.9 = f32[9,4,8,128]{3,2,1,0:T(8,128)S(1)} collective-permute-done((f32[9,4,8,128]{3,2,1,0:T(8,128)S(1)}, f32[9,4,8,128]{3,2,1,0:T(8,128)S(1)}, u32[]{:S(2)}, u32[]{:S(2)}) %collective-permute-start.9) | collective-permute-done | bytes 147488 | tf_op jit(solution)/shard_map/ppermute | solution.py:469
  64.2 0.7 collective-permute-start.11
  64.9 1.8 %collective-permute-start.10 = (f32[9,4,8,128]{3,2,1,0:T(8,128)S(1)}, f32[9,4,8,128]{3,2,1,0:T(8,128)S(1)}, u32[]{:S(2)}, u32[]{:S(2)}) collective-permute-start(f32[9,4,8,128]{3,2,1,0:T(8,128)S(1)} %add.7.cross), channel_id=1, source_target_pairs={{0,8},{8,0},{16,24},{24,16},{1,9},{9,1},{17,25},{25,17},{2,10},{10... | collective-permute-start | bytes 442376 | tf_op jit(solution)/shard_map/ppermute | solution.py:473
  66.6 0.0 collective-permute-done.11.corner_b
  66.6 1.0 %collective-permute-done.10.corner_a = f32[9,4,8,128]{3,2,1,0:T(8,128)S(1)} collective-permute-done((f32[9,4,8,128]{3,2,1,0:T(8,128)S(1)}, f32[9,4,8,128]{3,2,1,0:T(8,128)S(1)}, u32[]{:S(2)}, u32[]{:S(2)}) %collective-permute-start.10) | collective-permute-done | bytes 147488 | tf_op jit(solution)/shard_map/ppermute | solution.py:473
  67.6 0.0 collective-permute-done.7.lat_b
  67.6 0.0 collective-permute-done.6.lat_a
  67.7 4.9 %last.1 = f32[32,8,128]{2,1,0:T(8,128)S(1)} custom-call(f32[9,4,48,128]{3,2,1,0:T(8,128)S(1)} %get-tuple-element.23.own, f32[9,4,48,128]{3,2,1,0:T(8,128)S(1)} %collective-permute-done.6.lat_a, f32[9,4,48,128]{3,2,1,0:T(8,128)S(1)} %collective-permute-done.7.lat_b, f32[9,4,8,128]{3,2,1,0:T(8,128)S(1)} %add.7.cross, ...), custom_call_target="tpu_custom_call" | custom-call | tf_op jit(solution)/shard_map/last/pallas_call | solution.py:506
  72.6 0.9 copy-done.2
  73.5 0.9 copy-done.4
  74.4 0.7 copy-done.10
  75.1 0.6 copy-done.20
  75.7 0.6 copy-done.22
  76.4 0.7 copy-done.24
  77.0 5.1 %all-to-all-start.1 = ((f32[32,8,128]{2,1,0:T(8,128)}), f32[32,8,128]{2,1,0:T(8,128)}, u32[]{:S(2)}, u32[]{:S(2)}) async-start(f32[32,8,128]{2,1,0:T(8,128)} %copy-done.24), calls=%async_computation.1 | async-start | bytes 262144 | tf_op jit(solution)/shard_map/all_to_all | solution.py:444
  82.1 0.0 copy-start.9
  82.2 0.9 copy-done.9
  83.1 0.8 copy-done.13
  83.9 0.8 copy-done.15
  84.7 0.9 copy-done.17
  85.7 0.9 copy-done.19
  86.6 2.3 %control.2.early = f32[9,4,48,128]{3,2,1,0:T(8,128)S(1)} custom-call(f32[9,4,48,128]{3,2,1,0:T(8,128)S(1)} %get-tuple-element.18.own, f32[9,4,48,128]{3,2,1,0:T(8,128)S(1)} %collective-permute-done.lat_a, f32[9,4,48,128]{3,2,1,0:T(8,128)S(1)} %collective-permute-done.1.lat_b, f32[9,4,8,128]{3,2,1,0:T(8,128)S(1)} %copy-done.9, ...), custom_call_target="tpu_custom_call" | custom-call | tf_op jit(solution)/shard_map/control/pallas_call | solution.py:477
  88.9 0.9 copy-done.6
  89.8 0.0 copy-start.26
  89.9 2.3 %control.3.late = f32[9,4,48,128]{3,2,1,0:T(8,128)S(1)} custom-call(f32[9,4,48,128]{3,2,1,0:T(8,128)S(1)} %get-tuple-element.23.own, f32[9,4,48,128]{3,2,1,0:T(8,128)S(1)} %copy-done.5, f32[9,4,48,128]{3,2,1,0:T(8,128)S(1)} %copy-done.3, f32[9,4,8,128]{3,2,1,0:T(8,128)S(1)} %copy-done.11, f32[9,4,8,128]{3,2,1,0:T(8,128)S(1)} %copy-done.23, ...), custom_call_target="tpu_custom_call" | custom-call | tf_op jit(solution)/shard_map/control/pallas_call | solution.py:477
  92.2 0.0 all-to-all-done.1.recv
  92.2 1.2 %copy-done.7 = f32[9,4,48,128]{3,2,1,0:T(8,128)S(1)} copy-done((f32[9,4,48,128]{3,2,1,0:T(8,128)S(1)}, f32[9,4,48,128]{3,2,1,0:T(8,128)}, u32[]{:S(2)}) %copy-start.7) | copy-done | bytes 884760
  93.4 2.7 %final.1 = (f32[4,48,128]{2,1,0:T(8,128)}, f32[8,4,48,128]{3,2,1,0:T(8,128)}, f32[1,256]{1,0:T(1,128)}) custom-call(f32[32,8,128]{2,1,0:T(8,128)} %all-to-all-done.1.recv, s32[1,256]{1,0:T(1,128)S(1)} %bitcast.8, s32[1,256]{1,0:T(1,128)S(1)} %get-tuple-element.27.lane, f32[9,4,48,128]{3,2,1,0:T(8,128)S(1)} %copy-done.7, f32[9,4,48,128]{3,2,1,0:T(8,128)S(1)} %control.3.late), custom_call_target="tpu_custom_call" | custom-call | tf_op jit(solution)/shard_map/final/pallas_call | solution.py:517
  (42 shorter events, 0.1 us)
Async XLA Ops:
  0.6 41.8 %copy-start.14 = (f32[128,128]{1,0:T(8,128)S(1)}, f32[128,128]{1,0:T(8,128)}, u32[]{:S(2)}) copy-start(f32[128,128]{1,0:T(8,128)} %static_vert.5) | copy-start | bytes 196612
  0.6 41.7 %copy-start.12 = (f32[128,128]{1,0:T(8,128)S(1)}, f32[128,128]{1,0:T(8,128)}, u32[]{:S(2)}) copy-start(f32[128,128]{1,0:T(8,128)} %vert_loc.5) | copy-start | bytes 196612
  2.1 0.7 copy-start.25
  2.8 0.7 copy-start.28
  3.5 0.7 copy-start.29
  4.2 0.7 copy-start.30
  4.9 0.7 copy-start.31
  5.6 0.7 copy-start.32
  21.7 1.4 %copy-start = (bf16[8,4,4,48,128]{4,3,2,1,0:T(8,128)(2,1)S(1)}, bf16[8,4,4,48,128]{4,3,2,1,0:T(8,128)(2,1)}, u32[]{:S(2)}) copy-start(bf16[8,4,4,48,128]{4,3,2,1,0:T(8,128)(2,1)} %ens_hbm.5) | copy-start | bytes 4718596
  23.1 0.7 copy-start.27
  23.8 0.7 copy-start.33
  26.7 16.7 %collective-permute-start.1 = (f32[9,4,48,128]{3,2,1,0:T(8,128)S(1)}, f32[9,4,48,128]{3,2,1,0:T(8,128)S(1)}, u32[]{:S(2)}, u32[]{:S(2)}) collective-permute-start(f32[9,4,48,128]{3,2,1,0:T(8,128)S(1)} %get-tuple-element.18.own), channel_id=1, source_target_pairs={{8,16},{16,8},{9,17},{17,9},{10,18},{18,10},{11,19},{19,11},{12,20... | collective-permute-start | bytes 2654216 | tf_op jit(solution)/shard_map/ppermute | solution.py:467
  27.4 16.0 %collective-permute-start = (f32[9,4,48,128]{3,2,1,0:T(8,128)S(1)}, f32[9,4,48,128]{3,2,1,0:T(8,128)S(1)}, u32[]{:S(2)}, u32[]{:S(2)}) collective-permute-start(f32[9,4,48,128]{3,2,1,0:T(8,128)S(1)} %get-tuple-element.18.own), channel_id=1, source_target_pairs={{0,8},{8,0},{16,24},{24,16},{1,9},{9,1},{17,25},{25,17},{2,10},{10... | collective-permute-start | bytes 2654216 | tf_op jit(solution)/shard_map/ppermute | solution.py:470
  29.8 7.4 %collective-permute-start.2 = (f32[9,4,8,128]{3,2,1,0:T(8,128)S(1)}, f32[9,4,8,128]{3,2,1,0:T(8,128)S(1)}, u32[]{:S(2)}, u32[]{:S(2)}) collective-permute-start(f32[9,4,8,128]{3,2,1,0:T(8,128)S(1)} %get-tuple-element.19), channel_id=1, source_target_pairs={{0,1},{1,0},{2,3},{3,2},{4,5},{5,4},{6,7},{7,6},{8,9},{9,8},{10,11... | collective-permute-start | bytes 442376 | tf_op jit(solution)/shard_map/ppermute | solution.py:468
  30.7 8.2 %collective-permute-start.3 = (f32[9,4,8,128]{3,2,1,0:T(8,128)S(1)}, f32[9,4,8,128]{3,2,1,0:T(8,128)S(1)}, u32[]{:S(2)}, u32[]{:S(2)}) collective-permute-start(f32[9,4,8,128]{3,2,1,0:T(8,128)S(1)} %get-tuple-element.20), channel_id=1, source_target_pairs={{1,2},{2,1},{3,4},{4,3},{5,6},{6,5},{7,0},{0,7},{9,10},{10,9},{11,... | collective-permute-start | bytes 442376 | tf_op jit(solution)/shard_map/ppermute | solution.py:469
  38.9 10.7 %copy-start.8 = (f32[9,4,8,128]{3,2,1,0:T(8,128)}, f32[9,4,8,128]{3,2,1,0:T(8,128)S(1)}, u32[]{:S(2)}) copy-start(f32[9,4,8,128]{3,2,1,0:T(8,128)S(1)} %add.6.cross) | copy-start | bytes 442372
  39.0 3.7 %collective-permute-start.5 = (f32[9,4,8,128]{3,2,1,0:T(8,128)S(1)}, f32[9,4,8,128]{3,2,1,0:T(8,128)S(1)}, u32[]{:S(2)}, u32[]{:S(2)}) collective-permute-start(f32[9,4,8,128]{3,2,1,0:T(8,128)S(1)} %add.6.cross), channel_id=1, source_target_pairs={{8,16},{16,8},{9,17},{17,9},{10,18},{18,10},{11,19},{19,11},{12,20... | collective-permute-start | bytes 442376 | tf_op jit(solution)/shard_map/ppermute | solution.py:472
  39.6 3.8 %collective-permute-start.4 = (f32[9,4,8,128]{3,2,1,0:T(8,128)S(1)}, f32[9,4,8,128]{3,2,1,0:T(8,128)S(1)}, u32[]{:S(2)}, u32[]{:S(2)}) collective-permute-start(f32[9,4,8,128]{3,2,1,0:T(8,128)S(1)} %add.6.cross), channel_id=1, source_target_pairs={{0,8},{8,0},{16,24},{24,16},{1,9},{9,1},{17,25},{25,17},{2,10},{10... | collective-permute-start | bytes 442376 | tf_op jit(solution)/shard_map/ppermute | solution.py:473
  42.7 7.0 %copy-start.16 = (f32[9,4,8,128]{3,2,1,0:T(8,128)}, f32[9,4,8,128]{3,2,1,0:T(8,128)S(1)}, u32[]{:S(2)}) copy-start(f32[9,4,8,128]{3,2,1,0:T(8,128)S(1)} %collective-permute-done.5.corner_b) | copy-start | bytes 442372
  43.4 6.3 %copy-start.18 = (f32[9,4,8,128]{3,2,1,0:T(8,128)}, f32[9,4,8,128]{3,2,1,0:T(8,128)S(1)}, u32[]{:S(2)}) copy-start(f32[9,4,8,128]{3,2,1,0:T(8,128)S(1)} %collective-permute-done.4.corner_a) | copy-start | bytes 442372
  43.4 24.3 %copy-start.1 = (bf16[8,4,4,48,128]{4,3,2,1,0:T(8,128)(2,1)S(1)}, bf16[8,4,4,48,128]{4,3,2,1,0:T(8,128)(2,1)}, u32[]{:S(2)}) copy-start(bf16[8,4,4,48,128]{4,3,2,1,0:T(8,128)(2,1)} %ens_hbm.5) | copy-start | bytes 4718596
  49.7 17.9 %collective-permute-start.7 = (f32[9,4,48,128]{3,2,1,0:T(8,128)S(1)}, f32[9,4,48,128]{3,2,1,0:T(8,128)S(1)}, u32[]{:S(2)}, u32[]{:S(2)}) collective-permute-start(f32[9,4,48,128]{3,2,1,0:T(8,128)S(1)} %get-tuple-element.23.own), channel_id=1, source_target_pairs={{8,16},{16,8},{9,17},{17,9},{10,18},{18,10},{11,19},{19,11},{12,20... | collective-permute-start | bytes 2654216 | tf_op jit(solution)/shard_map/ppermute | solution.py:467
  50.4 17.2 %collective-permute-start.6 = (f32[9,4,48,128]{3,2,1,0:T(8,128)S(1)}, f32[9,4,48,128]{3,2,1,0:T(8,128)S(1)}, u32[]{:S(2)}, u32[]{:S(2)}) collective-permute-start(f32[9,4,48,128]{3,2,1,0:T(8,128)S(1)} %get-tuple-element.23.own), channel_id=1, source_target_pairs={{0,8},{8,0},{16,24},{24,16},{1,9},{9,1},{17,25},{25,17},{2,10},{10... | collective-permute-start | bytes 2654216 | tf_op jit(solution)/shard_map/ppermute | solution.py:470
  55.2 7.3 %collective-permute-start.8 = (f32[9,4,8,128]{3,2,1,0:T(8,128)S(1)}, f32[9,4,8,128]{3,2,1,0:T(8,128)S(1)}, u32[]{:S(2)}, u32[]{:S(2)}) collective-permute-start(f32[9,4,8,128]{3,2,1,0:T(8,128)S(1)} %get-tuple-element.24), channel_id=1, source_target_pairs={{0,1},{1,0},{2,3},{3,2},{4,5},{5,4},{6,7},{7,6},{8,9},{9,8},{10,11... | collective-permute-start | bytes 442376 | tf_op jit(solution)/shard_map/ppermute | solution.py:468
  55.9 8.2 %collective-permute-start.9 = (f32[9,4,8,128]{3,2,1,0:T(8,128)S(1)}, f32[9,4,8,128]{3,2,1,0:T(8,128)S(1)}, u32[]{:S(2)}, u32[]{:S(2)}) collective-permute-start(f32[9,4,8,128]{3,2,1,0:T(8,128)S(1)} %get-tuple-element.25), channel_id=1, source_target_pairs={{1,2},{2,1},{3,4},{4,3},{5,6},{6,5},{7,0},{0,7},{9,10},{10,9},{11,... | collective-permute-start | bytes 442376 | tf_op jit(solution)/shard_map/ppermute | solution.py:469
  64.2 2.4 %collective-permute-start.11 = (f32[9,4,8,128]{3,2,1,0:T(8,128)S(1)}, f32[9,4,8,128]{3,2,1,0:T(8,128)S(1)}, u32[]{:S(2)}, u32[]{:S(2)}) collective-permute-start(f32[9,4,8,128]{3,2,1,0:T(8,128)S(1)} %add.7.cross), channel_id=1, source_target_pairs={{8,16},{16,8},{9,17},{17,9},{10,18},{18,10},{11,19},{19,11},{12,20... | collective-permute-start | bytes 442376 | tf_op jit(solution)/shard_map/ppermute | solution.py:472
  64.9 2.8 %collective-permute-start.10 = (f32[9,4,8,128]{3,2,1,0:T(8,128)S(1)}, f32[9,4,8,128]{3,2,1,0:T(8,128)S(1)}, u32[]{:S(2)}, u32[]{:S(2)}) collective-permute-start(f32[9,4,8,128]{3,2,1,0:T(8,128)S(1)} %add.7.cross), channel_id=1, source_target_pairs={{0,8},{8,0},{16,24},{24,16},{1,9},{9,1},{17,25},{25,17},{2,10},{10... | collective-permute-start | bytes 442376 | tf_op jit(solution)/shard_map/ppermute | solution.py:473
  72.5 0.9 copy-start.2
  73.5 0.9 copy-start.4
  74.4 0.7 copy-start.10
  75.1 0.6 copy-start.20
  75.7 0.6 copy-start.22
  76.4 0.7 copy-start.24
  77.0 15.2 %all-to-all-start.1 = ((f32[32,8,128]{2,1,0:T(8,128)}), f32[32,8,128]{2,1,0:T(8,128)}, u32[]{:S(2)}, u32[]{:S(2)}) async-start(f32[32,8,128]{2,1,0:T(8,128)} %copy-done.24), calls=%async_computation.1 | async-start | bytes 262144 | tf_op jit(solution)/shard_map/all_to_all | solution.py:444
  82.1 0.9 copy-start.9
  83.1 0.8 copy-start.13
  83.9 0.8 copy-start.15
  84.7 0.9 copy-start.17
  85.6 0.9 copy-start.19
  86.6 3.3 %copy-start.3 = (f32[9,4,48,128]{3,2,1,0:T(8,128)S(1)}, f32[9,4,48,128]{3,2,1,0:T(8,128)}, u32[]{:S(2)}) copy-start(f32[9,4,48,128]{3,2,1,0:T(8,128)} %copy-done.2) | copy-start | bytes 2654212
  86.6 3.3 %copy-start.5 = (f32[9,4,48,128]{3,2,1,0:T(8,128)S(1)}, f32[9,4,48,128]{3,2,1,0:T(8,128)}, u32[]{:S(2)}) copy-start(f32[9,4,48,128]{3,2,1,0:T(8,128)} %copy-done.4) | copy-start | bytes 2654212
  86.6 3.3 %copy-start.11 = (f32[9,4,8,128]{3,2,1,0:T(8,128)S(1)}, f32[9,4,8,128]{3,2,1,0:T(8,128)}, u32[]{:S(2)}) copy-start(f32[9,4,8,128]{3,2,1,0:T(8,128)} %copy-done.10) | copy-start | bytes 442372
  86.6 3.3 %copy-start.21 = (f32[9,4,8,128]{3,2,1,0:T(8,128)S(1)}, f32[9,4,8,128]{3,2,1,0:T(8,128)}, u32[]{:S(2)}) copy-start(f32[9,4,8,128]{3,2,1,0:T(8,128)} %copy-done.20) | copy-start | bytes 442372
  86.6 3.3 %copy-start.23 = (f32[9,4,8,128]{3,2,1,0:T(8,128)S(1)}, f32[9,4,8,128]{3,2,1,0:T(8,128)}, u32[]{:S(2)}) copy-start(f32[9,4,8,128]{3,2,1,0:T(8,128)} %copy-done.22) | copy-start | bytes 442372
  88.9 0.9 copy-start.6
  89.8 2.3 %copy-start.26 = (s32[256,1]{0,1:T(1,128)S(1)}, s32[256,1]{0,1:T(1,128)}, u32[]{:S(2)}) copy-start(s32[256,1]{0,1:T(1,128)} %param.17) | copy-start | bytes 3076
  92.2 1.2 %copy-start.7 = (f32[9,4,48,128]{3,2,1,0:T(8,128)S(1)}, f32[9,4,48,128]{3,2,1,0:T(8,128)}, u32[]{:S(2)}) copy-start(f32[9,4,48,128]{3,2,1,0:T(8,128)} %copy-done.6) | copy-start | bytes 2654212
where the time goes:
time: 96.7 us; the launch traced here: 96 us
  starting transfers between devices  24.6 us (25%)
  Pallas kernels  21.5 us (22%)
  local copies, waits for them, and re-layouts  18.6 us (19%)
  blocking collectives  14.9 us (15%)
  waiting for transfers between devices  14.8 us (15%)
  between operations  1.61 us (2%)
    unnamed x69, local copies, waits for them, and re-layouts  18.6 us
    all_to_all x1, blocking collectives, exchange(): lax.all_to_all(blocks, ('lat', 'lon'), split_axis=0, concat_axis=0, tiled...  14.9 us
    ppermute x2, waiting for transfers between devices, halo(): side_a = lax.ppermute(edge_a, 'lon', lon_inner)  9.61 us
    ppermute x2, starting transfers between devices, halo(): lat_a = lax.ppermute(fields, 'lat', lat_inner)  7.08 us
    pallas_call x1, Pallas kernels, body(): pl.pallas_call(middle_kernel, out_shape=(shape(8, total), tile, edge, edg...  6.27 us
    all_to_all x1, starting transfers between devices, exchange(): lax.all_to_all(blocks, ('lat', 'lon'), split_axis=0, concat_axis=0, tiled...  5.13 us
    pallas_call x1, Pallas kernels, body(): pl.pallas_call(functools.partial(last_kernel, slots), out_shape=shape(own...  4.88 us
    pallas_call x2, Pallas kernels, control(): pl.pallas_call(control_kernel, out_shape=tile, in_specs=[ANY] * 6 + [VMEM...  4.63 us
  transfers between devices with their start and end apart: 13, of which 6 were waited for; matrix products, arithmetic and copies ran while one was open for 0% of the time, Pallas kernels for 5%

commit v1 on v0

--- a/solution.py
+++ b/solution.py
@@ -7,19 +7,23 @@
 from jax.experimental.pallas import tpu as pltpu
 from jax.sharding import PartitionSpec as P
 
+
 SMOOTH = 0.15
 CENTER = 1.0 - 4.0 * SMOOTH
 BETA_STATIC = 0.5
 BETA_ENSEMBLE = 0.85
 HALO = 4
+FOLD = 3
 LANES = 128
 HIGHEST = lax.Precision.HIGHEST
 F32 = jnp.float32
 
 ANY = pl.BlockSpec(memory_space=pl.ANY)
+HBM = pl.BlockSpec(memory_space=pltpu.HBM)
 VMEM = pl.BlockSpec(memory_space=pltpu.VMEM)
 SMEM = pl.BlockSpec(memory_space=pltpu.SMEM)
-PARAMS = pltpu.CompilerParams(vmem_limit_bytes=48 * 1024 * 1024)
+PARAMS = pltpu.CompilerParams(vmem_limit_bytes=32 * 1024 * 1024)
+DMA = pltpu.SemaphoreType.DMA
 
 
 def dot(left, right, dims=((1,), (0,))):
@@ -32,18 +36,49 @@
     return lax.broadcasted_iota(jnp.int32, shape, dim)
 
 
+def fetch(sources, targets, sems):
+    copies = [
+        pltpu.make_async_copy(source, target, sems.at[n])
+        for n, (source, target) in enumerate(zip(sources, targets))
+    ]
+    for copy in copies:
+        copy.start()
+    return copies
+
+
+def wait_all(copies):
+    for copy in copies:
+        copy.wait()
+
+
 def pack_kernel(
-    slots, patches, dest_col, dest, patch, window, inst, hweight, innov, count, send, lane, feat
+    slots, patches,
+    dest_hbm, patch_hbm, window_hbm, inst_hbm, hweight_hbm, innov_hbm, count,
+    send, lane_hbm,
+    dest, patch, window, inst, hweight, innov, feat, lane, sems,
 ):
+    wait_all(
+        fetch(
+            (dest_hbm, patch_hbm, window_hbm, inst_hbm, hweight_hbm, innov_hbm),
+            (dest, patch, window, inst, hweight, innov),
+            sems,
+        )
+    )
     owners = send.shape[0]
     rows = dest.shape[1]
     me = lax.axis_index("lat") * lax.axis_size("lon") + lax.axis_index("lon")
     base = lax.rem(me, LANES // slots) * slots
     destination = dest[...]
-    earlier = (dest_col[...] == destination) & (iota((rows, rows), 0) < iota((rows, rows), 1))
+    row, col = iota((rows, rows), 0), iota((rows, rows), 1)
+    upright = jnp.sum(
+        jnp.where(row == col, destination.astype(F32), 0.0), axis=1, keepdims=True
+    ).astype(jnp.int32)
+    earlier = (upright == destination) & (row < col)
     ranking = jnp.sum(jnp.where(earlier, 1.0, 0.0), axis=0, keepdims=True).astype(jnp.int32)
     position = ranking + base
     lane[...] = position
+    lane_copy = pltpu.make_async_copy(lane, lane_hbm, sems.at[6])
+    lane_copy.start()
     active = (iota((1, rows), 1) < count[0]).astype(F32)
     feat[...] = jnp.zeros_like(feat)
     feat[0:1] = (window[...] * patches + patch[...]).astype(F32)
@@ -54,6 +89,7 @@
     spread_out = jnp.where(chosen, feat[...][None], 0.0).reshape(owners * 8, rows)
     at_lane = (iota((LANES, rows), 0) == position).astype(F32)
     send[...] = dot(spread_out, at_lane, ((1,), (1,))).reshape(owners, 8, LANES)
+    lane_copy.wait()
 
 
 def prepare_kernel(vert_loc, static_vert, squares):
@@ -75,61 +111,53 @@
             weights[row : row + rows_lon] = jnp.where(half == cell - first, corner[a % 2], 0.0)
 
 
-def adjoint_fields(amount, weights, ivert, ens, grad, fields, edge_a, edge_b):
-    members, windows, rows_lat, rows_lon, levels = ens.shape
+def adjoint_fields(amount, weights, ivert, ens, ens_copies, grad, outs):
+    fields, edge_a, edge_b = outs
+    members, windows, rows_lat, rows_lon, _ = ens.shape
     block = rows_lat * rows_lon
     scaled = ivert[...] * amount
     for t in range(windows):
         rows = slice(t * block, (t + 1) * block)
         grad[rows] = dot(weights[rows], scaled, ((1,), (1,)))
     even = lax.rem(lax.axis_index("lon"), 2) == 0
-    upper = iota((8, levels), 0) >= 4
-
-    def put(k, a, value):
-        fields[k, a] = value
-        east = jnp.where(upper, value[rows_lon - 8 :], 0.0)
-        west = jnp.where(upper, 0.0, value[:8])
-        edge_a[k, a] = jnp.where(even, east, west)
-        edge_b[k, a] = jnp.where(even, west, east)
-
-    for a in range(rows_lat):
-        parts = [grad[
-            (t * rows_lat + a) * rows_lon : (t * rows_lat + a + 1) * rows_lon
-        ] for t in range(windows)]
-        for k in range(members):
-            total = ens[k, 0, a].astype(F32) * parts[0]
+
+    def part(t, a):
+        first = (t * rows_lat + a) * rows_lon
+        return grad[first : first + rows_lon]
+
+    for k in range(members + 1):
+        if k < members and ens_copies:
+            ens_copies[k].wait()
+        for a in range(rows_lat):
+            total = part(0, a) if k == members else ens[k, 0, a].astype(F32) * part(0, a)
             for t in range(1, windows):
-                total = total + ens[k, t, a].astype(F32) * parts[t]
-            put(k, a, total)
-        total = parts[0]
-        for t in range(1, windows):
-            total = total + parts[t]
-        put(members, a, total)
+                term = part(t, a) if k == members else ens[k, t, a].astype(F32) * part(t, a)
+                total = total + term
+            fields[k, a] = total
+            east = total[rows_lon - HALO :]
+            west = total[:HALO]
+            edge_a[k, a] = jnp.where(even, east, west)
+            edge_b[k, a] = jnp.where(even, west, east)
 
 
 def first_kernel(
     slots,
-    recv,
-    inst_vert,
-    inst_err,
-    ens_hbm,
-    feat,
-    ivert,
-    fields,
-    edge_a,
-    edge_b,
-    ens,
-    weights,
-    grad,
-    sem,
+    recv, inst_vert_hbm, inst_err_hbm, ens_hbm,
+    feat, ivert, fields, edge_a, edge_b,
+    inst_vert, inst_err, ens, weights, grad, sems,
 ):
-    copy = pltpu.make_async_copy(ens_hbm, ens, sem)
-    copy.start()
-    members, windows, rows_lat, rows_lon, levels = ens.shape
+    members = ens.shape[0]
+    copies = fetch(
+        [inst_vert_hbm, inst_err_hbm] + [ens_hbm.at[k] for k in range(members)],
+        [inst_vert, inst_err] + [ens.at[k] for k in range(members)],
+        sems,
+    )
+    members, windows, rows_lat, rows_lon, _ = ens.shape
     owners = recv.shape[0]
     per = LANES // slots
     for g in range(owners // per):
         feat[:, g * LANES : (g + 1) * LANES] = jnp.sum(recv[g * per : (g + 1) * per], axis=0)
+    wait_all(copies[:2])
     instruments = inst_vert.shape[0]
     total = feat.shape[1]
     onehot = (iota((instruments, total), 0) == feat[1:2].astype(jnp.int32)).astype(F32)
@@ -139,8 +167,8 @@
     feat[6:7] = feat[6:7] * rinv
     feat[7:8] = rinv
     fill_weights(feat, weights, windows, rows_lat, rows_lon)
-    copy.wait()
-    adjoint_fields(feat[6:7], weights, ivert, ens, grad, fields, edge_a, edge_b)
+    outs = (fields, edge_a, edge_b)
+    adjoint_fields(feat[6:7], weights, ivert, ens, copies[2:], grad, outs)
 
 
 def halo_copies(own, lat_a, lat_b, cross, corner_a, corner_b, field, sems):
@@ -160,14 +188,49 @@
         (lat_a.at[:, pl.ds(far_a, HALO)], field.at[:, pl.ds(row_a, HALO), main]),
         (lat_b.at[:, pl.ds(far_b, HALO)], field.at[:, pl.ds(row_b, HALO), main]),
         (corner_a.at[:, pl.ds(far_a, HALO)], field.at[:, pl.ds(row_a, HALO), side]),
-        (corner_b.at[:, pl.ds(far_b, HALO)], field.at[:, pl.ds(row_b, HALO), side]),
-    )
+        (corner_b.at[:, 0], field.at[:, row_b + (HALO - 1) * (1 - odd), side]),
+        (corner_b.at[:, 1], field.at[:, row_b + (HALO - 2) * (1 - odd) + odd, side]),
+    )
+    unused = row_b + (HALO - 1) * odd
+    field[:, pl.ds(unused, 1), rows_lon:] = jnp.zeros_like(field[:, pl.ds(unused, 1), rows_lon:])
     return [pltpu.make_async_copy(s, d, sems.at[n]) for n, (s, d) in enumerate(plan)]
 
 
+def unfold_corner(field, rows_lon):
+    odd = lax.rem(lax.axis_index("lat"), 2)
+    row_b = (field.shape[1] - HALO) * odd
+    second = row_b + (HALO - 2) * (1 - odd) + odd
+    third = row_b + (HALO - 3) * (1 - odd) + 2 * odd
+    for k in range(field.shape[0]):
+        field[k, third, rows_lon:] = pltpu.roll(field[k, second, rows_lon:], 8 - FOLD, 0)
+
+
+def sides_kernel(part_a, part_b, cross, folded):
+    count, rows_lat, _, levels = part_a.shape
+    even = lax.rem(lax.axis_index("lon"), 2) == 0
+    odd = lax.rem(lax.axis_index("lat"), 2) == 1
+    index = iota((8, levels), 0)
+    inner = (index == FOLD - 1) | (index == FOLD)
+    for k in range(count):
+        rows = []
+        for a in range(rows_lat):
+            first = jnp.where(even, part_a[k, a], part_b[k, a])
+            second = jnp.where(even, part_b[k, a], part_a[k, a])
+            rows.append(jnp.concatenate([first, second], axis=0))
+            cross[k, a] = rows[a]
+        near = [jnp.where(odd, rows[rows_lat - 1 - r], rows[r]) for r in range(HALO - 1)]
+        folded[k, 0] = near[0]
+        folded[k, 1] = jnp.where(inner, pltpu.roll(near[2], FOLD, 0), near[1])
+
+
+def keep_copy(field, kept, sems):
+    inner = pl.ds(HALO // 2, field.shape[1] - HALO)
+    return pltpu.make_async_copy(field.at[:, inner], kept, sems.at[7])
+
+
 def smooth_power(field, powers, out, order):
-    count, rows, width, levels = field.shape
-    rows_lat = rows - 2 * HALO
+    count, rows, width, _ = field.shape
+    rows_lat = rows - 2 * order
     rows_lon = width - 8
     lat = lax.axis_index("lat")
     north = (lat > 0).astype(F32)
@@ -177,22 +240,21 @@
     def one(k, carry):
         for c in range(width // 8):
             cols = slice(8 * c, 8 * c + 8)
-            low = HALO - order
-            line = {i: field[k, i, cols] for i in range(low, rows - low)}
+            line = {i: field[k, i, cols] for i in range(rows)}
             for m in range(1, order + 1):
                 fresh = {}
-                for i in range(low + m, rows - low - m):
+                for i in range(m, rows - m):
                     value = line[i - 1] + line[i + 1]
-                    if i < HALO:
+                    if i < order:
                         value = value * north
-                    if i >= HALO + rows_lat:
+                    if i >= order + rows_lat:
                         value = value * south
                     fresh[i] = value
                 line = fresh
                 for i in range(rows_lat):
-                    powers[m - 1, i, cols] = line[HALO + i]
+                    powers[m - 1, i, cols] = line[order + i]
         for i in range(rows_lat):
-            value = field[k, HALO + i]
+            value = field[k, order + i]
             for m in range(1, order + 1):
                 ring = pltpu.roll(value, 1, 0) + pltpu.roll(value, width - 1, 0)
                 value = CENTER * value + SMOOTH * ring
@@ -229,7 +291,7 @@
 
 def middle_kernel(
     own, lat_a, lat_b, cross, corner_a, corner_b, ens_hbm, feat, ivert, squares,
-    image, fields, edge_a, edge_b,
+    image, kept, fields, edge_a, edge_b,
     ens, field, powers, smooth, mixed, weights, grad, sem, sems,
 ):
     copies = halo_copies(own, lat_a, lat_b, cross, corner_a, corner_b, field, sems)
@@ -237,22 +299,26 @@
         copy.start()
     ens_copy = pltpu.make_async_copy(ens_hbm, ens, sem)
     ens_copy.start()
-    members, windows, rows_lat, rows_lon, levels = ens.shape
+    _, windows, rows_lat, rows_lon, _ = ens.shape
     fill_weights(feat, weights, windows, rows_lat, rows_lon)
-    for copy in copies:
-        copy.wait()
+    wait_all(copies)
+    unfold_corner(field, rows_lon)
+    keep = keep_copy(field, kept, sems)
+    keep.start()
     seen = observe(field, powers, smooth, mixed, squares, ivert, weights, ens, ens_copy)
     scaled = seen * feat[7:8]
     image[...] = jnp.zeros_like(image)
     image[0:1] = seen
     image[1:2] = scaled
-    adjoint_fields(scaled, weights, ivert, ens, grad, fields, edge_a, edge_b)
+    outs = (fields, edge_a, edge_b)
+    adjoint_fields(scaled, weights, ivert, ens, (), grad, outs)
+    keep.wait()
 
 
 def last_kernel(
     slots,
-    own, lat_a, lat_b, cross, corner_a, corner_b, ens_hbm, feat, ivert, squares, image,
-    send,
+    own, lat_a, lat_b, cross, corner_a, corner_b, ens_hbm, early, feat, ivert, squares, image,
+    send, kept,
     ens, field, powers, smooth, mixed, weights, terms, sem, sems,
 ):
     copies = halo_copies(own, lat_a, lat_b, cross, corner_a, corner_b, field, sems)
@@ -260,10 +326,12 @@
         copy.start()
     ens_copy = pltpu.make_async_copy(ens_hbm, ens, sem)
     ens_copy.start()
-    members, windows, rows_lat, rows_lon, levels = ens.shape
+    _, windows, rows_lat, rows_lon, _ = ens.shape
     fill_weights(feat, weights, windows, rows_lat, rows_lon)
-    for copy in copies:
-        copy.wait()
+    wait_all(copies)
+    unfold_corner(field, rows_lon)
+    keep = keep_copy(field, kept, sems)
+    keep.start()
     second = observe(field, powers, smooth, mixed, squares, ivert, weights, ens, ens_copy)
     start = feat[6:7]
     rinv = feat[7:8]
@@ -309,27 +377,43 @@
         block = jnp.where(row == 2, line, block)
         block = jnp.where(row == 3, guess, block)
         send[g * per : (g + 1) * per] = jnp.broadcast_to(block[None], (per, 8, LANES))
+    keep.wait()
 
 
 def control_kernel(
-    own, lat_a, lat_b, cross, corner_a, corner_b, vert_loc, static_vert,
+    kept, vert_hbm, static_hbm,
     control,
-    field, powers, smooth, sems,
+    field, powers, smooth, result, vert_loc, static_vert, sems, out_sems,
 ):
-    copies = halo_copies(own, lat_a, lat_b, cross, corner_a, corner_b, field, sems)
-    for copy in copies:
-        copy.start()
-    for copy in copies:
-        copy.wait()
+    copies = fetch((vert_hbm, static_hbm, kept), (vert_loc, static_vert, field), sems)
+    wait_all(copies)
+    count, rows_lat, rows_lon, levels = smooth.shape
     smooth_power(field, powers, smooth, 2)
-    count, rows_lat, rows_lon, levels = smooth.shape
+    stores = []
     for k in range(count):
-        scale, matrix = (BETA_ENSEMBLE, vert_loc) if k < count - 1 else (BETA_STATIC, static_vert)
+        member = k < count - 1
+        scale, matrix = (BETA_ENSEMBLE, vert_loc) if member else (BETA_STATIC, static_vert)
         value = dot(smooth[k].reshape(rows_lat * rows_lon, levels), matrix[...], ((1,), (1,)))
-        control[k] = (scale * value).reshape(rows_lat, rows_lon, levels)
-
-
-def final_kernel(recv, dest, lane, early, late, static, member, equivalent):
+        result[k] = (scale * value).reshape(rows_lat, rows_lon, levels)
+        stores.append(pltpu.make_async_copy(result.at[k], control.at[k], out_sems.at[k]))
+        stores[k].start()
+    wait_all(stores)
+
+
+def final_kernel(
+    recv, dest_hbm, lane_hbm, early_hbm, late_hbm,
+    static_hbm, member_hbm, equivalent,
+    dest, lane, early, late, result, sems, field_sems,
+):
+    small = fetch((dest_hbm, lane_hbm), (dest, lane), sems)
+    count = early.shape[0]
+    large = []
+    for k in range(count):
+        large.append(
+            fetch(
+                (early_hbm.at[k], late_hbm.at[k]), (early.at[k], late.at[k]), field_sems.at[k]
+            )
+        )
     owners = recv.shape[0]
     rows = dest.shape[1]
     blocks = recv[...]
@@ -354,10 +438,14 @@
     step_next = jnp.minimum(step_next, 1.0)
     near = step + step_next * ((1.0 - step) + beta)
     far = -step_next * step
-    members = member.shape[0]
-    for k in range(members):
-        member[k] = near[None] * early[k] + far[None] * late[k]
-    static[...] = near[None] * early[members] + far[None] * late[members]
+    stores = []
+    for k in range(count):
+        wait_all(large[k])
+        result[k] = near[None] * early[k] + far[None] * late[k]
+        target = member_hbm.at[k] if k < count - 1 else static_hbm
+        stores.append(pltpu.make_async_copy(result.at[k], target, field_sems.at[k, 2]))
+        stores[k].start()
+    wait_all(small)
     kind = iota((owners, 8, rows), 1)
     factor = jnp.where(kind == 0, near[None], jnp.where(kind == 1, far[None], 0.0))
     chosen = iota((owners, 8, rows), 0) == dest[...].reshape(1, 1, rows)
@@ -366,10 +454,15 @@
     equivalent[...] = jnp.sum(
         jnp.where(iota((LANES, rows), 0) == lane[...], table, 0.0), axis=0, keepdims=True
     )
+    wait_all(stores)
 
 
 def shape(*dims):
     return jax.ShapeDtypeStruct(dims, F32)
+
+
+def stay(*values):
+    return [pltpu.with_memory_space_constraint(value, pltpu.HBM) for value in values]
 
 
 def swaps(count, ring):
@@ -409,28 +502,37 @@
     lat_inner, lat_outer = swaps(lat_count, False)
     lon_inner, lon_outer = swaps(lon_count, True)
     tile = shape(count, rows_lat, rows_lon, levels)
-    edge = shape(count, rows_lat, 8, levels)
+    edge = shape(count, rows_lat, HALO, levels)
 
     def line(values):
         return values.reshape(1, rows)
 
     dest = line(obs_dest)
+    row_scratch = pltpu.VMEM((1, rows), jnp.int32)
     send, lane = pl.pallas_call(
         functools.partial(pack_kernel, slots, patches),
-        out_shape=(shape(owners, 8, LANES), jax.ShapeDtypeStruct((1, rows), jnp.int32)),
-        in_specs=[VMEM] * 7 + [SMEM],
-        out_specs=(VMEM, VMEM),
-        scratch_shapes=[pltpu.VMEM((8, rows), F32)],
+        out_shape=(shape(owners, 8, LANES), pltpu.HBM((1, rows), jnp.int32)),
+        in_specs=[HBM] * 6 + [SMEM],
+        out_specs=(VMEM, HBM),
+        scratch_shapes=[row_scratch] * 4
+        + [
+            pltpu.VMEM(obs_hweight.shape, F32),
+            pltpu.VMEM((1, rows), F32),
+            pltpu.VMEM((8, rows), F32),
+            row_scratch,
+            DMA((7,)),
+        ],
         compiler_params=PARAMS,
         name="pack",
     )(
-        obs_dest,
-        dest,
-        line(obs_patch),
-        line(obs_window),
-        line(obs_inst),
-        obs_hweight,
-        line(innovation),
+        *stay(
+            dest,
+            line(obs_patch),
+            line(obs_window),
+            line(obs_inst),
+            obs_hweight,
+            line(innovation),
+        ),
         obs_count,
     )
     squares = pl.pallas_call(
@@ -453,67 +555,93 @@
     def powers(order):
         return pltpu.VMEM((order, rows_lat, width, levels), F32)
 
-    feat, ivert, fields, edge_a, edge_b = pl.pallas_call(
+    feat, ivert, *outs = pl.pallas_call(
         functools.partial(first_kernel, slots),
         out_shape=(shape(8, total), shape(levels, total), tile, edge, edge),
-        in_specs=[VMEM, VMEM, VMEM, ANY],
+        in_specs=[VMEM, HBM, HBM, HBM],
         out_specs=(VMEM,) * 5,
-        scratch_shapes=[ens_scratch, weight_scratch, grad_scratch, pltpu.SemaphoreType.DMA],
+        scratch_shapes=[
+            pltpu.VMEM(inst_vert.shape, F32),
+            pltpu.VMEM((1, inst_err.shape[0]), F32),
+            ens_scratch,
+            weight_scratch,
+            grad_scratch,
+            DMA((2 + members,)),
+        ],
         compiler_params=PARAMS,
         name="first",
-    )(recv, inst_vert, inst_err.reshape(1, -1), ensemble)
+    )(recv, *stay(inst_vert, inst_err.reshape(1, -1), ensemble))
+
+    def sides(part_a, part_b):
+        return pl.pallas_call(
+            sides_kernel,
+            out_shape=(
+                shape(count, rows_lat, 8, levels),
+                shape(count, 2, 8, levels),
+            ),
+            in_specs=[VMEM] * 2,
+            out_specs=(VMEM,) * 2,
+            compiler_params=PARAMS,
+            name="sides",
+        )(part_a, part_b)
 
     def halo(fields, edge_a, edge_b):
         lat_b = lax.ppermute(fields, "lat", lat_outer)
         side_a = lax.ppermute(edge_a, "lon", lon_inner)
         side_b = lax.ppermute(edge_b, "lon", lon_outer)
         lat_a = lax.ppermute(fields, "lat", lat_inner)
-        cross = side_a + side_b
-        corner_b = lax.ppermute(cross, "lat", lat_outer)
+        cross, folded = sides(side_a, side_b)
+        corner_b = lax.ppermute(folded, "lat", lat_outer)
         corner_a = lax.ppermute(cross, "lat", lat_inner)
         return (fields, lat_a, lat_b, cross, corner_a, corner_b)
 
-    def control(parts):
+    def control(kept):
         return pl.pallas_call(
             control_kernel,
-            out_shape=tile,
-            in_specs=[ANY] * 6 + [VMEM] * 2,
-            out_specs=VMEM,
+            out_shape=pltpu.HBM(tile.shape, F32),
+            in_specs=[HBM] * 3,
+            out_specs=HBM,
             scratch_shapes=[
-                field_scratch,
+                pltpu.VMEM(kept_shape.shape, F32),
                 powers(2),
                 tile_scratch,
-                pltpu.SemaphoreType.DMA((6,)),
+                tile_scratch,
+                matrix_scratch,
+                matrix_scratch,
+                DMA((3,)),
+                DMA((count,)),
             ],
             compiler_params=PARAMS,
             name="control",
-        )(*parts, vert_loc, static_vert)
-
-    parts = halo(fields, edge_a, edge_b)
+        )(*stay(kept, vert_loc, static_vert))
+
+    parts = halo(*outs)
+    matrix_scratch = pltpu.VMEM(vert_loc.shape, F32)
     work = [ens_scratch, field_scratch, powers(4), tile_scratch, tile_scratch, weight_scratch]
-    sems = [pltpu.SemaphoreType.DMA, pltpu.SemaphoreType.DMA((6,))]
-    image, fields, edge_a, edge_b = pl.pallas_call(
+    sems = [DMA, DMA((8,))]
+    kept_shape = pltpu.HBM((count, rows_lat + HALO, width, levels), F32)
+    image, kept, *outs = pl.pallas_call(
         middle_kernel,
-        out_shape=(shape(8, total), tile, edge, edge),
-        in_specs=[ANY] * 7 + [VMEM] * 3,
-        out_specs=(VMEM,) * 4,
+        out_shape=(shape(8, total), kept_shape, tile, edge, edge),
+        in_specs=[ANY] * 6 + [HBM] + [VMEM] * 3,
+        out_specs=(VMEM, HBM) + (VMEM,) * 3,
         scratch_shapes=work + [grad_scratch] + sems,
         compiler_params=PARAMS,
         name="middle",
-    )(*parts, ensemble, feat, ivert, squares)
-    early = control(parts)
-    parts = halo(fields, edge_a, edge_b)
-    send = pl.pallas_call(
+    )(*parts, *stay(ensemble), feat, ivert, squares)
+    early = control(kept)
+    parts = halo(*outs)
+    send, kept = pl.pallas_call(
         functools.partial(last_kernel, slots),
-        out_shape=shape(owners, 8, LANES),
-        in_specs=[ANY] * 7 + [VMEM] * 4,
-        out_specs=VMEM,
+        out_shape=(shape(owners, 8, LANES), kept_shape),
+        in_specs=[ANY] * 6 + [HBM] * 2 + [VMEM] * 4,
+        out_specs=(VMEM, HBM),
         scratch_shapes=work + [pltpu.VMEM((16, total), F32)] + sems,
         compiler_params=PARAMS,
         name="last",
-    )(*parts, ensemble, feat, ivert, squares, image)
-    late = control(parts)
+    )(*parts, *stay(ensemble, early), feat, ivert, squares, image)
     recv = exchange(send)
+    late = control(kept)
     static, member, equivalent = pl.pallas_call(
         final_kernel,
         out_shape=(
@@ -521,9 +649,20 @@
             shape(members, rows_lat, rows_lon, levels),
             shape(1, rows),
         ),
+        in_specs=[VMEM] + [HBM] * 4,
+        out_specs=(HBM, HBM, VMEM),
+        scratch_shapes=[
+            row_scratch,
+            row_scratch,
+            tile_scratch,
+            tile_scratch,
+            tile_scratch,
+            DMA((2,)),
+            DMA((count, 3)),
+        ],
         compiler_params=PARAMS,
         name="final",
-    )(recv, dest, lane, early, late)
+    )(recv, *stay(dest, lane, early, late))
     return static, member, equivalent.reshape(rows)
 
 

time: 96.7 us -> 81.7 us (0.84)
  local copies, waits for them, and re-layouts: 18.6 us -> 0.01 us
  Pallas kernels: 21.5 us -> 29 us
  starting transfers between devices: 24.6 us -> 21.5 us
    unnamed x69 -> x4, local copies, waits for them, and re-layouts: 18.6 us -> 0.01 us
    ppermute x2, waiting for transfers between devices: 9.61 us -> 4.1 us  [halo(): side_a = lax.ppermute(edge_a, 'lon', lon_inner)]
    pallas_call x4 -> x6, Pallas kernels: 15.8 us -> 20.8 us  [the longest x2 8.93 us: control(): pl.pallas_call(control_kernel, out_shape=pltpu.HBM(tile.shape, F32), in_s...]
    ppermute x2, starting transfers between devices: 4.49 us -> 0.14 us  [halo(): corner_a = lax.ppermute(cross, 'lat', lat_inner)]
    all_to_all x1, waiting for transfers between devices: 0.01 us -> 3.33 us  [exchange(): lax.all_to_all(blocks, ('lat', 'lon'), split_axis=0, concat_axis=0, tiled...]
    ppermute x2, waiting for transfers between devices: 3.48 us -> 6.31 us  [halo(): side_b = lax.ppermute(edge_b, 'lon', lon_outer)]
    ppermute x2, starting transfers between devices: 7.08 us -> 9.01 us  [halo(): lat_a = lax.ppermute(fields, 'lat', lat_inner)]
    ppermute x2, waiting for transfers between devices: 1.67 us -> 0.34 us  [halo(): corner_a = lax.ppermute(cross, 'lat', lat_inner)]
  transfers between devices with their start and end apart: 13 -> 13, of which waited for: 6 -> 6; matrix products, arithmetic and copies ran while one was open for 0% -> 0% of each run, Pallas kernels for 5% -> 11%
where the time goes in v1:
time: 81.7 us; the launch traced here: 81.3 us
  Pallas kernels  29 us (35%)
  starting transfers between devices  21.5 us (26%)
  blocking collectives  14.9 us (18%)
  waiting for transfers between devices  14.1 us (17%)
  between operations  1.67 us (2%)
    all_to_all x1, blocking collectives, exchange(): lax.all_to_all(blocks, ('lat', 'lon'), split_axis=0, concat_axis=0, tiled...  14.9 us
    ppermute x2, starting transfers between devices, halo(): lat_a = lax.ppermute(fields, 'lat', lat_inner)  9.01 us
    pallas_call x2, Pallas kernels, control(): pl.pallas_call(control_kernel, out_shape=pltpu.HBM(tile.shape, F32), in_s...  8.93 us
    pallas_call x1, Pallas kernels, body(): pl.pallas_call(middle_kernel, out_shape=(shape(8, total), kept_shape, til...  6.32 us
    ppermute x2, waiting for transfers between devices, halo(): side_b = lax.ppermute(edge_b, 'lon', lon_outer)  6.31 us
    pallas_call x1, Pallas kernels, body(): pl.pallas_call(functools.partial(last_kernel, slots), out_shape=(shape(ow...  5.49 us
    all_to_all x1, starting transfers between devices, exchange(): lax.all_to_all(blocks, ('lat', 'lon'), split_axis=0, concat_axis=0, tiled...  4.84 us
    ppermute x2, waiting for transfers between devices, halo(): side_a = lax.ppermute(edge_a, 'lon', lon_inner)  4.1 us
  transfers between devices with their start and end apart: 13, of which 6 were waited for; matrix products, arithmetic and copies ran while one was open for 0% of the time, Pallas kernels for 11%

profile of v1, /device:TPU:0, one launch (start us, length us, event | category | flops | bytes accessed | tf_op | source)
XLA Modules:
  0.0 81.3 jit_solution(18215673124116947919)
XLA Ops:
  0.6 0.0 copy-start.1
  0.6 0.0 copy-start
  1.3 1.6 %pack.1 = (f32[32,8,128]{2,1,0:T(8,128)S(1)}, s32[1,256]{1,0:T(1,128)}) custom-call(s32[1,256]{1,0:T(1,128)} %bitcast.7, s32[1,256]{1,0:T(1,128)} %bitcast.9, s32[1,256]{1,0:T(1,128)} %bitcast.10, s32[1,256]{1,0:T(1,128)} %bitcast.11, f32[4,256]{1,0:T(4,128)} %hweight_hbm.1, f32[1,256]{1,0:T(1,128)} %bitcast.12, s32[1]{0:T(128)S(6)} %copy.15.count), custom_call_target="tpu_custom_call" | custom-call | tf_op jit(solution)/shard_map/pack/pallas_call | solution.py:512
  2.9 14.9 %all_to_all.10.recv = f32[32,8,128]{2,1,0:T(8,128)S(1)} all-to-all(f32[32,8,128]{2,1,0:T(8,128)S(1)} %get-tuple-element.24), channel_id=1, replica_groups=mesh['lat'=4,'lon'=8] {'lat','lon'}, dimensions={0} | all-to-all | bytes 262144 | tf_op jit(solution)/shard_map/all_to_all | solution.py:546
  17.9 3.0 %first.1 = (f32[8,512]{1,0:T(8,128)S(1)}, f32[128,512]{1,0:T(8,128)S(1)}, f32[9,4,48,128]{3,2,1,0:T(8,128)S(1)}, f32[9,4,4,128]{3,2,1,0:T(4,128)S(1)}, f32[9,4,4,128]{3,2,1,0:T(4,128)S(1)}) custom-call(f32[32,8,128]{2,1,0:T(8,128)S(1)} %all_to_all.10.recv, f32[16,128]{1,0:T(8,128)} %inst_vert_hbm.1, f32[1,16]{1,0:T(1,128)} %bitcast.13, ...), custom_call_target="tpu_custom_call" | custom-call | tf_op jit(solution)/shard_map/first/pallas_call | solution.py:558
  20.9 0.7 collective-permute-start.1
  21.6 2.3 %collective-permute-start = (f32[9,4,48,128]{3,2,1,0:T(8,128)S(1)}, f32[9,4,48,128]{3,2,1,0:T(8,128)S(1)}, u32[]{:S(2)}, u32[]{:S(2)}) collective-permute-start(f32[9,4,48,128]{3,2,1,0:T(8,128)S(1)} %get-tuple-element.25.own), channel_id=1, source_target_pairs={{0,8},{8,0},{16,24},{24,16},{1,9},{9,1},{17,25},{25,17},{2,10},{10... | collective-permute-start | bytes 2654216 | tf_op jit(solution)/shard_map/ppermute | solution.py:592
  24.0 0.9 %collective-permute-start.2 = (f32[9,4,4,128]{3,2,1,0:T(4,128)S(1)}, f32[9,4,4,128]{3,2,1,0:T(4,128)S(1)}, u32[]{:S(2)}, u32[]{:S(2)}) collective-permute-start(f32[9,4,4,128]{3,2,1,0:T(4,128)S(1)} %get-tuple-element.26), channel_id=1, source_target_pairs={{0,1},{1,0},{2,3},{3,2},{4,5},{5,4},{6,7},{7,6},{8,9},{9,8},{10,11... | collective-permute-start | bytes 221192 | tf_op jit(solution)/shard_map/ppermute | solution.py:590
  24.9 2.1 %collective-permute-start.3 = (f32[9,4,4,128]{3,2,1,0:T(4,128)S(1)}, f32[9,4,4,128]{3,2,1,0:T(4,128)S(1)}, u32[]{:S(2)}, u32[]{:S(2)}) collective-permute-start(f32[9,4,4,128]{3,2,1,0:T(4,128)S(1)} %get-tuple-element.27), channel_id=1, source_target_pairs={{1,2},{2,1},{3,4},{4,3},{5,6},{6,5},{7,0},{0,7},{9,10},{10,9},{11,... | collective-permute-start | bytes 221192 | tf_op jit(solution)/shard_map/ppermute | solution.py:591
  27.0 1.3 %collective-permute-done.2.part_a = f32[9,4,4,128]{3,2,1,0:T(4,128)S(1)} collective-permute-done((f32[9,4,4,128]{3,2,1,0:T(4,128)S(1)}, f32[9,4,4,128]{3,2,1,0:T(4,128)S(1)}, u32[]{:S(2)}, u32[]{:S(2)}) %collective-permute-start.2) | collective-permute-done | bytes 73760 | tf_op jit(solution)/shard_map/ppermute | solution.py:590
  28.3 3.6 %collective-permute-done.3.part_b = f32[9,4,4,128]{3,2,1,0:T(4,128)S(1)} collective-permute-done((f32[9,4,4,128]{3,2,1,0:T(4,128)S(1)}, f32[9,4,4,128]{3,2,1,0:T(4,128)S(1)}, u32[]{:S(2)}, u32[]{:S(2)}) %collective-permute-start.3) | collective-permute-done | bytes 73760 | tf_op jit(solution)/shard_map/ppermute | solution.py:591
  32.0 0.1 collective-permute-start.4
  32.1 0.7 collective-permute-start.5
  32.7 0.0 copy-done.1
  32.7 0.0 copy-done
  32.7 0.3 prepare.1.squares
  33.1 0.0 collective-permute-done.5.corner_b
  33.1 0.3 collective-permute-done.4.corner_a
  33.4 0.0 collective-permute-done.1.lat_b
  33.4 0.0 collective-permute-done.lat_a
  33.4 6.3 %middle.1 = (f32[8,512]{1,0:T(8,128)S(1)}, f32[9,8,56,128]{3,2,1,0:T(8,128)}, f32[9,4,48,128]{3,2,1,0:T(8,128)S(1)}, f32[9,4,4,128]{3,2,1,0:T(4,128)S(1)}, f32[9,4,4,128]{3,2,1,0:T(4,128)S(1)}) custom-call(f32[9,4,48,128]{3,2,1,0:T(8,128)S(1)} %get-tuple-element.25.own, f32[9,4,48,128]{3,2,1,0:T(8,128)S(1)} %collective-permute-done.lat_a, ...), custom_call_target="tpu_custom_call" | custom-call | tf_op jit(solution)/shard_map/middle/pallas_call | solution.py:623
  39.7 0.7 collective-permute-start.7
  40.5 6.7 %collective-permute-start.6 = (f32[9,4,48,128]{3,2,1,0:T(8,128)S(1)}, f32[9,4,48,128]{3,2,1,0:T(8,128)S(1)}, u32[]{:S(2)}, u32[]{:S(2)}) collective-permute-start(f32[9,4,48,128]{3,2,1,0:T(8,128)S(1)} %get-tuple-element.32.own), channel_id=1, source_target_pairs={{0,8},{8,0},{16,24},{24,16},{1,9},{9,1},{17,25},{25,17},{2,10},{10... | collective-permute-start | bytes 2654216 | tf_op jit(solution)/shard_map/ppermute | solution.py:592
  47.1 0.0 collective-permute-start.8
  47.1 1.6 %collective-permute-start.9 = (f32[9,4,4,128]{3,2,1,0:T(4,128)S(1)}, f32[9,4,4,128]{3,2,1,0:T(4,128)S(1)}, u32[]{:S(2)}, u32[]{:S(2)}) collective-permute-start(f32[9,4,4,128]{3,2,1,0:T(4,128)S(1)} %get-tuple-element.34), channel_id=1, source_target_pairs={{1,2},{2,1},{3,4},{4,3},{5,6},{6,5},{7,0},{0,7},{9,10},{10,9},{11,... | collective-permute-start | bytes 221192 | tf_op jit(solution)/shard_map/ppermute | solution.py:591
  48.7 2.8 %collective-permute-done.8.part_a = f32[9,4,4,128]{3,2,1,0:T(4,128)S(1)} collective-permute-done((f32[9,4,4,128]{3,2,1,0:T(4,128)S(1)}, f32[9,4,4,128]{3,2,1,0:T(4,128)S(1)}, u32[]{:S(2)}, u32[]{:S(2)}) %collective-permute-start.8) | collective-permute-done | bytes 73760 | tf_op jit(solution)/shard_map/ppermute | solution.py:590
  51.5 2.7 %collective-permute-done.9.part_b = f32[9,4,4,128]{3,2,1,0:T(4,128)S(1)} collective-permute-done((f32[9,4,4,128]{3,2,1,0:T(4,128)S(1)}, f32[9,4,4,128]{3,2,1,0:T(4,128)S(1)}, u32[]{:S(2)}, u32[]{:S(2)}) %collective-permute-start.9) | collective-permute-done | bytes 73760 | tf_op jit(solution)/shard_map/ppermute | solution.py:591
  54.2 0.1 collective-permute-start.10
  54.3 0.8 %collective-permute-start.11 = (f32[9,2,8,128]{3,2,1,0:T(8,128)S(1)}, f32[9,2,8,128]{3,2,1,0:T(8,128)S(1)}, u32[]{:S(2)}, u32[]{:S(2)}) collective-permute-start(f32[9,2,8,128]{3,2,1,0:T(8,128)S(1)} %get-tuple-element.36), channel_id=1, source_target_pairs={{8,16},{16,8},{9,17},{17,9},{10,18},{18,10},{11,19},{19,11},{12,20... | collective-permute-start | bytes 221192 | tf_op jit(solution)/shard_map/ppermute | solution.py:594
  55.2 4.5 %control.2.early.early_hbm = f32[9,4,48,128]{3,2,1,0:T(8,128)} custom-call(f32[9,8,56,128]{3,2,1,0:T(8,128)} %get-tuple-element.37.kept, f32[128,128]{1,0:T(8,128)} %vert_hbm.3, f32[128,128]{1,0:T(8,128)} %static_hbm.3), custom_call_target="tpu_custom_call" | custom-call | tf_op jit(solution)/shard_map/control/pallas_call | solution.py:599
  59.6 0.0 collective-permute-done.11.corner_b
  59.6 0.0 collective-permute-done.10.corner_a
  59.7 0.0 collective-permute-done.7.lat_b
  59.7 0.0 collective-permute-done.6.lat_a
  59.7 5.5 %last.1 = (f32[32,8,128]{2,1,0:T(8,128)}, f32[9,8,56,128]{3,2,1,0:T(8,128)}) custom-call(f32[9,4,48,128]{3,2,1,0:T(8,128)S(1)} %get-tuple-element.32.own, f32[9,4,48,128]{3,2,1,0:T(8,128)S(1)} %collective-permute-done.6.lat_a, f32[9,4,48,128]{3,2,1,0:T(8,128)S(1)} %collective-permute-done.7.lat_b, f32[9,4,8,128]{3,2,1,0:T(8,128)S(1)} %get-tuple-element.35.cross, ...), custom_call_target="tpu_custom_call" | custom-call | tf_op jit(solution)/shard_map/last/pallas_call | solution.py:634
  65.2 4.8 %all-to-all-start.1 = ((f32[32,8,128]{2,1,0:T(8,128)}), f32[32,8,128]{2,1,0:T(8,128)S(1)}, u32[]{:S(2)}, u32[]{:S(2)}) async-start(f32[32,8,128]{2,1,0:T(8,128)} %get-tuple-element.39), calls=%async_computation.1 | async-start | bytes 262144 | tf_op jit(solution)/shard_map/all_to_all | solution.py:546
  70.0 4.5 %control.3.late_hbm = f32[9,4,48,128]{3,2,1,0:T(8,128)} custom-call(f32[9,8,56,128]{3,2,1,0:T(8,128)} %get-tuple-element.41.kept, f32[128,128]{1,0:T(8,128)} %vert_hbm.3, f32[128,128]{1,0:T(8,128)} %static_hbm.3), custom_call_target="tpu_custom_call" | custom-call | tf_op jit(solution)/shard_map/control/pallas_call | solution.py:599
  74.5 3.3 %all-to-all-done.1.recv = f32[32,8,128]{2,1,0:T(8,128)S(1)} async-done(((f32[32,8,128]{2,1,0:T(8,128)}), f32[32,8,128]{2,1,0:T(8,128)S(1)}, u32[]{:S(2)}, u32[]{:S(2)}) %all-to-all-start.1) | async-done | bytes 131104 | tf_op jit(solution)/shard_map/all_to_all | solution.py:546
  77.8 3.3 %final.1 = (f32[4,48,128]{2,1,0:T(8,128)}, f32[8,4,48,128]{3,2,1,0:T(8,128)}, f32[1,256]{1,0:T(1,128)}) custom-call(f32[32,8,128]{2,1,0:T(8,128)S(1)} %all-to-all-done.1.recv, s32[1,256]{1,0:T(1,128)} %bitcast.8, s32[1,256]{1,0:T(1,128)} %get-tuple-element.40.lane_hbm, f32[9,4,48,128]{3,2,1,0:T(8,128)} %control.2.early.early_hbm, ...), custom_call_target="tpu_custom_call" | custom-call | tf_op jit(solution)/shard_map/final/pallas_call | solution.py:645
  (2 shorter events, 0.1 us)
Async XLA Ops:
  0.6 32.1 %copy-start.1 = (f32[128,128]{1,0:T(8,128)S(1)}, f32[128,128]{1,0:T(8,128)}, u32[]{:S(2)}) copy-start(f32[128,128]{1,0:T(8,128)} %static_hbm.3) | copy-start | bytes 196612
  0.6 32.1 %copy-start = (f32[128,128]{1,0:T(8,128)S(1)}, f32[128,128]{1,0:T(8,128)}, u32[]{:S(2)}) copy-start(f32[128,128]{1,0:T(8,128)} %vert_hbm.3) | copy-start | bytes 196612
  20.9 12.5 %collective-permute-start.1 = (f32[9,4,48,128]{3,2,1,0:T(8,128)S(1)}, f32[9,4,48,128]{3,2,1,0:T(8,128)S(1)}, u32[]{:S(2)}, u32[]{:S(2)}) collective-permute-start(f32[9,4,48,128]{3,2,1,0:T(8,128)S(1)} %get-tuple-element.25.own), channel_id=1, source_target_pairs={{8,16},{16,8},{9,17},{17,9},{10,18},{18,10},{11,19},{19,11},{12,20... | collective-permute-start | bytes 2654216 | tf_op jit(solution)/shard_map/ppermute | solution.py:589
  21.6 11.8 %collective-permute-start = (f32[9,4,48,128]{3,2,1,0:T(8,128)S(1)}, f32[9,4,48,128]{3,2,1,0:T(8,128)S(1)}, u32[]{:S(2)}, u32[]{:S(2)}) collective-permute-start(f32[9,4,48,128]{3,2,1,0:T(8,128)S(1)} %get-tuple-element.25.own), channel_id=1, source_target_pairs={{0,8},{8,0},{16,24},{24,16},{1,9},{9,1},{17,25},{25,17},{2,10},{10... | collective-permute-start | bytes 2654216 | tf_op jit(solution)/shard_map/ppermute | solution.py:592
  24.0 4.4 %collective-permute-start.2 = (f32[9,4,4,128]{3,2,1,0:T(4,128)S(1)}, f32[9,4,4,128]{3,2,1,0:T(4,128)S(1)}, u32[]{:S(2)}, u32[]{:S(2)}) collective-permute-start(f32[9,4,4,128]{3,2,1,0:T(4,128)S(1)} %get-tuple-element.26), channel_id=1, source_target_pairs={{0,1},{1,0},{2,3},{3,2},{4,5},{5,4},{6,7},{7,6},{8,9},{9,8},{10,11... | collective-permute-start | bytes 221192 | tf_op jit(solution)/shard_map/ppermute | solution.py:590
  24.9 7.0 %collective-permute-start.3 = (f32[9,4,4,128]{3,2,1,0:T(4,128)S(1)}, f32[9,4,4,128]{3,2,1,0:T(4,128)S(1)}, u32[]{:S(2)}, u32[]{:S(2)}) collective-permute-start(f32[9,4,4,128]{3,2,1,0:T(4,128)S(1)} %get-tuple-element.27), channel_id=1, source_target_pairs={{1,2},{2,1},{3,4},{4,3},{5,6},{6,5},{7,0},{0,7},{9,10},{10,9},{11,... | collective-permute-start | bytes 221192 | tf_op jit(solution)/shard_map/ppermute | solution.py:591
  32.0 1.4 %collective-permute-start.4 = (f32[9,4,8,128]{3,2,1,0:T(8,128)S(1)}, f32[9,4,8,128]{3,2,1,0:T(8,128)S(1)}, u32[]{:S(2)}, u32[]{:S(2)}) collective-permute-start(f32[9,4,8,128]{3,2,1,0:T(8,128)S(1)} %get-tuple-element.28.cross), channel_id=1, source_target_pairs={{0,8},{8,0},{16,24},{24,16},{1,9},{9,1},{17,25},{25,17},{2,10},{10... | collective-permute-start | bytes 442376 | tf_op jit(solution)/shard_map/ppermute | solution.py:595
  32.1 1.0 %collective-permute-start.5 = (f32[9,2,8,128]{3,2,1,0:T(8,128)S(1)}, f32[9,2,8,128]{3,2,1,0:T(8,128)S(1)}, u32[]{:S(2)}, u32[]{:S(2)}) collective-permute-start(f32[9,2,8,128]{3,2,1,0:T(8,128)S(1)} %get-tuple-element.29), channel_id=1, source_target_pairs={{8,16},{16,8},{9,17},{17,9},{10,18},{18,10},{11,19},{19,11},{12,20... | collective-permute-start | bytes 221192 | tf_op jit(solution)/shard_map/ppermute | solution.py:594
  39.7 19.9 %collective-permute-start.7 = (f32[9,4,48,128]{3,2,1,0:T(8,128)S(1)}, f32[9,4,48,128]{3,2,1,0:T(8,128)S(1)}, u32[]{:S(2)}, u32[]{:S(2)}) collective-permute-start(f32[9,4,48,128]{3,2,1,0:T(8,128)S(1)} %get-tuple-element.32.own), channel_id=1, source_target_pairs={{8,16},{16,8},{9,17},{17,9},{10,18},{18,10},{11,19},{19,11},{12,20... | collective-permute-start | bytes 2654216 | tf_op jit(solution)/shard_map/ppermute | solution.py:589
  40.5 19.2 %collective-permute-start.6 = (f32[9,4,48,128]{3,2,1,0:T(8,128)S(1)}, f32[9,4,48,128]{3,2,1,0:T(8,128)S(1)}, u32[]{:S(2)}, u32[]{:S(2)}) collective-permute-start(f32[9,4,48,128]{3,2,1,0:T(8,128)S(1)} %get-tuple-element.32.own), channel_id=1, source_target_pairs={{0,8},{8,0},{16,24},{24,16},{1,9},{9,1},{17,25},{25,17},{2,10},{10... | collective-permute-start | bytes 2654216 | tf_op jit(solution)/shard_map/ppermute | solution.py:592
  47.1 4.4 %collective-permute-start.8 = (f32[9,4,4,128]{3,2,1,0:T(4,128)S(1)}, f32[9,4,4,128]{3,2,1,0:T(4,128)S(1)}, u32[]{:S(2)}, u32[]{:S(2)}) collective-permute-start(f32[9,4,4,128]{3,2,1,0:T(4,128)S(1)} %get-tuple-element.33), channel_id=1, source_target_pairs={{0,1},{1,0},{2,3},{3,2},{4,5},{5,4},{6,7},{7,6},{8,9},{9,8},{10,11... | collective-permute-start | bytes 221192 | tf_op jit(solution)/shard_map/ppermute | solution.py:590
  47.1 7.0 %collective-permute-start.9 = (f32[9,4,4,128]{3,2,1,0:T(4,128)S(1)}, f32[9,4,4,128]{3,2,1,0:T(4,128)S(1)}, u32[]{:S(2)}, u32[]{:S(2)}) collective-permute-start(f32[9,4,4,128]{3,2,1,0:T(4,128)S(1)} %get-tuple-element.34), channel_id=1, source_target_pairs={{1,2},{2,1},{3,4},{4,3},{5,6},{6,5},{7,0},{0,7},{9,10},{10,9},{11,... | collective-permute-start | bytes 221192 | tf_op jit(solution)/shard_map/ppermute | solution.py:591
  54.2 5.4 %collective-permute-start.10 = (f32[9,4,8,128]{3,2,1,0:T(8,128)S(1)}, f32[9,4,8,128]{3,2,1,0:T(8,128)S(1)}, u32[]{:S(2)}, u32[]{:S(2)}) collective-permute-start(f32[9,4,8,128]{3,2,1,0:T(8,128)S(1)} %get-tuple-element.35.cross), channel_id=1, source_target_pairs={{0,8},{8,0},{16,24},{24,16},{1,9},{9,1},{17,25},{25,17},{2,10},{10... | collective-permute-start | bytes 442376 | tf_op jit(solution)/shard_map/ppermute | solution.py:595
  54.3 5.3 %collective-permute-start.11 = (f32[9,2,8,128]{3,2,1,0:T(8,128)S(1)}, f32[9,2,8,128]{3,2,1,0:T(8,128)S(1)}, u32[]{:S(2)}, u32[]{:S(2)}) collective-permute-start(f32[9,2,8,128]{3,2,1,0:T(8,128)S(1)} %get-tuple-element.36), channel_id=1, source_target_pairs={{8,16},{16,8},{9,17},{17,9},{10,18},{18,10},{11,19},{19,11},{12,20... | collective-permute-start | bytes 221192 | tf_op jit(solution)/shard_map/ppermute | solution.py:594
  65.2 12.7 %all-to-all-start.1 = ((f32[32,8,128]{2,1,0:T(8,128)}), f32[32,8,128]{2,1,0:T(8,128)S(1)}, u32[]{:S(2)}, u32[]{:S(2)}) async-start(f32[32,8,128]{2,1,0:T(8,128)} %get-tuple-element.39), calls=%async_computation.1 | async-start | bytes 262144 | tf_op jit(solution)/shard_map/all_to_all | solution.py:546

commit v2 on v1

--- a/solution.py
+++ b/solution.py
@@ -17,6 +17,7 @@
 LANES = 128
 HIGHEST = lax.Precision.HIGHEST
 F32 = jnp.float32
+BF16 = jnp.bfloat16
 
 ANY = pl.BlockSpec(memory_space=pl.ANY)
 HBM = pl.BlockSpec(memory_space=pltpu.HBM)
@@ -34,6 +35,11 @@
 
 def iota(shape, dim):
     return lax.broadcasted_iota(jnp.int32, shape, dim)
+
+
+def halves(value):
+    high = value.astype(BF16)
+    return high, (value - high.astype(F32)).astype(BF16)
 
 
 def fetch(sources, targets, sems):
@@ -49,6 +55,10 @@
 def wait_all(copies):
     for copy in copies:
         copy.wait()
+
+
+def short_dot(left, right, dims=((1,), (0,))):
+    return lax.dot_general(left, right, (dims, ((), ())), preferred_element_type=F32)
 
 
 def pack_kernel(
@@ -93,32 +103,45 @@
 
 
 def prepare_kernel(vert_loc, static_vert, squares):
-    squares[0] = BETA_ENSEMBLE**2 * dot(vert_loc[...], vert_loc[...], ((0,), (0,)))
-    squares[1] = BETA_STATIC**2 * dot(static_vert[...], static_vert[...], ((0,), (0,)))
-
-
-def fill_weights(feat, weights, windows, rows_lat, rows_lon):
+    levels = vert_loc.shape[0]
+    squares[...] = jnp.zeros_like(squares)
+    for n, (scale, matrix) in enumerate(((BETA_ENSEMBLE, vert_loc), (BETA_STATIC, static_vert))):
+        high, low = halves(scale**2 * dot(matrix[...], matrix[...], ((0,), (0,))))
+        squares[n, :levels, :levels] = high
+        squares[n, :levels, levels:] = low
+        squares[n, levels:, :levels] = high
+
+
+def fill_weights(feat, weights, high_weights, low_weights, windows, rows_lat, rows_lon):
     slots = feat.shape[1]
     cell = feat[0:1].astype(jnp.int32)
     half = iota((rows_lon, slots), 0) >> 1
     odd = (iota((rows_lon, slots), 0) & 1) == 1
-    corner = [jnp.where(odd, feat[3 + 2 * q : 4 + 2 * q], feat[2 + 2 * q : 3 + 2 * q]) for q in range(2)]
+    corner = [
+        jnp.where(odd, feat[3 + 2 * q : 4 + 2 * q], feat[2 + 2 * q : 3 + 2 * q]) for q in range(2)
+    ]
     per_window = rows_lat // 2 * (rows_lon // 2)
     for t in range(windows):
         for a in range(rows_lat):
             first = t * per_window + a // 2 * (rows_lon // 2)
             row = (t * rows_lat + a) * rows_lon
-            weights[row : row + rows_lon] = jnp.where(half == cell - first, corner[a % 2], 0.0)
-
-
-def adjoint_fields(amount, weights, ivert, ens, ens_copies, grad, outs):
+            rows = slice(row, row + rows_lon)
+            value = jnp.where(half == cell - first, corner[a % 2], 0.0)
+            weights[rows] = value
+            high_weights[rows], low_weights[rows] = halves(value)
+
+
+def adjoint_fields(amount, high_weights, low_weights, ivert, ens, ens_copies, grad, outs):
     fields, edge_a, edge_b = outs
-    members, windows, rows_lat, rows_lon, _ = ens.shape
+    members, windows, rows_lat, rows_lon, levels = ens.shape
     block = rows_lat * rows_lon
-    scaled = ivert[...] * amount
+    high, low = halves(ivert[...] * amount)
+    both = jnp.concatenate([high, low], axis=0)
     for t in range(windows):
         rows = slice(t * block, (t + 1) * block)
-        grad[rows] = dot(weights[rows], scaled, ((1,), (1,)))
+        pair = short_dot(high_weights[rows], both, ((1,), (1,)))
+        rest = short_dot(low_weights[rows], high, ((1,), (1,)))
+        grad[rows] = pair[:, :levels] + pair[:, levels:] + rest
     even = lax.rem(lax.axis_index("lon"), 2) == 0
 
     def part(t, a):
@@ -144,7 +167,7 @@
     slots,
     recv, inst_vert_hbm, inst_err_hbm, ens_hbm,
     feat, ivert, fields, edge_a, edge_b,
-    inst_vert, inst_err, ens, weights, grad, sems,
+    inst_vert, inst_err, ens, weights, high_weights, low_weights, grad, sems,
 ):
     members = ens.shape[0]
     copies = fetch(
@@ -166,9 +189,9 @@
     rinv = dot(inverse, onehot)[0:1]
     feat[6:7] = feat[6:7] * rinv
     feat[7:8] = rinv
-    fill_weights(feat, weights, windows, rows_lat, rows_lon)
+    fill_weights(feat, weights, high_weights, low_weights, windows, rows_lat, rows_lon)
     outs = (fields, edge_a, edge_b)
-    adjoint_fields(feat[6:7], weights, ivert, ens, copies[2:], grad, outs)
+    adjoint_fields(feat[6:7], high_weights, low_weights, ivert, ens, copies[2:], grad, outs)
 
 
 def halo_copies(own, lat_a, lat_b, cross, corner_a, corner_b, field, sems):
@@ -262,7 +285,7 @@
             out[k, i] = value[:rows_lon]
         return carry
 
-    lax.fori_loop(0, count, one, 0)
+    lax.fori_loop(0, count, one, 0, unroll=count)
 
 
 def observe(field, powers, smooth, mixed, squares, ivert, weights, ens, ens_copy):
@@ -272,10 +295,14 @@
     shape = (rows_lat, rows_lon, levels)
     for k in range(members + 1):
         square = squares[0] if k < members else squares[1]
-        mixed[k] = dot(smooth[k].reshape(block, levels), square).reshape(shape)
+        pair = jnp.concatenate(halves(smooth[k].reshape(block, levels)), axis=1)
+        product = short_dot(pair, square)
+        mixed[k] = (product[:, :levels] + product[:, levels:]).reshape(shape)
     ens_copy.wait()
     slots = weights.shape[1]
     image = jnp.zeros((8, slots), F32)
+    high, low = halves(ivert[...])
+    rows_of = jnp.concatenate([high, high, low], axis=0)
     for t in range(windows):
         lines = []
         for a in range(rows_lat):
@@ -284,7 +311,9 @@
                 total = total + ens[k, t, a].astype(F32) * mixed[k, a]
             lines.append(total)
         increment = jnp.stack(lines).reshape(block, levels)
-        seen = dot(increment, ivert[...]) * weights[t * block : (t + 1) * block]
+        high, low = halves(increment)
+        seen = short_dot(jnp.concatenate([high, low, high], axis=1), rows_of)
+        seen = seen * weights[t * block : (t + 1) * block]
         image = image + jnp.sum(seen.reshape(block // 8, 8, slots), axis=0)
     return jnp.sum(image, axis=0, keepdims=True)
 
@@ -292,7 +321,7 @@
 def middle_kernel(
     own, lat_a, lat_b, cross, corner_a, corner_b, ens_hbm, feat, ivert, squares,
     image, kept, fields, edge_a, edge_b,
-    ens, field, powers, smooth, mixed, weights, grad, sem, sems,
+    ens, field, powers, smooth, mixed, weights, high_weights, low_weights, grad, sem, sems,
 ):
     copies = halo_copies(own, lat_a, lat_b, cross, corner_a, corner_b, field, sems)
     for copy in copies:
@@ -300,7 +329,7 @@
     ens_copy = pltpu.make_async_copy(ens_hbm, ens, sem)
     ens_copy.start()
     _, windows, rows_lat, rows_lon, _ = ens.shape
-    fill_weights(feat, weights, windows, rows_lat, rows_lon)
+    fill_weights(feat, weights, high_weights, low_weights, windows, rows_lat, rows_lon)
     wait_all(copies)
     unfold_corner(field, rows_lon)
     keep = keep_copy(field, kept, sems)
@@ -311,15 +340,15 @@
     image[0:1] = seen
     image[1:2] = scaled
     outs = (fields, edge_a, edge_b)
-    adjoint_fields(scaled, weights, ivert, ens, (), grad, outs)
+    adjoint_fields(scaled, high_weights, low_weights, ivert, ens, (), grad, outs)
     keep.wait()
 
 
 def last_kernel(
     slots,
-    own, lat_a, lat_b, cross, corner_a, corner_b, ens_hbm, early, feat, ivert, squares, image,
+    own, lat_a, lat_b, cross, corner_a, corner_b, ens_hbm, feat, ivert, squares, image,
     send, kept,
-    ens, field, powers, smooth, mixed, weights, terms, sem, sems,
+    ens, field, powers, smooth, mixed, weights, high_weights, low_weights, terms, sem, sems,
 ):
     copies = halo_copies(own, lat_a, lat_b, cross, corner_a, corner_b, field, sems)
     for copy in copies:
@@ -327,7 +356,7 @@
     ens_copy = pltpu.make_async_copy(ens_hbm, ens, sem)
     ens_copy.start()
     _, windows, rows_lat, rows_lon, _ = ens.shape
-    fill_weights(feat, weights, windows, rows_lat, rows_lon)
+    fill_weights(feat, weights, high_weights, low_weights, windows, rows_lat, rows_lon)
     wait_all(copies)
     unfold_corner(field, rows_lon)
     keep = keep_copy(field, kept, sems)
@@ -381,39 +410,40 @@
 
 
 def control_kernel(
-    kept, vert_hbm, static_hbm,
-    control,
-    field, powers, smooth, result, vert_loc, static_vert, sems, out_sems,
+    kept_early, kept_late, vert_hbm, static_hbm,
+    early, late,
+    fields, powers, smooth, vert_loc, static_vert, sems,
 ):
-    copies = fetch((vert_hbm, static_hbm, kept), (vert_loc, static_vert, field), sems)
-    wait_all(copies)
+    copies = fetch(
+        (vert_hbm, static_hbm, kept_early, kept_late),
+        (vert_loc, static_vert, fields.at[0], fields.at[1]),
+        sems,
+    )
+    wait_all(copies[:2])
     count, rows_lat, rows_lon, levels = smooth.shape
-    smooth_power(field, powers, smooth, 2)
-    stores = []
-    for k in range(count):
-        member = k < count - 1
-        scale, matrix = (BETA_ENSEMBLE, vert_loc) if member else (BETA_STATIC, static_vert)
-        value = dot(smooth[k].reshape(rows_lat * rows_lon, levels), matrix[...], ((1,), (1,)))
-        result[k] = (scale * value).reshape(rows_lat, rows_lon, levels)
-        stores.append(pltpu.make_async_copy(result.at[k], control.at[k], out_sems.at[k]))
-        stores[k].start()
-    wait_all(stores)
+    blocks = []
+    for scale, matrix in ((BETA_ENSEMBLE, vert_loc), (BETA_STATIC, static_vert)):
+        high, low = halves(scale * matrix[...])
+        upper = jnp.concatenate([high, high], axis=1)
+        lower = jnp.concatenate([low, jnp.zeros_like(low)], axis=1)
+        blocks.append(jnp.concatenate([upper, lower], axis=0))
+    for n, control in enumerate((early, late)):
+        copies[2 + n].wait()
+        smooth_power(fields.at[n], powers, smooth, 2)
+        for k in range(count):
+            pair = jnp.concatenate(halves(smooth[k].reshape(rows_lat * rows_lon, levels)), axis=1)
+            product = short_dot(pair, blocks[k // (count - 1)], ((1,), (1,)))
+            product = product[:, :levels] + product[:, levels:]
+            control[k] = product.reshape(rows_lat, rows_lon, levels)
 
 
 def final_kernel(
-    recv, dest_hbm, lane_hbm, early_hbm, late_hbm,
-    static_hbm, member_hbm, equivalent,
-    dest, lane, early, late, result, sems, field_sems,
+    recv, early, late, dest_hbm, lane_hbm,
+    static_hbm, member_hbm, equivalent_hbm,
+    dest, lane, equivalent, result, sems, out_sems,
 ):
     small = fetch((dest_hbm, lane_hbm), (dest, lane), sems)
     count = early.shape[0]
-    large = []
-    for k in range(count):
-        large.append(
-            fetch(
-                (early_hbm.at[k], late_hbm.at[k]), (early.at[k], late.at[k]), field_sems.at[k]
-            )
-        )
     owners = recv.shape[0]
     rows = dest.shape[1]
     blocks = recv[...]
@@ -440,10 +470,9 @@
     far = -step_next * step
     stores = []
     for k in range(count):
-        wait_all(large[k])
         result[k] = near[None] * early[k] + far[None] * late[k]
         target = member_hbm.at[k] if k < count - 1 else static_hbm
-        stores.append(pltpu.make_async_copy(result.at[k], target, field_sems.at[k, 2]))
+        stores.append(pltpu.make_async_copy(result.at[k], target, out_sems.at[k]))
         stores[k].start()
     wait_all(small)
     kind = iota((owners, 8, rows), 1)
@@ -454,6 +483,8 @@
     equivalent[...] = jnp.sum(
         jnp.where(iota((LANES, rows), 0) == lane[...], table, 0.0), axis=0, keepdims=True
     )
+    stores.append(pltpu.make_async_copy(equivalent, equivalent_hbm, out_sems.at[count]))
+    stores[count].start()
     wait_all(stores)
 
 
@@ -537,7 +568,7 @@
     )
     squares = pl.pallas_call(
         prepare_kernel,
-        out_shape=shape(2, levels, levels),
+        out_shape=jax.ShapeDtypeStruct((2, 2 * levels, 2 * levels), BF16),
         compiler_params=PARAMS,
         name="prepare",
     )(vert_loc, static_vert)
@@ -550,6 +581,7 @@
     field_scratch = pltpu.VMEM((count, rows_lat + 2 * HALO, width, levels), F32)
     tile_scratch = pltpu.VMEM(tile.shape, F32)
     weight_scratch = pltpu.VMEM((windows * rows_lat * rows_lon, total), F32)
+    half_scratch = pltpu.VMEM(weight_scratch.shape, BF16)
     grad_scratch = pltpu.VMEM((windows * rows_lat * rows_lon, levels), F32)
 
     def powers(order):
@@ -565,6 +597,8 @@
             pltpu.VMEM((1, inst_err.shape[0]), F32),
             ens_scratch,
             weight_scratch,
+            half_scratch,
+            half_scratch,
             grad_scratch,
             DMA((2 + members,)),
         ],
@@ -595,32 +629,13 @@
         corner_a = lax.ppermute(cross, "lat", lat_inner)
         return (fields, lat_a, lat_b, cross, corner_a, corner_b)
 
-    def control(kept):
-        return pl.pallas_call(
-            control_kernel,
-            out_shape=pltpu.HBM(tile.shape, F32),
-            in_specs=[HBM] * 3,
-            out_specs=HBM,
-            scratch_shapes=[
-                pltpu.VMEM(kept_shape.shape, F32),
-                powers(2),
-                tile_scratch,
-                tile_scratch,
-                matrix_scratch,
-                matrix_scratch,
-                DMA((3,)),
-                DMA((count,)),
-            ],
-            compiler_params=PARAMS,
-            name="control",
-        )(*stay(kept, vert_loc, static_vert))
-
     parts = halo(*outs)
     matrix_scratch = pltpu.VMEM(vert_loc.shape, F32)
     work = [ens_scratch, field_scratch, powers(4), tile_scratch, tile_scratch, weight_scratch]
+    work += [half_scratch] * 2
     sems = [DMA, DMA((8,))]
     kept_shape = pltpu.HBM((count, rows_lat + HALO, width, levels), F32)
-    image, kept, *outs = pl.pallas_call(
+    image, kept_early, *outs = pl.pallas_call(
         middle_kernel,
         out_shape=(shape(8, total), kept_shape, tile, edge, edge),
         in_specs=[ANY] * 6 + [HBM] + [VMEM] * 3,
@@ -629,19 +644,33 @@
         compiler_params=PARAMS,
         name="middle",
     )(*parts, *stay(ensemble), feat, ivert, squares)
-    early = control(kept)
     parts = halo(*outs)
-    send, kept = pl.pallas_call(
+    send, kept_late = pl.pallas_call(
         functools.partial(last_kernel, slots),
         out_shape=(shape(owners, 8, LANES), kept_shape),
-        in_specs=[ANY] * 6 + [HBM] * 2 + [VMEM] * 4,
+        in_specs=[ANY] * 6 + [HBM] + [VMEM] * 4,
         out_specs=(VMEM, HBM),
         scratch_shapes=work + [pltpu.VMEM((16, total), F32)] + sems,
         compiler_params=PARAMS,
         name="last",
-    )(*parts, *stay(ensemble, early), feat, ivert, squares, image)
+    )(*parts, *stay(ensemble), feat, ivert, squares, image)
     recv = exchange(send)
-    late = control(kept)
+    early, late = pl.pallas_call(
+        control_kernel,
+        out_shape=(tile, tile),
+        in_specs=[HBM] * 4,
+        out_specs=(VMEM,) * 2,
+        scratch_shapes=[
+            pltpu.VMEM((2,) + kept_shape.shape, F32),
+            powers(2),
+            tile_scratch,
+            matrix_scratch,
+            matrix_scratch,
+            DMA((4,)),
+        ],
+        compiler_params=PARAMS,
+        name="control",
+    )(*stay(kept_early, kept_late, vert_loc, static_vert))
     static, member, equivalent = pl.pallas_call(
         final_kernel,
         out_shape=(
@@ -649,20 +678,19 @@
             shape(members, rows_lat, rows_lon, levels),
             shape(1, rows),
         ),
-        in_specs=[VMEM] + [HBM] * 4,
-        out_specs=(HBM, HBM, VMEM),
+        in_specs=[VMEM] * 3 + [HBM] * 2,
+        out_specs=(HBM,) * 3,
         scratch_shapes=[
             row_scratch,
             row_scratch,
-            tile_scratch,
-            tile_scratch,
+            pltpu.VMEM((1, rows), F32),
             tile_scratch,
             DMA((2,)),
-            DMA((count, 3)),
+            DMA((count + 1,)),
         ],
         compiler_params=PARAMS,
         name="final",
-    )(recv, *stay(dest, lane, early, late))
+    )(recv, early, late, *stay(dest, lane))
     return static, member, equivalent.reshape(rows)
 
 

time: 81.7 us -> 75.1 us (0.919)
  Pallas kernels: 29 us -> 18.5 us
  starting transfers between devices: 21.5 us -> 24.4 us
  waiting for transfers between devices: 14.1 us -> 15.3 us
    pallas_call x3 -> x2, Pallas kernels: 9.24 us -> 4.07 us  [the longest x1 3.75 us: body(): pl.pallas_call(control_kernel, out_shape=(tile, tile), in_specs=[HBM] * 4...]
    all_to_all x1, starting transfers between devices: 4.84 us -> 7.83 us  [exchange(): lax.all_to_all(blocks, ('lat', 'lon'), split_axis=0, concat_axis=0, tiled...]
    pallas_call x1, Pallas kernels: 6.32 us -> 4.2 us  [body(): pl.pallas_call(middle_kernel, out_shape=(shape(8, total), kept_shape, til...]
    pallas_call x1, Pallas kernels: 5.49 us -> 3.94 us  [body(): pl.pallas_call(functools.partial(last_kernel, slots), out_shape=(shape(ow...]
    pallas_call x1, Pallas kernels: 3.3 us -> 2.27 us  [body(): pl.pallas_call(final_kernel, out_shape=(shape(rows_lat, rows_lon, levels)...]
  transfers between devices with their start and end apart: 13 -> 13, of which waited for: 6 -> 7; matrix products, arithmetic and copies ran while one was open for 0% -> 0% of each run, Pallas kernels for 11% -> 6%
where the time goes in v2:
time: 75.1 us; the launch traced here: 74.7 us
  starting transfers between devices  24.4 us (32%)
  Pallas kernels  18.5 us (25%)
  waiting for transfers between devices  15.3 us (20%)
  blocking collectives  14.9 us (20%)
  between operations  1.64 us (2%)
    all_to_all x1, blocking collectives, exchange(): lax.all_to_all(blocks, ('lat', 'lon'), split_axis=0, concat_axis=0, tiled...  14.9 us
    ppermute x2, starting transfers between devices, halo(): lat_a = lax.ppermute(fields, 'lat', lat_inner)  9.02 us
    all_to_all x1, starting transfers between devices, exchange(): lax.all_to_all(blocks, ('lat', 'lon'), split_axis=0, concat_axis=0, tiled...  7.83 us
    ppermute x2, waiting for transfers between devices, halo(): side_b = lax.ppermute(edge_b, 'lon', lon_outer)  6.31 us
    pallas_call x1, Pallas kernels, body(): pl.pallas_call(middle_kernel, out_shape=(shape(8, total), kept_shape, til...  4.2 us
    ppermute x2, waiting for transfers between devices, halo(): side_a = lax.ppermute(edge_a, 'lon', lon_inner)  4.09 us
    pallas_call x1, Pallas kernels, body(): pl.pallas_call(functools.partial(last_kernel, slots), out_shape=(shape(ow...  3.94 us
    all_to_all x1, waiting for transfers between devices, exchange(): lax.all_to_all(blocks, ('lat', 'lon'), split_axis=0, concat_axis=0, tiled...  3.87 us
  transfers between devices with their start and end apart: 13, of which 7 were waited for; matrix products, arithmetic and copies ran while one was open for 0% of the time, Pallas kernels for 6%

profile of v2, /device:TPU:0, one launch (start us, length us, event | category | flops | bytes accessed | tf_op | source)
XLA Modules:
  0.0 74.7 jit_solution(11089713546436977615)
XLA Ops:
  0.6 0.0 copy-start.1
  0.6 0.0 copy-start
  1.3 1.6 %pack.1 = (f32[32,8,128]{2,1,0:T(8,128)S(1)}, s32[1,256]{1,0:T(1,128)}) custom-call(s32[1,256]{1,0:T(1,128)} %bitcast.7, s32[1,256]{1,0:T(1,128)} %bitcast.9, s32[1,256]{1,0:T(1,128)} %bitcast.10, s32[1,256]{1,0:T(1,128)} %bitcast.11, f32[4,256]{1,0:T(4,128)} %hweight_hbm.1, f32[1,256]{1,0:T(1,128)} %bitcast.12, s32[1]{0:T(128)S(6)} %copy.15.count), custom_call_target="tpu_custom_call" | custom-call | tf_op jit(solution)/shard_map/pack/pallas_call | solution.py:543
  3.0 14.9 %all_to_all.10.recv = f32[32,8,128]{2,1,0:T(8,128)S(1)} all-to-all(f32[32,8,128]{2,1,0:T(8,128)S(1)} %get-tuple-element.26), channel_id=1, replica_groups=mesh['lat'=4,'lon'=8] {'lat','lon'}, dimensions={0} | all-to-all | bytes 262144 | tf_op jit(solution)/shard_map/all_to_all | solution.py:577
  17.9 2.3 %first.1 = (f32[8,512]{1,0:T(8,128)S(1)}, f32[128,512]{1,0:T(8,128)S(1)}, f32[9,4,48,128]{3,2,1,0:T(8,128)S(1)}, f32[9,4,4,128]{3,2,1,0:T(4,128)S(1)}, f32[9,4,4,128]{3,2,1,0:T(4,128)S(1)}) custom-call(f32[32,8,128]{2,1,0:T(8,128)S(1)} %all_to_all.10.recv, f32[16,128]{1,0:T(8,128)} %inst_vert_hbm.1, f32[1,16]{1,0:T(1,128)} %bitcast.13, ...), custom_call_target="tpu_custom_call" | custom-call | tf_op jit(solution)/shard_map/first/pallas_call | solution.py:590
  20.2 0.7 collective-permute-start.1
  20.9 2.3 %collective-permute-start = (f32[9,4,48,128]{3,2,1,0:T(8,128)S(1)}, f32[9,4,48,128]{3,2,1,0:T(8,128)S(1)}, u32[]{:S(2)}, u32[]{:S(2)}) collective-permute-start(f32[9,4,48,128]{3,2,1,0:T(8,128)S(1)} %get-tuple-element.27.own), channel_id=1, source_target_pairs={{0,8},{8,0},{16,24},{24,16},{1,9},{9,1},{17,25},{25,17},{2,10},{10... | collective-permute-start | bytes 2654216 | tf_op jit(solution)/shard_map/ppermute | solution.py:626
  23.3 0.9 %collective-permute-start.2 = (f32[9,4,4,128]{3,2,1,0:T(4,128)S(1)}, f32[9,4,4,128]{3,2,1,0:T(4,128)S(1)}, u32[]{:S(2)}, u32[]{:S(2)}) collective-permute-start(f32[9,4,4,128]{3,2,1,0:T(4,128)S(1)} %get-tuple-element.28), channel_id=1, source_target_pairs={{0,1},{1,0},{2,3},{3,2},{4,5},{5,4},{6,7},{7,6},{8,9},{9,8},{10,11... | collective-permute-start | bytes 221192 | tf_op jit(solution)/shard_map/ppermute | solution.py:624
  24.2 2.1 %collective-permute-start.3 = (f32[9,4,4,128]{3,2,1,0:T(4,128)S(1)}, f32[9,4,4,128]{3,2,1,0:T(4,128)S(1)}, u32[]{:S(2)}, u32[]{:S(2)}) collective-permute-start(f32[9,4,4,128]{3,2,1,0:T(4,128)S(1)} %get-tuple-element.29), channel_id=1, source_target_pairs={{1,2},{2,1},{3,4},{4,3},{5,6},{6,5},{7,0},{0,7},{9,10},{10,9},{11,... | collective-permute-start | bytes 221192 | tf_op jit(solution)/shard_map/ppermute | solution.py:625
  26.3 1.3 %collective-permute-done.2.part_a = f32[9,4,4,128]{3,2,1,0:T(4,128)S(1)} collective-permute-done((f32[9,4,4,128]{3,2,1,0:T(4,128)S(1)}, f32[9,4,4,128]{3,2,1,0:T(4,128)S(1)}, u32[]{:S(2)}, u32[]{:S(2)}) %collective-permute-start.2) | collective-permute-done | bytes 73760 | tf_op jit(solution)/shard_map/ppermute | solution.py:624
  27.6 3.6 %collective-permute-done.3.part_b = f32[9,4,4,128]{3,2,1,0:T(4,128)S(1)} collective-permute-done((f32[9,4,4,128]{3,2,1,0:T(4,128)S(1)}, f32[9,4,4,128]{3,2,1,0:T(4,128)S(1)}, u32[]{:S(2)}, u32[]{:S(2)}) %collective-permute-start.3) | collective-permute-done | bytes 73760 | tf_op jit(solution)/shard_map/ppermute | solution.py:625
  31.3 0.1 collective-permute-start.4
  31.4 0.7 collective-permute-start.5
  32.0 0.0 copy-done.1
  32.0 0.0 copy-done
  32.0 0.3 prepare.1.squares
  32.4 0.0 collective-permute-done.5.corner_b
  32.4 0.3 collective-permute-done.4.corner_a
  32.7 0.0 collective-permute-done.1.lat_b
  32.7 0.0 collective-permute-done.lat_a
  32.7 4.2 %middle.1 = (f32[8,512]{1,0:T(8,128)S(1)}, f32[9,8,56,128]{3,2,1,0:T(8,128)}, f32[9,4,48,128]{3,2,1,0:T(8,128)S(1)}, f32[9,4,4,128]{3,2,1,0:T(4,128)S(1)}, f32[9,4,4,128]{3,2,1,0:T(4,128)S(1)}) custom-call(f32[9,4,48,128]{3,2,1,0:T(8,128)S(1)} %get-tuple-element.27.own, f32[9,4,48,128]{3,2,1,0:T(8,128)S(1)} %collective-permute-done.lat_a, ...), custom_call_target="tpu_custom_call" | custom-call | tf_op jit(solution)/shard_map/middle/pallas_call | solution.py:638
  36.9 0.7 collective-permute-start.7
  37.6 6.7 %collective-permute-start.6 = (f32[9,4,48,128]{3,2,1,0:T(8,128)S(1)}, f32[9,4,48,128]{3,2,1,0:T(8,128)S(1)}, u32[]{:S(2)}, u32[]{:S(2)}) collective-permute-start(f32[9,4,48,128]{3,2,1,0:T(8,128)S(1)} %get-tuple-element.34.own), channel_id=1, source_target_pairs={{0,8},{8,0},{16,24},{24,16},{1,9},{9,1},{17,25},{25,17},{2,10},{10... | collective-permute-start | bytes 2654216 | tf_op jit(solution)/shard_map/ppermute | solution.py:626
  44.3 0.0 collective-permute-start.8
  44.3 1.6 %collective-permute-start.9 = (f32[9,4,4,128]{3,2,1,0:T(4,128)S(1)}, f32[9,4,4,128]{3,2,1,0:T(4,128)S(1)}, u32[]{:S(2)}, u32[]{:S(2)}) collective-permute-start(f32[9,4,4,128]{3,2,1,0:T(4,128)S(1)} %get-tuple-element.36), channel_id=1, source_target_pairs={{1,2},{2,1},{3,4},{4,3},{5,6},{6,5},{7,0},{0,7},{9,10},{10,9},{11,... | collective-permute-start | bytes 221192 | tf_op jit(solution)/shard_map/ppermute | solution.py:625
  45.9 2.8 %collective-permute-done.8.part_a = f32[9,4,4,128]{3,2,1,0:T(4,128)S(1)} collective-permute-done((f32[9,4,4,128]{3,2,1,0:T(4,128)S(1)}, f32[9,4,4,128]{3,2,1,0:T(4,128)S(1)}, u32[]{:S(2)}, u32[]{:S(2)}) %collective-permute-start.8) | collective-permute-done | bytes 73760 | tf_op jit(solution)/shard_map/ppermute | solution.py:624
  48.7 2.7 %collective-permute-done.9.part_b = f32[9,4,4,128]{3,2,1,0:T(4,128)S(1)} collective-permute-done((f32[9,4,4,128]{3,2,1,0:T(4,128)S(1)}, f32[9,4,4,128]{3,2,1,0:T(4,128)S(1)}, u32[]{:S(2)}, u32[]{:S(2)}) %collective-permute-start.9) | collective-permute-done | bytes 73760 | tf_op jit(solution)/shard_map/ppermute | solution.py:625
  51.4 0.1 collective-permute-start.10
  51.5 0.7 collective-permute-start.11
  52.2 0.0 collective-permute-done.11.corner_b
  52.2 0.7 collective-permute-done.10.corner_a
  52.9 0.0 collective-permute-done.7.lat_b
  52.9 0.0 collective-permute-done.6.lat_a
  52.9 3.9 %last.1 = (f32[32,8,128]{2,1,0:T(8,128)}, f32[9,8,56,128]{3,2,1,0:T(8,128)}) custom-call(f32[9,4,48,128]{3,2,1,0:T(8,128)S(1)} %get-tuple-element.34.own, f32[9,4,48,128]{3,2,1,0:T(8,128)S(1)} %collective-permute-done.6.lat_a, f32[9,4,48,128]{3,2,1,0:T(8,128)S(1)} %collective-permute-done.7.lat_b, f32[9,4,8,128]{3,2,1,0:T(8,128)S(1)} %get-tuple-element.37.cross, ...), custom_call_target="tpu_custom_call" | custom-call | tf_op jit(solution)/shard_map/last/pallas_call | solution.py:648
  56.8 7.8 %all-to-all-start.1 = ((f32[32,8,128]{2,1,0:T(8,128)}), f32[32,8,128]{2,1,0:T(8,128)S(1)}, u32[]{:S(2)}, u32[]{:S(2)}) async-start(f32[32,8,128]{2,1,0:T(8,128)} %get-tuple-element.40), calls=%async_computation.1 | async-start | bytes 262144 | tf_op jit(solution)/shard_map/all_to_all | solution.py:577
  64.7 3.7 %control.1 = (f32[9,4,48,128]{3,2,1,0:T(8,128)S(1)}, f32[9,4,48,128]{3,2,1,0:T(8,128)S(1)}) custom-call(f32[9,8,56,128]{3,2,1,0:T(8,128)} %get-tuple-element.41.kept_early, f32[9,8,56,128]{3,2,1,0:T(8,128)} %get-tuple-element.42.kept_late, f32[128,128]{1,0:T(8,128)} %vert_hbm.1, f32[128,128]{1,0:T(8,128)} %static_hbm.1), custom_call_target="tpu_custom_call" | custom-call | tf_op jit(solution)/shard_map/control/pallas_call | solution.py:658
  68.4 3.9 %all-to-all-done.1.recv = f32[32,8,128]{2,1,0:T(8,128)S(1)} async-done(((f32[32,8,128]{2,1,0:T(8,128)}), f32[32,8,128]{2,1,0:T(8,128)S(1)}, u32[]{:S(2)}, u32[]{:S(2)}) %all-to-all-start.1) | async-done | bytes 131104 | tf_op jit(solution)/shard_map/all_to_all | solution.py:577
  72.3 2.3 %final.1 = (f32[4,48,128]{2,1,0:T(8,128)}, f32[8,4,48,128]{3,2,1,0:T(8,128)}, f32[1,256]{1,0:T(1,128)}) custom-call(f32[32,8,128]{2,1,0:T(8,128)S(1)} %all-to-all-done.1.recv, f32[9,4,48,128]{3,2,1,0:T(8,128)S(1)} %get-tuple-element.43.early, f32[9,4,48,128]{3,2,1,0:T(8,128)S(1)} %get-tuple-element.44.late, s32[1,256]{1,0:T(1,128)} %bitcast.8, ...), custom_call_target="tpu_custom_call" | custom-call | tf_op jit(solution)/shard_map/final/pallas_call | solution.py:674
  (2 shorter events, 0.1 us)
Async XLA Ops:
  0.6 31.4 %copy-start.1 = (f32[128,128]{1,0:T(8,128)S(1)}, f32[128,128]{1,0:T(8,128)}, u32[]{:S(2)}) copy-start(f32[128,128]{1,0:T(8,128)} %static_hbm.1) | copy-start | bytes 196612
  0.6 31.4 %copy-start = (f32[128,128]{1,0:T(8,128)S(1)}, f32[128,128]{1,0:T(8,128)}, u32[]{:S(2)}) copy-start(f32[128,128]{1,0:T(8,128)} %vert_hbm.1) | copy-start | bytes 196612
  20.2 12.5 %collective-permute-start.1 = (f32[9,4,48,128]{3,2,1,0:T(8,128)S(1)}, f32[9,4,48,128]{3,2,1,0:T(8,128)S(1)}, u32[]{:S(2)}, u32[]{:S(2)}) collective-permute-start(f32[9,4,48,128]{3,2,1,0:T(8,128)S(1)} %get-tuple-element.27.own), channel_id=1, source_target_pairs={{8,16},{16,8},{9,17},{17,9},{10,18},{18,10},{11,19},{19,11},{12,20... | collective-permute-start | bytes 2654216 | tf_op jit(solution)/shard_map/ppermute | solution.py:623
  20.9 11.8 %collective-permute-start = (f32[9,4,48,128]{3,2,1,0:T(8,128)S(1)}, f32[9,4,48,128]{3,2,1,0:T(8,128)S(1)}, u32[]{:S(2)}, u32[]{:S(2)}) collective-permute-start(f32[9,4,48,128]{3,2,1,0:T(8,128)S(1)} %get-tuple-element.27.own), channel_id=1, source_target_pairs={{0,8},{8,0},{16,24},{24,16},{1,9},{9,1},{17,25},{25,17},{2,10},{10... | collective-permute-start | bytes 2654216 | tf_op jit(solution)/shard_map/ppermute | solution.py:626
  23.3 4.4 %collective-permute-start.2 = (f32[9,4,4,128]{3,2,1,0:T(4,128)S(1)}, f32[9,4,4,128]{3,2,1,0:T(4,128)S(1)}, u32[]{:S(2)}, u32[]{:S(2)}) collective-permute-start(f32[9,4,4,128]{3,2,1,0:T(4,128)S(1)} %get-tuple-element.28), channel_id=1, source_target_pairs={{0,1},{1,0},{2,3},{3,2},{4,5},{5,4},{6,7},{7,6},{8,9},{9,8},{10,11... | collective-permute-start | bytes 221192 | tf_op jit(solution)/shard_map/ppermute | solution.py:624
  24.2 7.0 %collective-permute-start.3 = (f32[9,4,4,128]{3,2,1,0:T(4,128)S(1)}, f32[9,4,4,128]{3,2,1,0:T(4,128)S(1)}, u32[]{:S(2)}, u32[]{:S(2)}) collective-permute-start(f32[9,4,4,128]{3,2,1,0:T(4,128)S(1)} %get-tuple-element.29), channel_id=1, source_target_pairs={{1,2},{2,1},{3,4},{4,3},{5,6},{6,5},{7,0},{0,7},{9,10},{10,9},{11,... | collective-permute-start | bytes 221192 | tf_op jit(solution)/shard_map/ppermute | solution.py:625
  31.3 1.4 %collective-permute-start.4 = (f32[9,4,8,128]{3,2,1,0:T(8,128)S(1)}, f32[9,4,8,128]{3,2,1,0:T(8,128)S(1)}, u32[]{:S(2)}, u32[]{:S(2)}) collective-permute-start(f32[9,4,8,128]{3,2,1,0:T(8,128)S(1)} %get-tuple-element.30.cross), channel_id=1, source_target_pairs={{0,8},{8,0},{16,24},{24,16},{1,9},{9,1},{17,25},{25,17},{2,10},{10... | collective-permute-start | bytes 442376 | tf_op jit(solution)/shard_map/ppermute | solution.py:629
  31.4 1.0 %collective-permute-start.5 = (f32[9,2,8,128]{3,2,1,0:T(8,128)S(1)}, f32[9,2,8,128]{3,2,1,0:T(8,128)S(1)}, u32[]{:S(2)}, u32[]{:S(2)}) collective-permute-start(f32[9,2,8,128]{3,2,1,0:T(8,128)S(1)} %get-tuple-element.31), channel_id=1, source_target_pairs={{8,16},{16,8},{9,17},{17,9},{10,18},{18,10},{11,19},{19,11},{12,20... | collective-permute-start | bytes 221192 | tf_op jit(solution)/shard_map/ppermute | solution.py:628
  36.9 15.9 %collective-permute-start.7 = (f32[9,4,48,128]{3,2,1,0:T(8,128)S(1)}, f32[9,4,48,128]{3,2,1,0:T(8,128)S(1)}, u32[]{:S(2)}, u32[]{:S(2)}) collective-permute-start(f32[9,4,48,128]{3,2,1,0:T(8,128)S(1)} %get-tuple-element.34.own), channel_id=1, source_target_pairs={{8,16},{16,8},{9,17},{17,9},{10,18},{18,10},{11,19},{19,11},{12,20... | collective-permute-start | bytes 2654216 | tf_op jit(solution)/shard_map/ppermute | solution.py:623
  37.6 15.2 %collective-permute-start.6 = (f32[9,4,48,128]{3,2,1,0:T(8,128)S(1)}, f32[9,4,48,128]{3,2,1,0:T(8,128)S(1)}, u32[]{:S(2)}, u32[]{:S(2)}) collective-permute-start(f32[9,4,48,128]{3,2,1,0:T(8,128)S(1)} %get-tuple-element.34.own), channel_id=1, source_target_pairs={{0,8},{8,0},{16,24},{24,16},{1,9},{9,1},{17,25},{25,17},{2,10},{10... | collective-permute-start | bytes 2654216 | tf_op jit(solution)/shard_map/ppermute | solution.py:626
  44.3 4.4 %collective-permute-start.8 = (f32[9,4,4,128]{3,2,1,0:T(4,128)S(1)}, f32[9,4,4,128]{3,2,1,0:T(4,128)S(1)}, u32[]{:S(2)}, u32[]{:S(2)}) collective-permute-start(f32[9,4,4,128]{3,2,1,0:T(4,128)S(1)} %get-tuple-element.35), channel_id=1, source_target_pairs={{0,1},{1,0},{2,3},{3,2},{4,5},{5,4},{6,7},{7,6},{8,9},{9,8},{10,11... | collective-permute-start | bytes 221192 | tf_op jit(solution)/shard_map/ppermute | solution.py:624
  44.3 7.0 %collective-permute-start.9 = (f32[9,4,4,128]{3,2,1,0:T(4,128)S(1)}, f32[9,4,4,128]{3,2,1,0:T(4,128)S(1)}, u32[]{:S(2)}, u32[]{:S(2)}) collective-permute-start(f32[9,4,4,128]{3,2,1,0:T(4,128)S(1)} %get-tuple-element.36), channel_id=1, source_target_pairs={{1,2},{2,1},{3,4},{4,3},{5,6},{6,5},{7,0},{0,7},{9,10},{10,9},{11,... | collective-permute-start | bytes 221192 | tf_op jit(solution)/shard_map/ppermute | solution.py:625
  51.4 1.4 %collective-permute-start.10 = (f32[9,4,8,128]{3,2,1,0:T(8,128)S(1)}, f32[9,4,8,128]{3,2,1,0:T(8,128)S(1)}, u32[]{:S(2)}, u32[]{:S(2)}) collective-permute-start(f32[9,4,8,128]{3,2,1,0:T(8,128)S(1)} %get-tuple-element.37.cross), channel_id=1, source_target_pairs={{0,8},{8,0},{16,24},{24,16},{1,9},{9,1},{17,25},{25,17},{2,10},{10... | collective-permute-start | bytes 442376 | tf_op jit(solution)/shard_map/ppermute | solution.py:629
  51.5 0.7 collective-permute-start.11
  56.8 15.5 %all-to-all-start.1 = ((f32[32,8,128]{2,1,0:T(8,128)}), f32[32,8,128]{2,1,0:T(8,128)S(1)}, u32[]{:S(2)}, u32[]{:S(2)}) async-start(f32[32,8,128]{2,1,0:T(8,128)} %get-tuple-element.40), calls=%async_computation.1 | async-start | bytes 262144 | tf_op jit(solution)/shard_map/all_to_all | solution.py:577

commit v3 on v2

--- a/solution.py
+++ b/solution.py
@@ -14,6 +14,7 @@
 BETA_ENSEMBLE = 0.85
 HALO = 4
 FOLD = 3
+GUESS = 12
 LANES = 128
 HIGHEST = lax.Precision.HIGHEST
 F32 = jnp.float32
@@ -40,6 +41,17 @@
 def halves(value):
     high = value.astype(BF16)
     return high, (value - high.astype(F32)).astype(BF16)
+
+
+def thirds(value):
+    high = value.astype(BF16)
+    rest = value - high.astype(F32)
+    middle = rest.astype(BF16)
+    return high, middle, (rest - middle.astype(F32)).astype(BF16)
+
+
+def within(value, length):
+    return (value >= 0) & (value < length)
 
 
 def fetch(sources, targets, sems):
@@ -65,7 +77,7 @@
     slots, patches,
     dest_hbm, patch_hbm, window_hbm, inst_hbm, hweight_hbm, innov_hbm, count,
     send, lane_hbm,
-    dest, patch, window, inst, hweight, innov, feat, lane, sems,
+    dest, patch, window, inst, hweight, innov, feat, lane, table, sems,
 ):
     wait_all(
         fetch(
@@ -76,8 +88,6 @@
     )
     owners = send.shape[0]
     rows = dest.shape[1]
-    me = lax.axis_index("lat") * lax.axis_size("lon") + lax.axis_index("lon")
-    base = lax.rem(me, LANES // slots) * slots
     destination = dest[...]
     row, col = iota((rows, rows), 0), iota((rows, rows), 1)
     upright = jnp.sum(
@@ -85,20 +95,24 @@
     ).astype(jnp.int32)
     earlier = (upright == destination) & (row < col)
     ranking = jnp.sum(jnp.where(earlier, 1.0, 0.0), axis=0, keepdims=True).astype(jnp.int32)
-    position = ranking + base
-    lane[...] = position
+    lane[...] = ranking
     lane_copy = pltpu.make_async_copy(lane, lane_hbm, sems.at[6])
     lane_copy.start()
     active = (iota((1, rows), 1) < count[0]).astype(F32)
-    feat[...] = jnp.zeros_like(feat)
     feat[0:1] = (window[...] * patches + patch[...]).astype(F32)
     feat[1:2] = inst[...].astype(F32)
     feat[2:6] = hweight[...] * active
     feat[6:7] = innov[...]
-    chosen = iota((owners, 8, rows), 0) == destination.reshape(1, 1, rows)
-    spread_out = jnp.where(chosen, feat[...][None], 0.0).reshape(owners * 8, rows)
-    at_lane = (iota((LANES, rows), 0) == position).astype(F32)
-    send[...] = dot(spread_out, at_lane, ((1,), (1,))).reshape(owners, 8, LANES)
+    table[...] = jnp.zeros_like(table)
+    here = iota((slots, rows), 0) == ranking
+    for f in range(7):
+        table[f * slots : (f + 1) * slots] = jnp.where(here, feat[f : f + 1], 0.0)
+    chosen = (iota((owners, rows), 0) == destination).astype(F32).astype(BF16)
+    send[...] = short_dot(
+        jnp.concatenate([chosen] * 3, axis=1),
+        jnp.concatenate(thirds(table[...]), axis=1),
+        ((1,), (1,)),
+    )
     lane_copy.wait()
 
 
@@ -177,12 +191,20 @@
     )
     members, windows, rows_lat, rows_lon, _ = ens.shape
     owners = recv.shape[0]
-    per = LANES // slots
-    for g in range(owners // per):
-        feat[:, g * LANES : (g + 1) * LANES] = jnp.sum(recv[g * per : (g + 1) * per], axis=0)
+    total = feat.shape[1]
+    source = iota((owners, total), 1) - iota((owners, total), 0) * slots
+    mine = within(source, slots).astype(F32).astype(BF16)
+    lines = short_dot(
+        jnp.concatenate(thirds(recv[...]), axis=0),
+        jnp.concatenate([mine] * 3, axis=0),
+        ((0,), (0,)),
+    )
+    same = (iota((LANES, total), 0) & (slots - 1)) == (iota((LANES, total), 1) & (slots - 1))
+    lines = jnp.where(same, lines, 0.0)
+    for f in range(8):
+        feat[f : f + 1] = jnp.sum(lines[f * slots : (f + 1) * slots], axis=0, keepdims=True)
     wait_all(copies[:2])
     instruments = inst_vert.shape[0]
-    total = feat.shape[1]
     onehot = (iota((instruments, total), 0) == feat[1:2].astype(jnp.int32)).astype(F32)
     ivert[...] = dot(inst_vert[...].T, onehot)
     inverse = jnp.broadcast_to(1.0 / (inst_err[...] * inst_err[...]), (8, instruments))
@@ -251,7 +273,7 @@
     return pltpu.make_async_copy(field.at[:, inner], kept, sems.at[7])
 
 
-def smooth_power(field, powers, out, order):
+def smooth_power(field, powers, out, order, twice=None):
     count, rows, width, _ = field.shape
     rows_lat = rows - 2 * order
     rows_lon = width - 8
@@ -276,11 +298,19 @@
                 line = fresh
                 for i in range(rows_lat):
                     powers[m - 1, i, cols] = line[order + i]
+
+        def step(value):
+            ring = pltpu.roll(value, 1, 0) + pltpu.roll(value, width - 1, 0)
+            return CENTER * value + SMOOTH * ring
+
         for i in range(rows_lat):
             value = field[k, order + i]
             for m in range(1, order + 1):
-                ring = pltpu.roll(value, 1, 0) + pltpu.roll(value, width - 1, 0)
-                value = CENTER * value + SMOOTH * ring
+                value = step(value)
+                if m == 1 and twice is not None:
+                    other = step(value + (2.0 * SMOOTH) * powers[0, i])
+                    other = other + SMOOTH**2 * powers[1, i]
+                    twice[k, i] = other[:rows_lon]
                 value = value + (factor[m - 1] * SMOOTH**m) * powers[m - 1, i]
             out[k, i] = value[:rows_lon]
         return carry
@@ -288,10 +318,10 @@
     lax.fori_loop(0, count, one, 0, unroll=count)
 
 
-def observe(field, powers, smooth, mixed, squares, ivert, weights, ens, ens_copy):
+def observe(field, powers, smooth, mixed, squares, ivert, weights, ens, ens_copy, twice=None):
     members, windows, rows_lat, rows_lon, levels = ens.shape
     block = rows_lat * rows_lon
-    smooth_power(field, powers, smooth, 4)
+    smooth_power(field, powers, smooth, 4, twice)
     shape = (rows_lat, rows_lon, levels)
     for k in range(members + 1):
         square = squares[0] if k < members else squares[1]
@@ -346,9 +376,11 @@
 
 def last_kernel(
     slots,
-    own, lat_a, lat_b, cross, corner_a, corner_b, ens_hbm, feat, ivert, squares, image,
-    send, kept,
-    ens, field, powers, smooth, mixed, weights, high_weights, low_weights, terms, sem, sems,
+    own, lat_a, lat_b, cross, corner_a, corner_b, ens_hbm, vert_hbm, static_hbm,
+    feat, ivert, squares, image,
+    send, late,
+    ens, field, powers, smooth, mixed, weights, high_weights, low_weights, terms, twice,
+    vert_loc, static_vert, sem, sems,
 ):
     copies = halo_copies(own, lat_a, lat_b, cross, corner_a, corner_b, field, sems)
     for copy in copies:
@@ -357,11 +389,12 @@
     ens_copy.start()
     _, windows, rows_lat, rows_lon, _ = ens.shape
     fill_weights(feat, weights, high_weights, low_weights, windows, rows_lat, rows_lon)
+    matrices = fetch((vert_hbm, static_hbm), (vert_loc, static_vert), sems.at[pl.ds(8, 2)])
     wait_all(copies)
     unfold_corner(field, rows_lon)
-    keep = keep_copy(field, kept, sems)
-    keep.start()
-    second = observe(field, powers, smooth, mixed, squares, ivert, weights, ens, ens_copy)
+    second = observe(field, powers, smooth, mixed, squares, ivert, weights, ens, ens_copy, twice)
+    wait_all(matrices)
+    to_control(twice, vert_loc, static_vert, late)
     start = feat[6:7]
     rinv = feat[7:8]
     first = image[0:1]
@@ -392,34 +425,34 @@
     for n, value in enumerate(products):
         terms[n : n + 1] = value
     sums = jnp.sum(terms[...], axis=1, keepdims=True)
-    square = (16, LANES)
-    line = jnp.sum(
-        jnp.where(iota(square, 0) == iota(square, 1), sums, 0.0), axis=0, keepdims=True
-    )
     owners = send.shape[0]
     per = LANES // slots
-    row = iota((8, LANES), 0)
-    for g in range(owners // per):
-        lanes = slice(g * LANES, (g + 1) * LANES)
-        block = jnp.where(row == 0, first[:, lanes], 0.0)
-        block = jnp.where(row == 1, second[:, lanes], block)
-        block = jnp.where(row == 2, line, block)
-        block = jnp.where(row == 3, guess, block)
-        send[g * per : (g + 1) * per] = jnp.broadcast_to(block[None], (per, 8, LANES))
-    keep.wait()
-
-
-def control_kernel(
-    kept_early, kept_late, vert_hbm, static_hbm,
-    early, late,
-    fields, powers, smooth, vert_loc, static_vert, sems,
-):
-    copies = fetch(
-        (vert_hbm, static_hbm, kept_early, kept_late),
-        (vert_loc, static_vert, fields.at[0], fields.at[1]),
-        sems,
-    )
-    wait_all(copies[:2])
+    below, across = iota((16, LANES), 0), iota((16, LANES), 1)
+    line = jnp.sum(
+        jnp.where(across == below + 2 * slots, sums, 0.0), axis=0, keepdims=True
+    )
+    spot = iota((owners, LANES), 1)
+    source = spot - (iota((owners, LANES), 0) & (per - 1)) * slots
+    mine = within(source, slots)
+    parts = []
+    targets = []
+    target = iota((LANES, LANES), 0)
+    slot = iota((LANES, LANES), 1) & (slots - 1)
+    for n, value in enumerate((first, second)):
+        groups = [
+            jnp.broadcast_to(value[:, g * LANES : (g + 1) * LANES], (per, LANES))
+            for g in range(owners // per)
+        ]
+        parts += halves(jnp.where(mine, jnp.concatenate(groups, axis=0), 0.0))
+        targets += [(target == slot + n * slots).astype(F32).astype(BF16)] * 2
+    moved = short_dot(
+        jnp.concatenate(parts, axis=1), jnp.concatenate(targets, axis=1), ((1,), (1,))
+    )
+    tail = jnp.where(spot == 2 * slots + GUESS, guess, line)
+    send[...] = jnp.where(spot < 2 * slots, moved, tail)
+
+
+def to_control(smooth, vert_loc, static_vert, control):
     count, rows_lat, rows_lon, levels = smooth.shape
     blocks = []
     for scale, matrix in ((BETA_ENSEMBLE, vert_loc), (BETA_STATIC, static_vert)):
@@ -427,14 +460,21 @@
         upper = jnp.concatenate([high, high], axis=1)
         lower = jnp.concatenate([low, jnp.zeros_like(low)], axis=1)
         blocks.append(jnp.concatenate([upper, lower], axis=0))
-    for n, control in enumerate((early, late)):
-        copies[2 + n].wait()
-        smooth_power(fields.at[n], powers, smooth, 2)
-        for k in range(count):
-            pair = jnp.concatenate(halves(smooth[k].reshape(rows_lat * rows_lon, levels)), axis=1)
-            product = short_dot(pair, blocks[k // (count - 1)], ((1,), (1,)))
-            product = product[:, :levels] + product[:, levels:]
-            control[k] = product.reshape(rows_lat, rows_lon, levels)
+    for k in range(count):
+        pair = jnp.concatenate(halves(smooth[k].reshape(rows_lat * rows_lon, levels)), axis=1)
+        product = short_dot(pair, blocks[k // (count - 1)], ((1,), (1,)))
+        product = product[:, :levels] + product[:, levels:]
+        control[k] = product.reshape(rows_lat, rows_lon, levels)
+
+
+def control_kernel(
+    kept, vert_hbm, static_hbm,
+    control,
+    field, powers, smooth, vert_loc, static_vert, sems,
+):
+    wait_all(fetch((vert_hbm, static_hbm, kept), (vert_loc, static_vert, field), sems))
+    smooth_power(field, powers, smooth, 2)
+    to_control(smooth, vert_loc, static_vert, control)
 
 
 def final_kernel(
@@ -446,18 +486,18 @@
     count = early.shape[0]
     owners = recv.shape[0]
     rows = dest.shape[1]
+    slots = 2 * rows // owners
     blocks = recv[...]
-    line = blocks[:, 2:3]
-    sums = jnp.sum(line, axis=0)
+    sums = jnp.sum(blocks, axis=0, keepdims=True)
 
     def pick(values, n):
-        return values[:, n : n + 1]
+        return values[:, 2 * slots + n : 2 * slots + n + 1]
 
     norm = pick(sums, 0)
     step = norm / (norm + pick(sums, 1))
-    off = blocks[:, 3:4] - step[None]
-    linear = jnp.sum(off * line, axis=0)
-    square = jnp.sum(off * off * line, axis=0)
+    off = pick(blocks, GUESS) - step
+    linear = jnp.sum(off * blocks, axis=0, keepdims=True)
+    square = jnp.sum(off * off * blocks, axis=0, keepdims=True)
     norm_next = jnp.maximum(pick(sums, 2) + pick(linear, 3) + pick(square, 4), 0.0)
     beta = norm_next / norm
     bend = pick(sums, 5) + pick(linear, 6) + pick(square, 7)
@@ -475,14 +515,16 @@
         stores.append(pltpu.make_async_copy(result.at[k], target, out_sems.at[k]))
         stores[k].start()
     wait_all(small)
-    kind = iota((owners, 8, rows), 1)
-    factor = jnp.where(kind == 0, near[None], jnp.where(kind == 1, far[None], 0.0))
-    chosen = iota((owners, 8, rows), 0) == dest[...].reshape(1, 1, rows)
-    picked = jnp.where(chosen, factor, 0.0).reshape(owners * 8, rows)
-    table = dot(blocks.reshape(owners * 8, LANES), picked, ((0,), (0,)))
-    equivalent[...] = jnp.sum(
-        jnp.where(iota((LANES, rows), 0) == lane[...], table, 0.0), axis=0, keepdims=True
-    )
+    chosen = (iota((owners, rows), 0) == dest[...]).astype(F32).astype(BF16)
+    table = short_dot(
+        jnp.concatenate(halves(blocks), axis=0),
+        jnp.concatenate([chosen] * 2, axis=0),
+        ((0,), (0,)),
+    )
+    spot = iota((LANES, rows), 0)
+    factor = jnp.where(spot == lane[...], near, 0.0)
+    factor = jnp.where(spot == lane[...] + slots, far, factor)
+    equivalent[...] = jnp.sum(factor * table, axis=0, keepdims=True)
     stores.append(pltpu.make_async_copy(equivalent, equivalent_hbm, out_sems.at[count]))
     stores[count].start()
     wait_all(stores)
@@ -542,7 +584,7 @@
     row_scratch = pltpu.VMEM((1, rows), jnp.int32)
     send, lane = pl.pallas_call(
         functools.partial(pack_kernel, slots, patches),
-        out_shape=(shape(owners, 8, LANES), pltpu.HBM((1, rows), jnp.int32)),
+        out_shape=(shape(owners, LANES), pltpu.HBM((1, rows), jnp.int32)),
         in_specs=[HBM] * 6 + [SMEM],
         out_specs=(VMEM, HBM),
         scratch_shapes=[row_scratch] * 4
@@ -551,6 +593,7 @@
             pltpu.VMEM((1, rows), F32),
             pltpu.VMEM((8, rows), F32),
             row_scratch,
+            pltpu.VMEM((LANES, rows), F32),
             DMA((7,)),
         ],
         compiler_params=PARAMS,
@@ -644,33 +687,35 @@
         compiler_params=PARAMS,
         name="middle",
     )(*parts, *stay(ensemble), feat, ivert, squares)
-    parts = halo(*outs)
-    send, kept_late = pl.pallas_call(
-        functools.partial(last_kernel, slots),
-        out_shape=(shape(owners, 8, LANES), kept_shape),
-        in_specs=[ANY] * 6 + [HBM] + [VMEM] * 4,
-        out_specs=(VMEM, HBM),
-        scratch_shapes=work + [pltpu.VMEM((16, total), F32)] + sems,
-        compiler_params=PARAMS,
-        name="last",
-    )(*parts, *stay(ensemble), feat, ivert, squares, image)
-    recv = exchange(send)
-    early, late = pl.pallas_call(
+    early = pl.pallas_call(
         control_kernel,
-        out_shape=(tile, tile),
-        in_specs=[HBM] * 4,
-        out_specs=(VMEM,) * 2,
+        out_shape=tile,
+        in_specs=[HBM] * 3,
+        out_specs=VMEM,
         scratch_shapes=[
-            pltpu.VMEM((2,) + kept_shape.shape, F32),
+            pltpu.VMEM(kept_shape.shape, F32),
             powers(2),
             tile_scratch,
             matrix_scratch,
             matrix_scratch,
-            DMA((4,)),
+            DMA((3,)),
         ],
         compiler_params=PARAMS,
         name="control",
-    )(*stay(kept_early, kept_late, vert_loc, static_vert))
+    )(*stay(kept_early, vert_loc, static_vert))
+    parts = halo(*outs)
+    send, late = pl.pallas_call(
+        functools.partial(last_kernel, slots),
+        out_shape=(shape(owners, LANES), tile),
+        in_specs=[ANY] * 6 + [HBM] * 3 + [VMEM] * 4,
+        out_specs=(VMEM,) * 2,
+        scratch_shapes=work
+        + [pltpu.VMEM((16, total), F32), tile_scratch, matrix_scratch, matrix_scratch]
+        + [DMA, DMA((10,))],
+        compiler_params=PARAMS,
+        name="last",
+    )(*parts, *stay(ensemble, vert_loc, static_vert), feat, ivert, squares, image)
+    recv = exchange(send)
     static, member, equivalent = pl.pallas_call(
         final_kernel,
         out_shape=(

time: 75.1 us -> 72.8 us (0.969)
  starting transfers between devices: 24.4 us -> 20.5 us
  local copies, waits for them, and re-layouts: 0.01 us -> 1.67 us
  waiting for transfers between devices: 15.3 us -> 16.3 us
    ppermute x2, starting transfers between devices: 9.02 us -> 7.14 us  [halo(): lat_a = lax.ppermute(fields, 'lat', lat_inner)]
    unnamed x4, local copies, waits for them, and re-layouts: 0.01 us -> 1.67 us
    ppermute x2, waiting for transfers between devices: 4.09 us -> 5.29 us  [halo(): side_a = lax.ppermute(edge_a, 'lon', lon_inner)]
    pallas_call x1, Pallas kernels: 3.75 us -> 2.74 us  [body(): pl.pallas_call(control_kernel, out_shape=tile, in_specs=[HBM] * 3, out_sp...]
    ppermute x2, starting transfers between devices: 3.69 us -> 2.8 us  [halo(): side_b = lax.ppermute(edge_b, 'lon', lon_outer)]
    all_to_all x1, starting transfers between devices: 7.83 us -> 7.05 us  [exchange(): lax.all_to_all(blocks, ('lat', 'lon'), split_axis=0, concat_axis=0, tiled...]
  transfers between devices with their start and end apart: 13 -> 13, of which waited for: 7 -> 6; matrix products, arithmetic and copies ran while one was open for 0% -> 0% of each run, Pallas kernels for 6% -> 4%
where the time goes in v3:
time: 72.8 us; the launch traced here: 72.3 us
  starting transfers between devices  20.5 us (28%)
  Pallas kernels  18.1 us (25%)
  waiting for transfers between devices  16.3 us (22%)
  blocking collectives  14.3 us (20%)
  local copies, waits for them, and re-layouts  1.67 us (2%)
  between operations  1.45 us (2%)
    all_to_all x1, blocking collectives, exchange(): lax.all_to_all(blocks, ('lat', 'lon'), split_axis=0, concat_axis=0, tiled...  14.3 us
    ppermute x2, starting transfers between devices, halo(): lat_a = lax.ppermute(fields, 'lat', lat_inner)  7.14 us
    all_to_all x1, starting transfers between devices, exchange(): lax.all_to_all(blocks, ('lat', 'lon'), split_axis=0, concat_axis=0, tiled...  7.05 us
    ppermute x2, waiting for transfers between devices, halo(): side_b = lax.ppermute(edge_b, 'lon', lon_outer)  6 us
    ppermute x2, waiting for transfers between devices, halo(): side_a = lax.ppermute(edge_a, 'lon', lon_inner)  5.29 us
    pallas_call x1, Pallas kernels, body(): pl.pallas_call(functools.partial(last_kernel, slots), out_shape=(shape(ow...  4.68 us
    all_to_all x1, waiting for transfers between devices, exchange(): lax.all_to_all(blocks, ('lat', 'lon'), split_axis=0, concat_axis=0, tiled...  4.32 us
    pallas_call x1, Pallas kernels, body(): pl.pallas_call(middle_kernel, out_shape=(shape(8, total), kept_shape, til...  4.23 us
  transfers between devices with their start and end apart: 13, of which 6 were waited for; matrix products, arithmetic and copies ran while one was open for 0% of the time, Pallas kernels for 4%

profile of v3, /device:TPU:0, one launch (start us, length us, event | category | flops | bytes accessed | tf_op | source)
XLA Modules:
  0.0 72.3 jit_solution(14454501456024950601)
XLA Ops:
  1.3 1.5 %pack.1 = (f32[32,128]{1,0:T(8,128)S(1)}, s32[1,256]{1,0:T(1,128)}) custom-call(s32[1,256]{1,0:T(1,128)} %bitcast.18, s32[1,256]{1,0:T(1,128)} %bitcast.20, s32[1,256]{1,0:T(1,128)} %bitcast.21, s32[1,256]{1,0:T(1,128)} %bitcast.22, f32[4,256]{1,0:T(4,128)} %hweight_hbm.1, f32[1,256]{1,0:T(1,128)} %bitcast.23, s32[1]{0:T(128)S(6)} %copy.17.count), custom_call_target="tpu_custom_call" | custom-call | tf_op jit(solution)/shard_map/pack/pallas_call | solution.py:585
  2.8 14.3 %all_to_all.22 = f32[32,1,128]{2,1,0:T(1,128)S(1)} all-to-all(f32[32,1,128]{2,1,0:T(1,128)S(1)} %bitcast.17), channel_id=1, replica_groups=mesh['lat'=4,'lon'=8] {'lat','lon'}, dimensions={0} | all-to-all | bytes 32768 | tf_op jit(solution)/shard_map/all_to_all | solution.py:620
  17.1 2.3 %first.1 = (f32[8,512]{1,0:T(8,128)S(1)}, f32[128,512]{1,0:T(8,128)S(1)}, f32[9,4,48,128]{3,2,1,0:T(8,128)S(1)}, f32[9,4,4,128]{3,2,1,0:T(4,128)S(1)}, f32[9,4,4,128]{3,2,1,0:T(4,128)S(1)}) custom-call(f32[32,128]{1,0:T(8,128)S(1)} %bitcast.16, f32[16,128]{1,0:T(8,128)} %inst_vert_hbm.1, f32[1,16]{1,0:T(1,128)} %bitcast.24, bf16[8,4,4,48,128]{4,3,2,1,0:T(8,128)(2,1)} %ens_hbm.5), custom_call_target="tpu_custom_call" | custom-call | tf_op jit(solution)/shard_map/first/pallas_call | solution.py:633
  19.4 0.7 collective-permute-start.1
  20.1 2.0 %collective-permute-start = (f32[9,4,48,128]{3,2,1,0:T(8,128)S(1)}, f32[9,4,48,128]{3,2,1,0:T(8,128)S(1)}, u32[]{:S(2)}, u32[]{:S(2)}) collective-permute-start(f32[9,4,48,128]{3,2,1,0:T(8,128)S(1)} %get-tuple-element.25.own), channel_id=1, source_target_pairs={{0,8},{8,0},{16,24},{24,16},{1,9},{9,1},{17,25},{25,17},{2,10},{10... | collective-permute-start | bytes 2654216 | tf_op jit(solution)/shard_map/ppermute | solution.py:669
  22.1 0.6 collective-permute-start.2
  22.7 1.4 %collective-permute-start.3 = (f32[9,4,4,128]{3,2,1,0:T(4,128)S(1)}, f32[9,4,4,128]{3,2,1,0:T(4,128)S(1)}, u32[]{:S(2)}, u32[]{:S(2)}) collective-permute-start(f32[9,4,4,128]{3,2,1,0:T(4,128)S(1)} %get-tuple-element.27), channel_id=1, source_target_pairs={{1,2},{2,1},{3,4},{4,3},{5,6},{6,5},{7,0},{0,7},{9,10},{10,9},{11,... | collective-permute-start | bytes 221192 | tf_op jit(solution)/shard_map/ppermute | solution.py:668
  24.1 2.3 %collective-permute-done.2.part_a = f32[9,4,4,128]{3,2,1,0:T(4,128)S(1)} collective-permute-done((f32[9,4,4,128]{3,2,1,0:T(4,128)S(1)}, f32[9,4,4,128]{3,2,1,0:T(4,128)S(1)}, u32[]{:S(2)}, u32[]{:S(2)}) %collective-permute-start.2) | collective-permute-done | bytes 73760 | tf_op jit(solution)/shard_map/ppermute | solution.py:667
  26.4 3.3 %collective-permute-done.3.part_b = f32[9,4,4,128]{3,2,1,0:T(4,128)S(1)} collective-permute-done((f32[9,4,4,128]{3,2,1,0:T(4,128)S(1)}, f32[9,4,4,128]{3,2,1,0:T(4,128)S(1)}, u32[]{:S(2)}, u32[]{:S(2)}) %collective-permute-start.3) | collective-permute-done | bytes 73760 | tf_op jit(solution)/shard_map/ppermute | solution.py:668
  29.8 0.1 collective-permute-start.4
  29.9 0.7 collective-permute-start.5
  30.5 0.0 copy-start
  30.6 0.8 %copy-done = f32[128,128]{1,0:T(8,128)S(1)} copy-done((f32[128,128]{1,0:T(8,128)S(1)}, f32[128,128]{1,0:T(8,128)}, u32[]{:S(2)}) %copy-start) | copy-done | bytes 65560
  31.4 0.0 copy-start.1
  31.4 0.8 %copy-done.1 = f32[128,128]{1,0:T(8,128)S(1)} copy-done((f32[128,128]{1,0:T(8,128)S(1)}, f32[128,128]{1,0:T(8,128)}, u32[]{:S(2)}) %copy-start.1) | copy-done | bytes 65560
  32.2 0.3 prepare.1.squares
  32.6 0.0 collective-permute-done.5.corner_b
  32.6 0.0 collective-permute-done.4.corner_a
  32.6 0.0 collective-permute-done.1.lat_b
  32.6 0.0 collective-permute-done.lat_a
  32.6 4.2 %middle.1 = (f32[8,512]{1,0:T(8,128)S(1)}, f32[9,8,56,128]{3,2,1,0:T(8,128)}, f32[9,4,48,128]{3,2,1,0:T(8,128)S(1)}, f32[9,4,4,128]{3,2,1,0:T(4,128)S(1)}, f32[9,4,4,128]{3,2,1,0:T(4,128)S(1)}) custom-call(f32[9,4,48,128]{3,2,1,0:T(8,128)S(1)} %get-tuple-element.25.own, f32[9,4,48,128]{3,2,1,0:T(8,128)S(1)} %collective-permute-done.lat_a, ...), custom_call_target="tpu_custom_call" | custom-call | tf_op jit(solution)/shard_map/middle/pallas_call | solution.py:681
  36.8 0.7 collective-permute-start.7
  37.6 5.2 %collective-permute-start.6 = (f32[9,4,48,128]{3,2,1,0:T(8,128)S(1)}, f32[9,4,48,128]{3,2,1,0:T(8,128)S(1)}, u32[]{:S(2)}, u32[]{:S(2)}) collective-permute-start(f32[9,4,48,128]{3,2,1,0:T(8,128)S(1)} %get-tuple-element.32.own), channel_id=1, source_target_pairs={{0,8},{8,0},{16,24},{24,16},{1,9},{9,1},{17,25},{25,17},{2,10},{10... | collective-permute-start | bytes 2654216 | tf_op jit(solution)/shard_map/ppermute | solution.py:669
  42.7 0.0 collective-permute-start.8
  42.7 1.4 %collective-permute-start.9 = (f32[9,4,4,128]{3,2,1,0:T(4,128)S(1)}, f32[9,4,4,128]{3,2,1,0:T(4,128)S(1)}, u32[]{:S(2)}, u32[]{:S(2)}) collective-permute-start(f32[9,4,4,128]{3,2,1,0:T(4,128)S(1)} %get-tuple-element.34), channel_id=1, source_target_pairs={{1,2},{2,1},{3,4},{4,3},{5,6},{6,5},{7,0},{0,7},{9,10},{10,9},{11,... | collective-permute-start | bytes 221192 | tf_op jit(solution)/shard_map/ppermute | solution.py:668
  44.1 3.0 %collective-permute-done.8.part_a = f32[9,4,4,128]{3,2,1,0:T(4,128)S(1)} collective-permute-done((f32[9,4,4,128]{3,2,1,0:T(4,128)S(1)}, f32[9,4,4,128]{3,2,1,0:T(4,128)S(1)}, u32[]{:S(2)}, u32[]{:S(2)}) %collective-permute-start.8) | collective-permute-done | bytes 73760 | tf_op jit(solution)/shard_map/ppermute | solution.py:667
  47.1 2.7 %collective-permute-done.9.part_b = f32[9,4,4,128]{3,2,1,0:T(4,128)S(1)} collective-permute-done((f32[9,4,4,128]{3,2,1,0:T(4,128)S(1)}, f32[9,4,4,128]{3,2,1,0:T(4,128)S(1)}, u32[]{:S(2)}, u32[]{:S(2)}) %collective-permute-start.9) | collective-permute-done | bytes 73760 | tf_op jit(solution)/shard_map/ppermute | solution.py:668
  49.8 0.1 collective-permute-start.10
  49.9 0.7 collective-permute-start.11
  50.6 0.0 collective-permute-done.11.corner_b
  50.6 0.7 collective-permute-done.10.corner_a
  51.3 0.0 collective-permute-done.7.lat_b
  51.3 0.0 collective-permute-done.6.lat_a
  51.3 4.7 %last.1 = (f32[32,128]{1,0:T(8,128)}, f32[9,4,48,128]{3,2,1,0:T(8,128)S(1)}) custom-call(f32[9,4,48,128]{3,2,1,0:T(8,128)S(1)} %get-tuple-element.32.own, f32[9,4,48,128]{3,2,1,0:T(8,128)S(1)} %collective-permute-done.6.lat_a, f32[9,4,48,128]{3,2,1,0:T(8,128)S(1)} %collective-permute-done.7.lat_b, f32[9,4,8,128]{3,2,1,0:T(8,128)S(1)} %get-tuple-element.35.cross, ...), custom_call_target="tpu_custom_call" | custom-call | tf_op jit(solution)/shard_map/last/pallas_call | solution.py:707
  55.9 7.1 %all-to-all-start.1 = ((f32[32,1,128]{2,1,0:T(1,128)}), f32[32,1,128]{2,1,0:T(1,128)S(1)}, u32[]{:S(2)}, u32[]{:S(2)}) async-start(f32[32,1,128]{2,1,0:T(1,128)} %bitcast.10), calls=%async_computation.1 | async-start | bytes 32768 | tf_op jit(solution)/shard_map/all_to_all | solution.py:620
  63.0 2.7 %control.1.early = f32[9,4,48,128]{3,2,1,0:T(8,128)S(1)} custom-call(f32[9,8,56,128]{3,2,1,0:T(8,128)} %get-tuple-element.39.kept, f32[128,128]{1,0:T(8,128)} %vert_hbm.3, f32[128,128]{1,0:T(8,128)} %static_hbm.3), custom_call_target="tpu_custom_call" | custom-call | tf_op jit(solution)/shard_map/control/pallas_call | solution.py:690
  65.8 4.3 %all-to-all-done.1 = f32[32,1,128]{2,1,0:T(1,128)S(1)} async-done(((f32[32,1,128]{2,1,0:T(1,128)}), f32[32,1,128]{2,1,0:T(1,128)S(1)}, u32[]{:S(2)}, u32[]{:S(2)}) %all-to-all-start.1) | async-done | bytes 16416 | tf_op jit(solution)/shard_map/all_to_all | solution.py:620
  70.1 2.2 %final.1 = (f32[4,48,128]{2,1,0:T(8,128)}, f32[8,4,48,128]{3,2,1,0:T(8,128)}, f32[1,256]{1,0:T(1,128)}) custom-call(f32[32,128]{1,0:T(8,128)S(1)} %bitcast.15, f32[9,4,48,128]{3,2,1,0:T(8,128)S(1)} %control.1.early, f32[9,4,48,128]{3,2,1,0:T(8,128)S(1)} %get-tuple-element.40.late, s32[1,256]{1,0:T(1,128)} %bitcast.19, s32[1,256]{1,0:T(1,128)} %get-tuple-element.41.lane_hbm), custom_call_target="tpu_custom_call" | custom-call | tf_op jit(solution)/shard_map/final/pallas_call | solution.py:719
  (2 shorter events, 0.1 us)
Async XLA Ops:
  19.4 13.2 %collective-permute-start.1 = (f32[9,4,48,128]{3,2,1,0:T(8,128)S(1)}, f32[9,4,48,128]{3,2,1,0:T(8,128)S(1)}, u32[]{:S(2)}, u32[]{:S(2)}) collective-permute-start(f32[9,4,48,128]{3,2,1,0:T(8,128)S(1)} %get-tuple-element.25.own), channel_id=1, source_target_pairs={{8,16},{16,8},{9,17},{17,9},{10,18},{18,10},{11,19},{19,11},{12,20... | collective-permute-start | bytes 2654216 | tf_op jit(solution)/shard_map/ppermute | solution.py:666
  20.1 12.5 %collective-permute-start = (f32[9,4,48,128]{3,2,1,0:T(8,128)S(1)}, f32[9,4,48,128]{3,2,1,0:T(8,128)S(1)}, u32[]{:S(2)}, u32[]{:S(2)}) collective-permute-start(f32[9,4,48,128]{3,2,1,0:T(8,128)S(1)} %get-tuple-element.25.own), channel_id=1, source_target_pairs={{0,8},{8,0},{16,24},{24,16},{1,9},{9,1},{17,25},{25,17},{2,10},{10... | collective-permute-start | bytes 2654216 | tf_op jit(solution)/shard_map/ppermute | solution.py:669
  22.1 4.4 %collective-permute-start.2 = (f32[9,4,4,128]{3,2,1,0:T(4,128)S(1)}, f32[9,4,4,128]{3,2,1,0:T(4,128)S(1)}, u32[]{:S(2)}, u32[]{:S(2)}) collective-permute-start(f32[9,4,4,128]{3,2,1,0:T(4,128)S(1)} %get-tuple-element.26), channel_id=1, source_target_pairs={{0,1},{1,0},{2,3},{3,2},{4,5},{5,4},{6,7},{7,6},{8,9},{9,8},{10,11... | collective-permute-start | bytes 221192 | tf_op jit(solution)/shard_map/ppermute | solution.py:667
  22.7 7.0 %collective-permute-start.3 = (f32[9,4,4,128]{3,2,1,0:T(4,128)S(1)}, f32[9,4,4,128]{3,2,1,0:T(4,128)S(1)}, u32[]{:S(2)}, u32[]{:S(2)}) collective-permute-start(f32[9,4,4,128]{3,2,1,0:T(4,128)S(1)} %get-tuple-element.27), channel_id=1, source_target_pairs={{1,2},{2,1},{3,4},{4,3},{5,6},{6,5},{7,0},{0,7},{9,10},{10,9},{11,... | collective-permute-start | bytes 221192 | tf_op jit(solution)/shard_map/ppermute | solution.py:668
  29.8 2.8 %collective-permute-start.4 = (f32[9,4,8,128]{3,2,1,0:T(8,128)S(1)}, f32[9,4,8,128]{3,2,1,0:T(8,128)S(1)}, u32[]{:S(2)}, u32[]{:S(2)}) collective-permute-start(f32[9,4,8,128]{3,2,1,0:T(8,128)S(1)} %get-tuple-element.28.cross), channel_id=1, source_target_pairs={{0,8},{8,0},{16,24},{24,16},{1,9},{9,1},{17,25},{25,17},{2,10},{10... | collective-permute-start | bytes 442376 | tf_op jit(solution)/shard_map/ppermute | solution.py:672
  29.9 2.7 %collective-permute-start.5 = (f32[9,2,8,128]{3,2,1,0:T(8,128)S(1)}, f32[9,2,8,128]{3,2,1,0:T(8,128)S(1)}, u32[]{:S(2)}, u32[]{:S(2)}) collective-permute-start(f32[9,2,8,128]{3,2,1,0:T(8,128)S(1)} %get-tuple-element.29), channel_id=1, source_target_pairs={{8,16},{16,8},{9,17},{17,9},{10,18},{18,10},{11,19},{19,11},{12,20... | collective-permute-start | bytes 221192 | tf_op jit(solution)/shard_map/ppermute | solution.py:671
  30.5 0.8 %copy-start = (f32[128,128]{1,0:T(8,128)S(1)}, f32[128,128]{1,0:T(8,128)}, u32[]{:S(2)}) copy-start(f32[128,128]{1,0:T(8,128)} %vert_hbm.3) | copy-start | bytes 196612
  31.4 0.8 %copy-start.1 = (f32[128,128]{1,0:T(8,128)S(1)}, f32[128,128]{1,0:T(8,128)}, u32[]{:S(2)}) copy-start(f32[128,128]{1,0:T(8,128)} %static_hbm.3) | copy-start | bytes 196612
  36.8 14.4 %collective-permute-start.7 = (f32[9,4,48,128]{3,2,1,0:T(8,128)S(1)}, f32[9,4,48,128]{3,2,1,0:T(8,128)S(1)}, u32[]{:S(2)}, u32[]{:S(2)}) collective-permute-start(f32[9,4,48,128]{3,2,1,0:T(8,128)S(1)} %get-tuple-element.32.own), channel_id=1, source_target_pairs={{8,16},{16,8},{9,17},{17,9},{10,18},{18,10},{11,19},{19,11},{12,20... | collective-permute-start | bytes 2654216 | tf_op jit(solution)/shard_map/ppermute | solution.py:666
  37.6 13.7 %collective-permute-start.6 = (f32[9,4,48,128]{3,2,1,0:T(8,128)S(1)}, f32[9,4,48,128]{3,2,1,0:T(8,128)S(1)}, u32[]{:S(2)}, u32[]{:S(2)}) collective-permute-start(f32[9,4,48,128]{3,2,1,0:T(8,128)S(1)} %get-tuple-element.32.own), channel_id=1, source_target_pairs={{0,8},{8,0},{16,24},{24,16},{1,9},{9,1},{17,25},{25,17},{2,10},{10... | collective-permute-start | bytes 2654216 | tf_op jit(solution)/shard_map/ppermute | solution.py:669
  42.7 4.4 %collective-permute-start.8 = (f32[9,4,4,128]{3,2,1,0:T(4,128)S(1)}, f32[9,4,4,128]{3,2,1,0:T(4,128)S(1)}, u32[]{:S(2)}, u32[]{:S(2)}) collective-permute-start(f32[9,4,4,128]{3,2,1,0:T(4,128)S(1)} %get-tuple-element.33), channel_id=1, source_target_pairs={{0,1},{1,0},{2,3},{3,2},{4,5},{5,4},{6,7},{7,6},{8,9},{9,8},{10,11... | collective-permute-start | bytes 221192 | tf_op jit(solution)/shard_map/ppermute | solution.py:667
  42.7 7.0 %collective-permute-start.9 = (f32[9,4,4,128]{3,2,1,0:T(4,128)S(1)}, f32[9,4,4,128]{3,2,1,0:T(4,128)S(1)}, u32[]{:S(2)}, u32[]{:S(2)}) collective-permute-start(f32[9,4,4,128]{3,2,1,0:T(4,128)S(1)} %get-tuple-element.34), channel_id=1, source_target_pairs={{1,2},{2,1},{3,4},{4,3},{5,6},{6,5},{7,0},{0,7},{9,10},{10,9},{11,... | collective-permute-start | bytes 221192 | tf_op jit(solution)/shard_map/ppermute | solution.py:668
  49.8 1.4 %collective-permute-start.10 = (f32[9,4,8,128]{3,2,1,0:T(8,128)S(1)}, f32[9,4,8,128]{3,2,1,0:T(8,128)S(1)}, u32[]{:S(2)}, u32[]{:S(2)}) collective-permute-start(f32[9,4,8,128]{3,2,1,0:T(8,128)S(1)} %get-tuple-element.35.cross), channel_id=1, source_target_pairs={{0,8},{8,0},{16,24},{24,16},{1,9},{9,1},{17,25},{25,17},{2,10},{10... | collective-permute-start | bytes 442376 | tf_op jit(solution)/shard_map/ppermute | solution.py:672
  49.9 0.7 collective-permute-start.11
  55.9 14.1 %all-to-all-start.1 = ((f32[32,1,128]{2,1,0:T(1,128)}), f32[32,1,128]{2,1,0:T(1,128)S(1)}, u32[]{:S(2)}, u32[]{:S(2)}) async-start(f32[32,1,128]{2,1,0:T(1,128)} %bitcast.10), calls=%async_computation.1 | async-start | bytes 32768 | tf_op jit(solution)/shard_map/all_to_all | solution.py:620

commit v4 on v3

--- a/solution.py
+++ b/solution.py
@@ -20,7 +20,6 @@
 F32 = jnp.float32
 BF16 = jnp.bfloat16
 
-ANY = pl.BlockSpec(memory_space=pl.ANY)
 HBM = pl.BlockSpec(memory_space=pltpu.HBM)
 VMEM = pl.BlockSpec(memory_space=pltpu.VMEM)
 SMEM = pl.BlockSpec(memory_space=pltpu.SMEM)
@@ -180,8 +179,8 @@
 def first_kernel(
     slots,
     recv, inst_vert_hbm, inst_err_hbm, ens_hbm,
-    feat, ivert, fields, edge_a, edge_b,
-    inst_vert, inst_err, ens, weights, high_weights, low_weights, grad, sems,
+    feat, ivert, ens, weights, high_weights, low_weights, fields, edge_a, edge_b,
+    inst_vert, inst_err, grad, sems,
 ):
     members = ens.shape[0]
     copies = fetch(
@@ -216,38 +215,51 @@
     adjoint_fields(feat[6:7], high_weights, low_weights, ivert, ens, copies[2:], grad, outs)
 
 
-def halo_copies(own, lat_a, lat_b, cross, corner_a, corner_b, field, sems):
-    rows_lat, rows_lon = own.shape[1:3]
-    odd = lax.rem(lax.axis_index("lat"), 2)
-    south = HALO + rows_lat
-    row_a = south * (1 - odd)
-    row_b = south * odd
-    far_a = (rows_lat - HALO) * odd
-    far_b = (rows_lat - HALO) * (1 - odd)
-    main = pl.ds(0, rows_lon)
-    side = pl.ds(rows_lon, 8)
-    mid = pl.ds(HALO, rows_lat)
-    plan = (
-        (own, field.at[:, mid, main]),
-        (cross, field.at[:, mid, side]),
-        (lat_a.at[:, pl.ds(far_a, HALO)], field.at[:, pl.ds(row_a, HALO), main]),
-        (lat_b.at[:, pl.ds(far_b, HALO)], field.at[:, pl.ds(row_b, HALO), main]),
-        (corner_a.at[:, pl.ds(far_a, HALO)], field.at[:, pl.ds(row_a, HALO), side]),
-        (corner_b.at[:, 0], field.at[:, row_b + (HALO - 1) * (1 - odd), side]),
-        (corner_b.at[:, 1], field.at[:, row_b + (HALO - 2) * (1 - odd) + odd, side]),
-    )
-    unused = row_b + (HALO - 1) * odd
-    field[:, pl.ds(unused, 1), rows_lon:] = jnp.zeros_like(field[:, pl.ds(unused, 1), rows_lon:])
-    return [pltpu.make_async_copy(s, d, sems.at[n]) for n, (s, d) in enumerate(plan)]
-
-
-def unfold_corner(field, rows_lon):
-    odd = lax.rem(lax.axis_index("lat"), 2)
-    row_b = (field.shape[1] - HALO) * odd
-    second = row_b + (HALO - 2) * (1 - odd) + odd
-    third = row_b + (HALO - 3) * (1 - odd) + 2 * odd
-    for k in range(field.shape[0]):
-        field[k, third, rows_lon:] = pltpu.roll(field[k, second, rows_lon:], 8 - FOLD, 0)
+def corner_terms(corner_a, corner_b, k, rows_lat, order):
+    odd = lax.rem(lax.axis_index("lat"), 2) == 1
+    near = {}
+    for r in range(1, HALO):
+        tile_a = jnp.where(odd, corner_a[k, rows_lat - r], corner_a[k, r - 1])
+        tile_b = corner_b[k, min(r, 2) - 1]
+        if r == 3:
+            tile_b = pltpu.roll(tile_b, 8 - FOLD, 0)
+        near[-r] = jnp.where(odd, tile_a, tile_b)
+        near[rows_lat - 1 + r] = jnp.where(odd, tile_b, tile_a)
+    none = jnp.zeros_like(near[-1])
+    line = {i: near.get(i, none) for i in range(1 - HALO, rows_lat + HALO - 1)}
+    powers = []
+    for m in range(1, order):
+        line = {
+            i: line[i - 1] + line[i + 1]
+            for i in range(1 - HALO + m, rows_lat + HALO - 1 - m)
+        }
+        powers.append(line)
+    factor = {2: (2.0,), 4: (4.0, 6.0, 4.0)}[order]
+    added = []
+    for i in range(rows_lat):
+        value = None
+        for m in range(1, order):
+            fresh = (factor[m - 1] * SMOOTH**m) * powers[m - 1][i]
+            fresh = jnp.concatenate([none, fresh, none], axis=0)
+            value = fresh if value is None else value + fresh
+            ring = pltpu.roll(value, 1, 0) + pltpu.roll(value, value.shape[0] - 1, 0)
+            value = CENTER * value + SMOOTH * ring
+        added.append((value[:8], value[16:]))
+    return added
+
+
+def with_corners(smooth, corner_a, corner_b, k, order):
+    rows_lat, rows_lon = smooth.shape[1:3]
+    added = corner_terms(corner_a, corner_b, k, rows_lat, order)
+    pieces = []
+    for i in range(rows_lat):
+        last, first = added[i]
+        pieces += [
+            smooth[k, i, :8] + first,
+            smooth[k, i, 8 : rows_lon - 8],
+            smooth[k, i, rows_lon - 8 :] + last,
+        ]
+    return jnp.concatenate(pieces, axis=0)
 
 
 def sides_kernel(part_a, part_b, cross, folded):
@@ -268,67 +280,68 @@
         folded[k, 1] = jnp.where(inner, pltpu.roll(near[2], FOLD, 0), near[1])
 
 
-def keep_copy(field, kept, sems):
-    inner = pl.ds(HALO // 2, field.shape[1] - HALO)
-    return pltpu.make_async_copy(field.at[:, inner], kept, sems.at[7])
-
-
-def smooth_power(field, powers, out, order, twice=None):
-    count, rows, width, _ = field.shape
-    rows_lat = rows - 2 * order
-    rows_lon = width - 8
+def smooth_kernel(own, lat_a, lat_b, cross, smooth, twice, powers):
+    count, rows_lat, rows_lon, _ = own.shape
+    width = rows_lon + 8
+    order = HALO
     lat = lax.axis_index("lat")
-    north = (lat > 0).astype(F32)
-    south = (lat < lax.axis_size("lat") - 1).astype(F32)
-    factor = {2: (2.0, 1.0), 4: (4.0, 6.0, 4.0, 1.0)}[order]
+    odd = lax.rem(lat, 2)
+    inside = jnp.where(odd == 1, lat < lax.axis_size("lat") - 1, lat > 0).astype(F32)
+    factor = (4.0, 6.0, 4.0, 1.0)
+
+    def turned(row):
+        return rows_lat - 1 - row + odd * (2 * row - rows_lat + 1)
+
+    def step(value):
+        ring = pltpu.roll(value, 1, 0) + pltpu.roll(value, width - 1, 0)
+        return CENTER * value + SMOOTH * ring
 
     def one(k, carry):
         for c in range(width // 8):
             cols = slice(8 * c, 8 * c + 8)
-            line = {i: field[k, i, cols] for i in range(rows)}
+            if c < rows_lon // 8:
+                line = {i: own[k, turned(i), cols] for i in range(rows_lat)}
+                for r in range(order):
+                    line[-1 - r] = lat_a[k, turned(rows_lat - 1 - r), cols]
+                    line[rows_lat + r] = lat_b[k, turned(r), cols]
+            else:
+                line = {i: cross[k, turned(i)] for i in range(rows_lat)}
+                none = jnp.zeros_like(line[0])
+                for r in range(order):
+                    line[-1 - r] = line[rows_lat + r] = none
             for m in range(1, order + 1):
                 fresh = {}
-                for i in range(m, rows - m):
+                for i in range(m - order, rows_lat + order - m):
                     value = line[i - 1] + line[i + 1]
-                    if i < order:
-                        value = value * north
-                    if i >= order + rows_lat:
-                        value = value * south
-                    fresh[i] = value
+                    fresh[i] = value * inside if i >= rows_lat else value
                 line = fresh
                 for i in range(rows_lat):
-                    powers[m - 1, i, cols] = line[order + i]
-
-        def step(value):
-            ring = pltpu.roll(value, 1, 0) + pltpu.roll(value, width - 1, 0)
-            return CENTER * value + SMOOTH * ring
-
+                    powers[m - 1, i, cols] = line[i]
         for i in range(rows_lat):
-            value = field[k, order + i]
+            row = turned(i)
+            value = jnp.concatenate([own[k, row], cross[k, row]], axis=0)
             for m in range(1, order + 1):
                 value = step(value)
-                if m == 1 and twice is not None:
+                if m == 1:
                     other = step(value + (2.0 * SMOOTH) * powers[0, i])
                     other = other + SMOOTH**2 * powers[1, i]
-                    twice[k, i] = other[:rows_lon]
+                    twice[k, row] = other[:rows_lon]
                 value = value + (factor[m - 1] * SMOOTH**m) * powers[m - 1, i]
-            out[k, i] = value[:rows_lon]
+            smooth[k, row] = value[:rows_lon]
         return carry
 
     lax.fori_loop(0, count, one, 0, unroll=count)
 
 
-def observe(field, powers, smooth, mixed, squares, ivert, weights, ens, ens_copy, twice=None):
+def observe(smooth, corner_a, corner_b, mixed, squares, ivert, weights, ens):
     members, windows, rows_lat, rows_lon, levels = ens.shape
     block = rows_lat * rows_lon
-    smooth_power(field, powers, smooth, 4, twice)
     shape = (rows_lat, rows_lon, levels)
     for k in range(members + 1):
         square = squares[0] if k < members else squares[1]
-        pair = jnp.concatenate(halves(smooth[k].reshape(block, levels)), axis=1)
+        pair = jnp.concatenate(halves(with_corners(smooth, corner_a, corner_b, k, 4)), axis=1)
         product = short_dot(pair, square)
         mixed[k] = (product[:, :levels] + product[:, levels:]).reshape(shape)
-    ens_copy.wait()
     slots = weights.shape[1]
     image = jnp.zeros((8, slots), F32)
     high, low = halves(ivert[...])
@@ -349,52 +362,30 @@
 
 
 def middle_kernel(
-    own, lat_a, lat_b, cross, corner_a, corner_b, ens_hbm, feat, ivert, squares,
-    image, kept, fields, edge_a, edge_b,
-    ens, field, powers, smooth, mixed, weights, high_weights, low_weights, grad, sem, sems,
+    smooth, corner_a, corner_b, feat, ivert, ens, weights, high_weights, low_weights, squares,
+    image, fields, edge_a, edge_b,
+    mixed, grad,
 ):
-    copies = halo_copies(own, lat_a, lat_b, cross, corner_a, corner_b, field, sems)
-    for copy in copies:
-        copy.start()
-    ens_copy = pltpu.make_async_copy(ens_hbm, ens, sem)
-    ens_copy.start()
-    _, windows, rows_lat, rows_lon, _ = ens.shape
-    fill_weights(feat, weights, high_weights, low_weights, windows, rows_lat, rows_lon)
-    wait_all(copies)
-    unfold_corner(field, rows_lon)
-    keep = keep_copy(field, kept, sems)
-    keep.start()
-    seen = observe(field, powers, smooth, mixed, squares, ivert, weights, ens, ens_copy)
+    seen = observe(smooth, corner_a, corner_b, mixed, squares, ivert, weights, ens)
     scaled = seen * feat[7:8]
     image[...] = jnp.zeros_like(image)
     image[0:1] = seen
     image[1:2] = scaled
     outs = (fields, edge_a, edge_b)
     adjoint_fields(scaled, high_weights, low_weights, ivert, ens, (), grad, outs)
-    keep.wait()
 
 
 def last_kernel(
     slots,
-    own, lat_a, lat_b, cross, corner_a, corner_b, ens_hbm, vert_hbm, static_hbm,
-    feat, ivert, squares, image,
+    smooth, corner_a, corner_b, vert_hbm, static_hbm,
+    feat, ivert, ens, weights, squares, image, twice,
     send, late,
-    ens, field, powers, smooth, mixed, weights, high_weights, low_weights, terms, twice,
-    vert_loc, static_vert, sem, sems,
+    mixed, terms, vert_loc, static_vert, sems,
 ):
-    copies = halo_copies(own, lat_a, lat_b, cross, corner_a, corner_b, field, sems)
-    for copy in copies:
-        copy.start()
-    ens_copy = pltpu.make_async_copy(ens_hbm, ens, sem)
-    ens_copy.start()
-    _, windows, rows_lat, rows_lon, _ = ens.shape
-    fill_weights(feat, weights, high_weights, low_weights, windows, rows_lat, rows_lon)
-    matrices = fetch((vert_hbm, static_hbm), (vert_loc, static_vert), sems.at[pl.ds(8, 2)])
-    wait_all(copies)
-    unfold_corner(field, rows_lon)
-    second = observe(field, powers, smooth, mixed, squares, ivert, weights, ens, ens_copy, twice)
+    matrices = fetch((vert_hbm, static_hbm), (vert_loc, static_vert), sems)
+    second = observe(smooth, corner_a, corner_b, mixed, squares, ivert, weights, ens)
     wait_all(matrices)
-    to_control(twice, vert_loc, static_vert, late)
+    to_control(twice, corner_a, corner_b, vert_loc, static_vert, late)
     start = feat[6:7]
     rinv = feat[7:8]
     first = image[0:1]
@@ -452,7 +443,7 @@
     send[...] = jnp.where(spot < 2 * slots, moved, tail)
 
 
-def to_control(smooth, vert_loc, static_vert, control):
+def to_control(smooth, corner_a, corner_b, vert_loc, static_vert, control):
     count, rows_lat, rows_lon, levels = smooth.shape
     blocks = []
     for scale, matrix in ((BETA_ENSEMBLE, vert_loc), (BETA_STATIC, static_vert)):
@@ -461,20 +452,17 @@
         lower = jnp.concatenate([low, jnp.zeros_like(low)], axis=1)
         blocks.append(jnp.concatenate([upper, lower], axis=0))
     for k in range(count):
-        pair = jnp.concatenate(halves(smooth[k].reshape(rows_lat * rows_lon, levels)), axis=1)
+        pair = jnp.concatenate(halves(with_corners(smooth, corner_a, corner_b, k, 2)), axis=1)
         product = short_dot(pair, blocks[k // (count - 1)], ((1,), (1,)))
         product = product[:, :levels] + product[:, levels:]
         control[k] = product.reshape(rows_lat, rows_lon, levels)
 
 
 def control_kernel(
-    kept, vert_hbm, static_hbm,
-    control,
-    field, powers, smooth, vert_loc, static_vert, sems,
+    twice, corner_a, corner_b, vert_hbm, static_hbm, control, vert_loc, static_vert, sems
 ):
-    wait_all(fetch((vert_hbm, static_hbm, kept), (vert_loc, static_vert, field), sems))
-    smooth_power(field, powers, smooth, 2)
-    to_control(smooth, vert_loc, static_vert, control)
+    wait_all(fetch((vert_hbm, static_hbm), (vert_loc, static_vert), sems))
+    to_control(twice, corner_a, corner_b, vert_loc, static_vert, control)
 
 
 def final_kernel(
@@ -571,7 +559,6 @@
     total = owners * slots
     patches = rows_lat // 2 * (rows_lon // 2)
     count = members + 1
-    width = rows_lon + 8
     lat_inner, lat_outer = swaps(lat_count, False)
     lon_inner, lon_outer = swaps(lon_count, True)
     tile = shape(count, rows_lat, rows_lon, levels)
@@ -620,28 +607,28 @@
         return lax.all_to_all(blocks, ("lat", "lon"), split_axis=0, concat_axis=0, tiled=True)
 
     recv = exchange(send)
-    ens_scratch = pltpu.VMEM(ensemble.shape, ensemble.dtype)
-    field_scratch = pltpu.VMEM((count, rows_lat + 2 * HALO, width, levels), F32)
+    cells = windows * rows_lat * rows_lon
     tile_scratch = pltpu.VMEM(tile.shape, F32)
-    weight_scratch = pltpu.VMEM((windows * rows_lat * rows_lon, total), F32)
-    half_scratch = pltpu.VMEM(weight_scratch.shape, BF16)
-    grad_scratch = pltpu.VMEM((windows * rows_lat * rows_lon, levels), F32)
-
-    def powers(order):
-        return pltpu.VMEM((order, rows_lat, width, levels), F32)
-
-    feat, ivert, *outs = pl.pallas_call(
+    grad_scratch = pltpu.VMEM((cells, levels), F32)
+
+    feat, ivert, ens, *weights, fields, edge_a, edge_b = pl.pallas_call(
         functools.partial(first_kernel, slots),
-        out_shape=(shape(8, total), shape(levels, total), tile, edge, edge),
+        out_shape=(
+            shape(8, total),
+            shape(levels, total),
+            jax.ShapeDtypeStruct(ensemble.shape, ensemble.dtype),
+            shape(cells, total),
+            jax.ShapeDtypeStruct((cells, total), BF16),
+            jax.ShapeDtypeStruct((cells, total), BF16),
+            tile,
+            edge,
+            edge,
+        ),
         in_specs=[VMEM, HBM, HBM, HBM],
-        out_specs=(VMEM,) * 5,
+        out_specs=(VMEM,) * 9,
         scratch_shapes=[
             pltpu.VMEM(inst_vert.shape, F32),
             pltpu.VMEM((1, inst_err.shape[0]), F32),
-            ens_scratch,
-            weight_scratch,
-            half_scratch,
-            half_scratch,
             grad_scratch,
             DMA((2 + members,)),
         ],
@@ -670,51 +657,66 @@
         cross, folded = sides(side_a, side_b)
         corner_b = lax.ppermute(folded, "lat", lat_outer)
         corner_a = lax.ppermute(cross, "lat", lat_inner)
-        return (fields, lat_a, lat_b, cross, corner_a, corner_b)
-
-    parts = halo(*outs)
+        smooth, twice = pl.pallas_call(
+            smooth_kernel,
+            out_shape=(tile, tile),
+            in_specs=[VMEM] * 4,
+            out_specs=(VMEM,) * 2,
+            scratch_shapes=[pltpu.VMEM((HALO, rows_lat, rows_lon + 8, levels), F32)],
+            compiler_params=PARAMS,
+            name="smooth",
+        )(fields, lat_a, lat_b, cross)
+        return smooth, twice, corner_a, corner_b
+
+
+    smooth, twice, corner_a, corner_b = halo(fields, edge_a, edge_b)
     matrix_scratch = pltpu.VMEM(vert_loc.shape, F32)
-    work = [ens_scratch, field_scratch, powers(4), tile_scratch, tile_scratch, weight_scratch]
-    work += [half_scratch] * 2
-    sems = [DMA, DMA((8,))]
-    kept_shape = pltpu.HBM((count, rows_lat + HALO, width, levels), F32)
-    image, kept_early, *outs = pl.pallas_call(
+    image, *outs = pl.pallas_call(
         middle_kernel,
-        out_shape=(shape(8, total), kept_shape, tile, edge, edge),
-        in_specs=[ANY] * 6 + [HBM] + [VMEM] * 3,
-        out_specs=(VMEM, HBM) + (VMEM,) * 3,
-        scratch_shapes=work + [grad_scratch] + sems,
+        out_shape=(shape(8, total), tile, edge, edge),
+        in_specs=[VMEM] * 10,
+        out_specs=(VMEM,) * 4,
+        scratch_shapes=[tile_scratch, grad_scratch],
         compiler_params=PARAMS,
         name="middle",
-    )(*parts, *stay(ensemble), feat, ivert, squares)
+    )(smooth, corner_a, corner_b, feat, ivert, ens, *weights, squares)
     early = pl.pallas_call(
         control_kernel,
         out_shape=tile,
-        in_specs=[HBM] * 3,
+        in_specs=[VMEM] * 3 + [HBM] * 2,
         out_specs=VMEM,
-        scratch_shapes=[
-            pltpu.VMEM(kept_shape.shape, F32),
-            powers(2),
-            tile_scratch,
-            matrix_scratch,
-            matrix_scratch,
-            DMA((3,)),
-        ],
+        scratch_shapes=[matrix_scratch, matrix_scratch, DMA((2,))],
         compiler_params=PARAMS,
         name="control",
-    )(*stay(kept_early, vert_loc, static_vert))
-    parts = halo(*outs)
+    )(twice, corner_a, corner_b, *stay(vert_loc, static_vert))
+    smooth, twice, corner_a, corner_b = halo(*outs)
     send, late = pl.pallas_call(
         functools.partial(last_kernel, slots),
         out_shape=(shape(owners, LANES), tile),
-        in_specs=[ANY] * 6 + [HBM] * 3 + [VMEM] * 4,
+        in_specs=[VMEM] * 3 + [HBM] * 2 + [VMEM] * 7,
         out_specs=(VMEM,) * 2,
-        scratch_shapes=work
-        + [pltpu.VMEM((16, total), F32), tile_scratch, matrix_scratch, matrix_scratch]
-        + [DMA, DMA((10,))],
+        scratch_shapes=[
+            tile_scratch,
+            pltpu.VMEM((16, total), F32),
+            matrix_scratch,
+            matrix_scratch,
+            DMA((2,)),
+        ],
         compiler_params=PARAMS,
         name="last",
-    )(*parts, *stay(ensemble, vert_loc, static_vert), feat, ivert, squares, image)
+    )(
+        smooth,
+        corner_a,
+        corner_b,
+        *stay(vert_loc, static_vert),
+        feat,
+        ivert,
+        ens,
+        weights[0],
+        squares,
+        image,
+        twice,
+    )
     recv = exchange(send)
     static, member, equivalent = pl.pallas_call(
         final_kernel,

time: 72.8 us -> 69.3 us (0.952)
  starting transfers between devices: 20.5 us -> 18.7 us
  local copies, waits for them, and re-layouts: 1.67 us -> 0.01 us
  Pallas kernels: 18.1 us -> 16.9 us
  waiting for transfers between devices: 16.3 us -> 17.5 us
    ppermute x2, starting transfers between devices: 7.14 us -> 4.79 us  [halo(): lat_a = lax.ppermute(fields, 'lat', lat_inner)]
    pallas_call x1, Pallas kernels: 4.68 us -> 2.49 us  [body(): pl.pallas_call(functools.partial(last_kernel, slots), out_shape=(shape(ow...]
    unnamed x4, local copies, waits for them, and re-layouts: 1.67 us -> 0.01 us
    all_to_all x1, waiting for transfers between devices: 4.32 us -> 5.6 us  [exchange(): lax.all_to_all(blocks, ('lat', 'lon'), split_axis=0, concat_axis=0, tiled...]
    ppermute x2, waiting for transfers between devices: 6 us -> 7.2 us  [halo(): side_b = lax.ppermute(edge_b, 'lon', lon_outer)]
    pallas_call x2 -> x4, Pallas kernels: 6.96 us -> 7.89 us  [the longest x2 4.26 us: halo(): pl.pallas_call(smooth_kernel, out_shape=(tile, tile), in_specs=[VMEM] * 4...]
    all_to_all x1, starting transfers between devices: 7.05 us -> 6.28 us  [exchange(): lax.all_to_all(blocks, ('lat', 'lon'), split_axis=0, concat_axis=0, tiled...]
    ppermute x2, starting transfers between devices: 0.61 us -> 1.37 us  [halo(): side_a = lax.ppermute(edge_a, 'lon', lon_inner)]
  transfers between devices with their start and end apart: 13 -> 13, of which waited for: 6 -> 5; matrix products, arithmetic and copies ran while one was open for 0% -> 0% of each run, Pallas kernels for 4% -> 9%
where the time goes in v4:
time: 69.3 us; the launch traced here: 68.9 us
  starting transfers between devices  18.7 us (27%)
  waiting for transfers between devices  17.5 us (25%)
  Pallas kernels  16.9 us (24%)
  blocking collectives  14.3 us (21%)
  between operations  1.52 us (2%)
    all_to_all x1, blocking collectives, exchange(): lax.all_to_all(blocks, ('lat', 'lon'), split_axis=0, concat_axis=0, tiled...  14.3 us
    ppermute x2, waiting for transfers between devices, halo(): side_b = lax.ppermute(edge_b, 'lon', lon_outer)  7.2 us
    all_to_all x1, starting transfers between devices, exchange(): lax.all_to_all(blocks, ('lat', 'lon'), split_axis=0, concat_axis=0, tiled...  6.28 us
    all_to_all x1, waiting for transfers between devices, exchange(): lax.all_to_all(blocks, ('lat', 'lon'), split_axis=0, concat_axis=0, tiled...  5.6 us
    ppermute x2, starting transfers between devices, halo(): lat_a = lax.ppermute(fields, 'lat', lat_inner)  4.79 us
    ppermute x2, waiting for transfers between devices, halo(): side_a = lax.ppermute(edge_a, 'lon', lon_inner)  4.68 us
    pallas_call x2, Pallas kernels, halo(): pl.pallas_call(smooth_kernel, out_shape=(tile, tile), in_specs=[VMEM] * 4...  4.26 us
    ppermute x2, starting transfers between devices, halo(): side_b = lax.ppermute(edge_b, 'lon', lon_outer)  2.78 us
  transfers between devices with their start and end apart: 13, of which 5 were waited for; matrix products, arithmetic and copies ran while one was open for 0% of the time, Pallas kernels for 9%

profile of v4, /device:TPU:0, one launch (start us, length us, event | category | flops | bytes accessed | tf_op | source)
XLA Modules:
  0.0 68.9 jit_solution(17966427154674099671)
XLA Ops:
  0.6 0.0 copy-start
  0.6 0.0 copy-start.1
  1.3 1.5 %pack.1 = (f32[32,128]{1,0:T(8,128)S(1)}, s32[1,256]{1,0:T(1,128)}) custom-call(s32[1,256]{1,0:T(1,128)} %bitcast.18, s32[1,256]{1,0:T(1,128)} %bitcast.20, s32[1,256]{1,0:T(1,128)} %bitcast.21, s32[1,256]{1,0:T(1,128)} %bitcast.22, f32[4,256]{1,0:T(4,128)} %hweight_hbm.1, f32[1,256]{1,0:T(1,128)} %bitcast.23, s32[1]{0:T(128)S(6)} %copy.17.count), custom_call_target="tpu_custom_call" | custom-call | tf_op jit(solution)/shard_map/pack/pallas_call | solution.py:572
  2.8 14.3 %all_to_all.22 = f32[32,1,128]{2,1,0:T(1,128)S(1)} all-to-all(f32[32,1,128]{2,1,0:T(1,128)S(1)} %bitcast.17), channel_id=1, replica_groups=mesh['lat'=4,'lon'=8] {'lat','lon'}, dimensions={0} | all-to-all | bytes 32768 | tf_op jit(solution)/shard_map/all_to_all | solution.py:607
  17.1 2.4 %first.1 = (f32[8,512]{1,0:T(8,128)S(1)}, f32[128,512]{1,0:T(8,128)S(1)}, bf16[8,4,4,48,128]{4,3,2,1,0:T(8,128)(2,1)S(1)}, f32[768,512]{1,0:T(8,128)S(1)}, bf16[...) custom-call(f32[32,128]{1,0:T(8,128)S(1)} %bitcast.16, ...), custom_call_target="tpu_custom_call" | custom-call | tf_op jit(solution)/shard_map/first/pallas_call | solution.py:614
  19.5 0.1 collective-permute-start
  19.6 0.7 %collective-permute-start.1 = (f32[9,4,48,128]{3,2,1,0:T(8,128)S(1)}, f32[9,4,48,128]{3,2,1,0:T(8,128)S(1)}, u32[]{:S(2)}, u32[]{:S(2)}) collective-permute-start(f32[9,4,48,128]{3,2,1,0:T(8,128)S(1)} %get-tuple-element.32.own), channel_id=1, source_target_pairs={{8,16},{16,8},{9,17},{17,9},{10,18},{18,10},{11,19},{19,11},{12,20... | collective-permute-start | bytes 2654216 | tf_op jit(solution)/shard_map/ppermute | solution.py:653
  20.3 0.7 collective-permute-start.2
  21.0 1.4 %collective-permute-start.3 = (f32[9,4,4,128]{3,2,1,0:T(4,128)S(1)}, f32[9,4,4,128]{3,2,1,0:T(4,128)S(1)}, u32[]{:S(2)}, u32[]{:S(2)}) collective-permute-start(f32[9,4,4,128]{3,2,1,0:T(4,128)S(1)} %get-tuple-element.34), channel_id=1, source_target_pairs={{1,2},{2,1},{3,4},{4,3},{5,6},{6,5},{7,0},{0,7},{9,10},{10,9},{11,... | collective-permute-start | bytes 221192 | tf_op jit(solution)/shard_map/ppermute | solution.py:655
  22.4 2.3 %collective-permute-done.2.part_a = f32[9,4,4,128]{3,2,1,0:T(4,128)S(1)} collective-permute-done((f32[9,4,4,128]{3,2,1,0:T(4,128)S(1)}, f32[9,4,4,128]{3,2,1,0:T(4,128)S(1)}, u32[]{:S(2)}, u32[]{:S(2)}) %collective-permute-start.2) | collective-permute-done | bytes 73760 | tf_op jit(solution)/shard_map/ppermute | solution.py:654
  24.8 3.5 %collective-permute-done.3.part_b = f32[9,4,4,128]{3,2,1,0:T(4,128)S(1)} collective-permute-done((f32[9,4,4,128]{3,2,1,0:T(4,128)S(1)}, f32[9,4,4,128]{3,2,1,0:T(4,128)S(1)}, u32[]{:S(2)}, u32[]{:S(2)}) %collective-permute-start.3) | collective-permute-done | bytes 73760 | tf_op jit(solution)/shard_map/ppermute | solution.py:655
  28.3 0.5 collective-permute-start.4
  28.8 0.7 collective-permute-start.5
  29.5 0.0 copy-done
  29.5 0.0 copy-done.1
  29.5 0.3 prepare.1.squares
  29.8 0.0 collective-permute-done.lat_a
  29.8 0.0 collective-permute-done.1.lat_b
  29.8 2.1 %smooth.2 = (f32[9,4,48,128]{3,2,1,0:T(8,128)S(1)}, f32[9,4,48,128]{3,2,1,0:T(8,128)S(1)}) custom-call(f32[9,4,48,128]{3,2,1,0:T(8,128)S(1)} %get-tuple-element.32.own, f32[9,4,48,128]{3,2,1,0:T(8,128)S(1)} %collective-permute-done.lat_a, f32[9,4,48,128]{3,2,1,0:T(8,128)S(1)} %collective-permute-done.1.lat_b, f32[9,4,8,128]{3,2,1,0:T(8,128)S(1)} %get-tuple-element.35.cross), custom_call_target="tpu_custom_call" | custom-call | tf_op jit(solution)/shard_map/smooth/pallas_call | solution.py:660
  32.0 0.0 collective-permute-done.5.corner_b
  32.0 0.0 collective-permute-done.4.corner_a
  32.0 2.2 %middle.1 = (f32[8,512]{1,0:T(8,128)S(1)}, f32[9,4,48,128]{3,2,1,0:T(8,128)S(1)}, f32[9,4,4,128]{3,2,1,0:T(4,128)S(1)}, f32[9,4,4,128]{3,2,1,0:T(4,128)S(1)}) custom-call(f32[9,4,48,128]{3,2,1,0:T(8,128)S(1)} %get-tuple-element.36.smooth, f32[9,4,8,128]{3,2,1,0:T(8,128)S(1)} %collective-permute-done.4.corner_a, ...), custom_call_target="tpu_custom_call" | custom-call | tf_op jit(solution)/shard_map/middle/pallas_call | solution.py:674
  34.2 4.7 %collective-permute-start.6 = (f32[9,4,48,128]{3,2,1,0:T(8,128)S(1)}, f32[9,4,48,128]{3,2,1,0:T(8,128)S(1)}, u32[]{:S(2)}, u32[]{:S(2)}) collective-permute-start(f32[9,4,48,128]{3,2,1,0:T(8,128)S(1)} %get-tuple-element.44.own), channel_id=1, source_target_pairs={{0,8},{8,0},{16,24},{24,16},{1,9},{9,1},{17,25},{25,17},{2,10},{10... | collective-permute-start | bytes 2654216 | tf_op jit(solution)/shard_map/ppermute | solution.py:656
  38.9 0.7 %collective-permute-start.7 = (f32[9,4,48,128]{3,2,1,0:T(8,128)S(1)}, f32[9,4,48,128]{3,2,1,0:T(8,128)S(1)}, u32[]{:S(2)}, u32[]{:S(2)}) collective-permute-start(f32[9,4,48,128]{3,2,1,0:T(8,128)S(1)} %get-tuple-element.44.own), channel_id=1, source_target_pairs={{8,16},{16,8},{9,17},{17,9},{10,18},{18,10},{11,19},{19,11},{12,20... | collective-permute-start | bytes 2654216 | tf_op jit(solution)/shard_map/ppermute | solution.py:653
  39.6 0.7 collective-permute-start.8
  40.3 1.4 %collective-permute-start.9 = (f32[9,4,4,128]{3,2,1,0:T(4,128)S(1)}, f32[9,4,4,128]{3,2,1,0:T(4,128)S(1)}, u32[]{:S(2)}, u32[]{:S(2)}) collective-permute-start(f32[9,4,4,128]{3,2,1,0:T(4,128)S(1)} %get-tuple-element.46), channel_id=1, source_target_pairs={{1,2},{2,1},{3,4},{4,3},{5,6},{6,5},{7,0},{0,7},{9,10},{10,9},{11,... | collective-permute-start | bytes 221192 | tf_op jit(solution)/shard_map/ppermute | solution.py:655
  41.7 2.3 %collective-permute-done.8.part_a = f32[9,4,4,128]{3,2,1,0:T(4,128)S(1)} collective-permute-done((f32[9,4,4,128]{3,2,1,0:T(4,128)S(1)}, f32[9,4,4,128]{3,2,1,0:T(4,128)S(1)}, u32[]{:S(2)}, u32[]{:S(2)}) %collective-permute-start.8) | collective-permute-done | bytes 73760 | tf_op jit(solution)/shard_map/ppermute | solution.py:654
  44.0 3.7 %collective-permute-done.9.part_b = f32[9,4,4,128]{3,2,1,0:T(4,128)S(1)} collective-permute-done((f32[9,4,4,128]{3,2,1,0:T(4,128)S(1)}, f32[9,4,4,128]{3,2,1,0:T(4,128)S(1)}, u32[]{:S(2)}, u32[]{:S(2)}) %collective-permute-start.9) | collective-permute-done | bytes 73760 | tf_op jit(solution)/shard_map/ppermute | solution.py:655
  47.8 0.3 collective-permute-start.10
  48.0 0.7 collective-permute-start.11
  48.7 0.0 collective-permute-done.6.lat_a
  48.7 0.0 collective-permute-done.7.lat_b
  48.7 2.1 %smooth.3 = (f32[9,4,48,128]{3,2,1,0:T(8,128)S(1)}, f32[9,4,48,128]{3,2,1,0:T(8,128)S(1)}) custom-call(f32[9,4,48,128]{3,2,1,0:T(8,128)S(1)} %get-tuple-element.44.own, f32[9,4,48,128]{3,2,1,0:T(8,128)S(1)} %collective-permute-done.6.lat_a, f32[9,4,48,128]{3,2,1,0:T(8,128)S(1)} %collective-permute-done.7.lat_b, f32[9,4,8,128]{3,2,1,0:T(8,128)S(1)} %get-tuple-element.47.cross), custom_call_target="tpu_custom_call" | custom-call | tf_op jit(solution)/shard_map/smooth/pallas_call | solution.py:660
  50.9 0.0 collective-permute-done.11.corner_b
  50.9 0.0 collective-permute-done.10.corner_a
  50.9 2.5 %last.1 = (f32[32,128]{1,0:T(8,128)}, f32[9,4,48,128]{3,2,1,0:T(8,128)S(1)}) custom-call(f32[9,4,48,128]{3,2,1,0:T(8,128)S(1)} %get-tuple-element.48.smooth, f32[9,4,8,128]{3,2,1,0:T(8,128)S(1)} %collective-permute-done.10.corner_a, f32[9,2,8,128]{3,2,1,0:T(8,128)S(1)} %collective-permute-done.11.corner_b, f32[128,128]{1,0:T(8,128)} %vert_hbm.3, ...), custom_call_target="tpu_custom_call" | custom-call | tf_op jit(solution)/shard_map/last/pallas_call | solution.py:693
  53.4 6.3 %all-to-all-start.1 = ((f32[32,1,128]{2,1,0:T(1,128)}), f32[32,1,128]{2,1,0:T(1,128)S(1)}, u32[]{:S(2)}, u32[]{:S(2)}) async-start(f32[32,1,128]{2,1,0:T(1,128)} %bitcast.10), calls=%async_computation.1 | async-start | bytes 32768 | tf_op jit(solution)/shard_map/all_to_all | solution.py:607
  59.7 1.5 %control.1.early = f32[9,4,48,128]{3,2,1,0:T(8,128)S(1)} custom-call(f32[9,4,48,128]{3,2,1,0:T(8,128)S(1)} %get-tuple-element.53.twice, f32[9,4,8,128]{3,2,1,0:T(8,128)S(1)} %collective-permute-done.4.corner_a, f32[9,2,8,128]{3,2,1,0:T(8,128)S(1)} %collective-permute-done.5.corner_b, f32[128,128]{1,0:T(8,128)} %vert_hbm.3, f32[128,128]{1,0:T(8,128)} %static_hbm.3), custom_call_target="tpu_custom_call" | custom-call | tf_op jit(solution)/shard_map/control/pallas_call | solution.py:683
  61.1 5.6 %all-to-all-done.1 = f32[32,1,128]{2,1,0:T(1,128)S(1)} async-done(((f32[32,1,128]{2,1,0:T(1,128)}), f32[32,1,128]{2,1,0:T(1,128)S(1)}, u32[]{:S(2)}, u32[]{:S(2)}) %all-to-all-start.1) | async-done | bytes 16416 | tf_op jit(solution)/shard_map/all_to_all | solution.py:607
  66.7 2.2 %final.1 = (f32[4,48,128]{2,1,0:T(8,128)}, f32[8,4,48,128]{3,2,1,0:T(8,128)}, f32[1,256]{1,0:T(1,128)}) custom-call(f32[32,128]{1,0:T(8,128)S(1)} %bitcast.15, f32[9,4,48,128]{3,2,1,0:T(8,128)S(1)} %control.1.early, f32[9,4,48,128]{3,2,1,0:T(8,128)S(1)} %get-tuple-element.54.late, s32[1,256]{1,0:T(1,128)} %bitcast.19, s32[1,256]{1,0:T(1,128)} %get-tuple-element.55.lane_hbm), custom_call_target="tpu_custom_call" | custom-call | tf_op jit(solution)/shard_map/final/pallas_call | solution.py:721
  (2 shorter events, 0.1 us)
Async XLA Ops:
  0.6 28.8 %copy-start = (f32[128,128]{1,0:T(8,128)S(1)}, f32[128,128]{1,0:T(8,128)}, u32[]{:S(2)}) copy-start(f32[128,128]{1,0:T(8,128)} %vert_hbm.3) | copy-start | bytes 196612
  0.6 28.8 %copy-start.1 = (f32[128,128]{1,0:T(8,128)S(1)}, f32[128,128]{1,0:T(8,128)}, u32[]{:S(2)}) copy-start(f32[128,128]{1,0:T(8,128)} %static_hbm.3) | copy-start | bytes 196612
  19.5 10.3 %collective-permute-start = (f32[9,4,48,128]{3,2,1,0:T(8,128)S(1)}, f32[9,4,48,128]{3,2,1,0:T(8,128)S(1)}, u32[]{:S(2)}, u32[]{:S(2)}) collective-permute-start(f32[9,4,48,128]{3,2,1,0:T(8,128)S(1)} %get-tuple-element.32.own), channel_id=1, source_target_pairs={{0,8},{8,0},{16,24},{24,16},{1,9},{9,1},{17,25},{25,17},{2,10},{10... | collective-permute-start | bytes 2654216 | tf_op jit(solution)/shard_map/ppermute | solution.py:656
  19.6 10.2 %collective-permute-start.1 = (f32[9,4,48,128]{3,2,1,0:T(8,128)S(1)}, f32[9,4,48,128]{3,2,1,0:T(8,128)S(1)}, u32[]{:S(2)}, u32[]{:S(2)}) collective-permute-start(f32[9,4,48,128]{3,2,1,0:T(8,128)S(1)} %get-tuple-element.32.own), channel_id=1, source_target_pairs={{8,16},{16,8},{9,17},{17,9},{10,18},{18,10},{11,19},{19,11},{12,20... | collective-permute-start | bytes 2654216 | tf_op jit(solution)/shard_map/ppermute | solution.py:653
  20.3 4.4 %collective-permute-start.2 = (f32[9,4,4,128]{3,2,1,0:T(4,128)S(1)}, f32[9,4,4,128]{3,2,1,0:T(4,128)S(1)}, u32[]{:S(2)}, u32[]{:S(2)}) collective-permute-start(f32[9,4,4,128]{3,2,1,0:T(4,128)S(1)} %get-tuple-element.33), channel_id=1, source_target_pairs={{0,1},{1,0},{2,3},{3,2},{4,5},{5,4},{6,7},{7,6},{8,9},{9,8},{10,11... | collective-permute-start | bytes 221192 | tf_op jit(solution)/shard_map/ppermute | solution.py:654
  21.0 7.2 %collective-permute-start.3 = (f32[9,4,4,128]{3,2,1,0:T(4,128)S(1)}, f32[9,4,4,128]{3,2,1,0:T(4,128)S(1)}, u32[]{:S(2)}, u32[]{:S(2)}) collective-permute-start(f32[9,4,4,128]{3,2,1,0:T(4,128)S(1)} %get-tuple-element.34), channel_id=1, source_target_pairs={{1,2},{2,1},{3,4},{4,3},{5,6},{6,5},{7,0},{0,7},{9,10},{10,9},{11,... | collective-permute-start | bytes 221192 | tf_op jit(solution)/shard_map/ppermute | solution.py:655
  28.3 3.7 %collective-permute-start.4 = (f32[9,4,8,128]{3,2,1,0:T(8,128)S(1)}, f32[9,4,8,128]{3,2,1,0:T(8,128)S(1)}, u32[]{:S(2)}, u32[]{:S(2)}) collective-permute-start(f32[9,4,8,128]{3,2,1,0:T(8,128)S(1)} %get-tuple-element.35.cross), channel_id=1, source_target_pairs={{0,8},{8,0},{16,24},{24,16},{1,9},{9,1},{17,25},{25,17},{2,10},{10... | collective-permute-start | bytes 442376 | tf_op jit(solution)/shard_map/ppermute | solution.py:659
  28.8 3.2 %collective-permute-start.5 = (f32[9,2,8,128]{3,2,1,0:T(8,128)S(1)}, f32[9,2,8,128]{3,2,1,0:T(8,128)S(1)}, u32[]{:S(2)}, u32[]{:S(2)}) collective-permute-start(f32[9,2,8,128]{3,2,1,0:T(8,128)S(1)} %get-tuple-element.37), channel_id=1, source_target_pairs={{8,16},{16,8},{9,17},{17,9},{10,18},{18,10},{11,19},{19,11},{12,20... | collective-permute-start | bytes 221192 | tf_op jit(solution)/shard_map/ppermute | solution.py:658
  34.2 14.5 %collective-permute-start.6 = (f32[9,4,48,128]{3,2,1,0:T(8,128)S(1)}, f32[9,4,48,128]{3,2,1,0:T(8,128)S(1)}, u32[]{:S(2)}, u32[]{:S(2)}) collective-permute-start(f32[9,4,48,128]{3,2,1,0:T(8,128)S(1)} %get-tuple-element.44.own), channel_id=1, source_target_pairs={{0,8},{8,0},{16,24},{24,16},{1,9},{9,1},{17,25},{25,17},{2,10},{10... | collective-permute-start | bytes 2654216 | tf_op jit(solution)/shard_map/ppermute | solution.py:656
  38.9 9.8 %collective-permute-start.7 = (f32[9,4,48,128]{3,2,1,0:T(8,128)S(1)}, f32[9,4,48,128]{3,2,1,0:T(8,128)S(1)}, u32[]{:S(2)}, u32[]{:S(2)}) collective-permute-start(f32[9,4,48,128]{3,2,1,0:T(8,128)S(1)} %get-tuple-element.44.own), channel_id=1, source_target_pairs={{8,16},{16,8},{9,17},{17,9},{10,18},{18,10},{11,19},{19,11},{12,20... | collective-permute-start | bytes 2654216 | tf_op jit(solution)/shard_map/ppermute | solution.py:653
  39.6 4.4 %collective-permute-start.8 = (f32[9,4,4,128]{3,2,1,0:T(4,128)S(1)}, f32[9,4,4,128]{3,2,1,0:T(4,128)S(1)}, u32[]{:S(2)}, u32[]{:S(2)}) collective-permute-start(f32[9,4,4,128]{3,2,1,0:T(4,128)S(1)} %get-tuple-element.45), channel_id=1, source_target_pairs={{0,1},{1,0},{2,3},{3,2},{4,5},{5,4},{6,7},{7,6},{8,9},{9,8},{10,11... | collective-permute-start | bytes 221192 | tf_op jit(solution)/shard_map/ppermute | solution.py:654
  40.3 7.5 %collective-permute-start.9 = (f32[9,4,4,128]{3,2,1,0:T(4,128)S(1)}, f32[9,4,4,128]{3,2,1,0:T(4,128)S(1)}, u32[]{:S(2)}, u32[]{:S(2)}) collective-permute-start(f32[9,4,4,128]{3,2,1,0:T(4,128)S(1)} %get-tuple-element.46), channel_id=1, source_target_pairs={{1,2},{2,1},{3,4},{4,3},{5,6},{6,5},{7,0},{0,7},{9,10},{10,9},{11,... | collective-permute-start | bytes 221192 | tf_op jit(solution)/shard_map/ppermute | solution.py:655
  47.8 3.1 %collective-permute-start.10 = (f32[9,4,8,128]{3,2,1,0:T(8,128)S(1)}, f32[9,4,8,128]{3,2,1,0:T(8,128)S(1)}, u32[]{:S(2)}, u32[]{:S(2)}) collective-permute-start(f32[9,4,8,128]{3,2,1,0:T(8,128)S(1)} %get-tuple-element.47.cross), channel_id=1, source_target_pairs={{0,8},{8,0},{16,24},{24,16},{1,9},{9,1},{17,25},{25,17},{2,10},{10... | collective-permute-start | bytes 442376 | tf_op jit(solution)/shard_map/ppermute | solution.py:659
  48.0 2.8 %collective-permute-start.11 = (f32[9,2,8,128]{3,2,1,0:T(8,128)S(1)}, f32[9,2,8,128]{3,2,1,0:T(8,128)S(1)}, u32[]{:S(2)}, u32[]{:S(2)}) collective-permute-start(f32[9,2,8,128]{3,2,1,0:T(8,128)S(1)} %get-tuple-element.49), channel_id=1, source_target_pairs={{8,16},{16,8},{9,17},{17,9},{10,18},{18,10},{11,19},{19,11},{12,20... | collective-permute-start | bytes 221192 | tf_op jit(solution)/shard_map/ppermute | solution.py:658
  53.4 13.4 %all-to-all-start.1 = ((f32[32,1,128]{2,1,0:T(1,128)}), f32[32,1,128]{2,1,0:T(1,128)S(1)}, u32[]{:S(2)}, u32[]{:S(2)}) async-start(f32[32,1,128]{2,1,0:T(1,128)} %bitcast.10), calls=%async_computation.1 | async-start | bytes 32768 | tf_op jit(solution)/shard_map/all_to_all | solution.py:607

commit v5 on v4

--- a/solution.py
+++ b/solution.py
@@ -215,42 +215,49 @@
     adjoint_fields(feat[6:7], high_weights, low_weights, ivert, ens, copies[2:], grad, outs)
 
 
-def corner_terms(corner_a, corner_b, k, rows_lat, order):
-    odd = lax.rem(lax.axis_index("lat"), 2) == 1
-    near = {}
+def ring_step(value):
+    ring = pltpu.roll(value, 1, 0) + pltpu.roll(value, value.shape[0] - 1, 0)
+    return CENTER * value + SMOOTH * ring
+
+
+def side_terms(cross, corner_a, corner_b, k, order):
+    rows_lat = cross.shape[1]
+    lat = lax.axis_index("lat")
+    odd = lax.rem(lat, 2) == 1
+    north = (lat > 0).astype(F32)
+    south = (lat < lax.axis_size("lat") - 1).astype(F32)
+    line = {i: cross[k, i] for i in range(rows_lat)}
+    none = jnp.zeros_like(line[0])
     for r in range(1, HALO):
         tile_a = jnp.where(odd, corner_a[k, rows_lat - r], corner_a[k, r - 1])
         tile_b = corner_b[k, min(r, 2) - 1]
         if r == 3:
             tile_b = pltpu.roll(tile_b, 8 - FOLD, 0)
-        near[-r] = jnp.where(odd, tile_a, tile_b)
-        near[rows_lat - 1 + r] = jnp.where(odd, tile_b, tile_a)
-    none = jnp.zeros_like(near[-1])
-    line = {i: near.get(i, none) for i in range(1 - HALO, rows_lat + HALO - 1)}
-    powers = []
+        line[-r] = jnp.where(odd, tile_a, tile_b)
+        line[rows_lat - 1 + r] = jnp.where(odd, tile_b, tile_a)
+    powers = [line]
     for m in range(1, order):
-        line = {
-            i: line[i - 1] + line[i + 1]
-            for i in range(1 - HALO + m, rows_lat + HALO - 1 - m)
-        }
+        fresh = {}
+        for i in range(1 - HALO + m, rows_lat + HALO - 1 - m):
+            value = line[i - 1] + line[i + 1]
+            fresh[i] = value * north if i < 0 else value * south if i >= rows_lat else value
+        line = fresh
         powers.append(line)
-    factor = {2: (2.0,), 4: (4.0, 6.0, 4.0)}[order]
+    factor = {2: (1.0, 2.0), 4: (1.0, 4.0, 6.0, 4.0)}[order]
     added = []
     for i in range(rows_lat):
         value = None
-        for m in range(1, order):
-            fresh = (factor[m - 1] * SMOOTH**m) * powers[m - 1][i]
+        for m in range(order):
+            fresh = (factor[m] * SMOOTH**m) * powers[m][i]
             fresh = jnp.concatenate([none, fresh, none], axis=0)
-            value = fresh if value is None else value + fresh
-            ring = pltpu.roll(value, 1, 0) + pltpu.roll(value, value.shape[0] - 1, 0)
-            value = CENTER * value + SMOOTH * ring
+            value = ring_step(fresh if value is None else value + fresh)
         added.append((value[:8], value[16:]))
     return added
 
 
-def with_corners(smooth, corner_a, corner_b, k, order):
+def with_sides(smooth, cross, corner_a, corner_b, k, order):
     rows_lat, rows_lon = smooth.shape[1:3]
-    added = corner_terms(corner_a, corner_b, k, rows_lat, order)
+    added = side_terms(cross, corner_a, corner_b, k, order)
     pieces = []
     for i in range(rows_lat):
         last, first = added[i]
@@ -280,50 +287,42 @@
         folded[k, 1] = jnp.where(inner, pltpu.roll(near[2], FOLD, 0), near[1])
 
 
-def smooth_kernel(own, lat_a, lat_b, cross, smooth, twice, powers):
-    count, rows_lat, rows_lon, _ = own.shape
-    width = rows_lon + 8
-    order = HALO
+def row_turner(rows_lat):
+    odd = lax.rem(lax.axis_index("lat"), 2)
+    return lambda row: rows_lat - 1 - row + odd * (2 * row - rows_lat + 1)
+
+
+def near_kernel(own, lat_a, smooth, twice, powers):
+    count, rows_lat, rows_lon, levels = own.shape
     lat = lax.axis_index("lat")
     odd = lax.rem(lat, 2)
     inside = jnp.where(odd == 1, lat < lax.axis_size("lat") - 1, lat > 0).astype(F32)
+    turned = row_turner(rows_lat)
     factor = (4.0, 6.0, 4.0, 1.0)
-
-    def turned(row):
-        return rows_lat - 1 - row + odd * (2 * row - rows_lat + 1)
-
-    def step(value):
-        ring = pltpu.roll(value, 1, 0) + pltpu.roll(value, width - 1, 0)
-        return CENTER * value + SMOOTH * ring
+    powers[:, :, rows_lon:] = jnp.zeros_like(powers[:, :, rows_lon:])
+    none = jnp.zeros((8, levels), F32)
 
     def one(k, carry):
-        for c in range(width // 8):
+        for c in range(rows_lon // 8):
             cols = slice(8 * c, 8 * c + 8)
-            if c < rows_lon // 8:
-                line = {i: own[k, turned(i), cols] for i in range(rows_lat)}
-                for r in range(order):
-                    line[-1 - r] = lat_a[k, turned(rows_lat - 1 - r), cols]
-                    line[rows_lat + r] = lat_b[k, turned(r), cols]
-            else:
-                line = {i: cross[k, turned(i)] for i in range(rows_lat)}
-                none = jnp.zeros_like(line[0])
-                for r in range(order):
-                    line[-1 - r] = line[rows_lat + r] = none
-            for m in range(1, order + 1):
+            line = {i: own[k, turned(i), cols] for i in range(rows_lat)}
+            for r in range(HALO):
+                line[-1 - r] = lat_a[k, turned(rows_lat - 1 - r), cols]
+            for m in range(1, HALO + 1):
                 fresh = {}
-                for i in range(m - order, rows_lat + order - m):
-                    value = line[i - 1] + line[i + 1]
+                for i in range(m - HALO, rows_lat + min(m, HALO - m)):
+                    value = line[i - 1] + line[i + 1] if i + 1 in line else line[i - 1]
                     fresh[i] = value * inside if i >= rows_lat else value
                 line = fresh
                 for i in range(rows_lat):
                     powers[m - 1, i, cols] = line[i]
         for i in range(rows_lat):
             row = turned(i)
-            value = jnp.concatenate([own[k, row], cross[k, row]], axis=0)
-            for m in range(1, order + 1):
-                value = step(value)
+            value = jnp.concatenate([own[k, row], none], axis=0)
+            for m in range(1, HALO + 1):
+                value = ring_step(value)
                 if m == 1:
-                    other = step(value + (2.0 * SMOOTH) * powers[0, i])
+                    other = ring_step(value + (2.0 * SMOOTH) * powers[0, i])
                     other = other + SMOOTH**2 * powers[1, i]
                     twice[k, row] = other[:rows_lon]
                 value = value + (factor[m - 1] * SMOOTH**m) * powers[m - 1, i]
@@ -333,13 +332,49 @@
     lax.fori_loop(0, count, one, 0, unroll=count)
 
 
-def observe(smooth, corner_a, corner_b, mixed, squares, ivert, weights, ens):
+def far_kernel(lat_b, smooth_near, twice_near, smooth, twice, powers):
+    count, rows_lat, rows_lon, _ = lat_b.shape
+    turned = row_turner(rows_lat)
+    factor = (4.0, 6.0, 4.0, 1.0)
+    powers[:, :, rows_lon:] = jnp.zeros_like(powers[:, :, rows_lon:])
+
+    def one(k, carry):
+        for c in range(rows_lon // 8):
+            cols = slice(8 * c, 8 * c + 8)
+            line = {rows_lat + r: lat_b[k, turned(r), cols] for r in range(HALO)}
+            for m in range(1, HALO + 1):
+                fresh = {}
+                for i in range(rows_lat - m, rows_lat + HALO - m):
+                    terms = [line[n] for n in (i - 1, i + 1) if n in line]
+                    fresh[i] = sum(terms[1:], terms[0])
+                line = fresh
+                for i in range(max(rows_lat - m, 0), rows_lat):
+                    powers[m - 1, i, cols] = line[i]
+        for i in range(rows_lat):
+            row = turned(i)
+            value = None
+            for m in range(max(rows_lat - i, 1), HALO + 1):
+                fresh = (factor[m - 1] * SMOOTH**m) * powers[m - 1, i]
+                value = fresh if value is None else ring_step(value) + fresh
+            smooth[k, row] = smooth_near[k, row] + value[:rows_lon]
+            value = twice_near[k, row]
+            if i >= rows_lat - 1:
+                value = value + ring_step((2.0 * SMOOTH) * powers[0, i])[:rows_lon]
+            if i >= rows_lat - 2:
+                value = value + SMOOTH**2 * powers[1, i, :rows_lon]
+            twice[k, row] = value
+        return carry
+
+    lax.fori_loop(0, count, one, 0, unroll=count)
+
+
+def observe(smooth, cross, corner_a, corner_b, mixed, squares, ivert, weights, ens):
     members, windows, rows_lat, rows_lon, levels = ens.shape
     block = rows_lat * rows_lon
     shape = (rows_lat, rows_lon, levels)
     for k in range(members + 1):
         square = squares[0] if k < members else squares[1]
-        pair = jnp.concatenate(halves(with_corners(smooth, corner_a, corner_b, k, 4)), axis=1)
+        pair = jnp.concatenate(halves(with_sides(smooth, cross, corner_a, corner_b, k, 4)), axis=1)
         product = short_dot(pair, square)
         mixed[k] = (product[:, :levels] + product[:, levels:]).reshape(shape)
     slots = weights.shape[1]
@@ -362,11 +397,11 @@
 
 
 def middle_kernel(
-    smooth, corner_a, corner_b, feat, ivert, ens, weights, high_weights, low_weights, squares,
+    smooth, cross, corner_a, corner_b, feat, ivert, ens, weights, high_weights, low_weights, squares,
     image, fields, edge_a, edge_b,
     mixed, grad,
 ):
-    seen = observe(smooth, corner_a, corner_b, mixed, squares, ivert, weights, ens)
+    seen = observe(smooth, cross, corner_a, corner_b, mixed, squares, ivert, weights, ens)
     scaled = seen * feat[7:8]
     image[...] = jnp.zeros_like(image)
     image[0:1] = seen
@@ -377,15 +412,15 @@
 
 def last_kernel(
     slots,
-    smooth, corner_a, corner_b, vert_hbm, static_hbm,
+    smooth, cross, corner_a, corner_b, vert_hbm, static_hbm,
     feat, ivert, ens, weights, squares, image, twice,
     send, late,
     mixed, terms, vert_loc, static_vert, sems,
 ):
     matrices = fetch((vert_hbm, static_hbm), (vert_loc, static_vert), sems)
-    second = observe(smooth, corner_a, corner_b, mixed, squares, ivert, weights, ens)
+    second = observe(smooth, cross, corner_a, corner_b, mixed, squares, ivert, weights, ens)
     wait_all(matrices)
-    to_control(twice, corner_a, corner_b, vert_loc, static_vert, late)
+    to_control(twice, cross, corner_a, corner_b, vert_loc, static_vert, late)
     start = feat[6:7]
     rinv = feat[7:8]
     first = image[0:1]
@@ -443,7 +478,7 @@
     send[...] = jnp.where(spot < 2 * slots, moved, tail)
 
 
-def to_control(smooth, corner_a, corner_b, vert_loc, static_vert, control):
+def to_control(smooth, cross, corner_a, corner_b, vert_loc, static_vert, control):
     count, rows_lat, rows_lon, levels = smooth.shape
     blocks = []
     for scale, matrix in ((BETA_ENSEMBLE, vert_loc), (BETA_STATIC, static_vert)):
@@ -452,17 +487,17 @@
         lower = jnp.concatenate([low, jnp.zeros_like(low)], axis=1)
         blocks.append(jnp.concatenate([upper, lower], axis=0))
     for k in range(count):
-        pair = jnp.concatenate(halves(with_corners(smooth, corner_a, corner_b, k, 2)), axis=1)
+        pair = jnp.concatenate(halves(with_sides(smooth, cross, corner_a, corner_b, k, 2)), axis=1)
         product = short_dot(pair, blocks[k // (count - 1)], ((1,), (1,)))
         product = product[:, :levels] + product[:, levels:]
         control[k] = product.reshape(rows_lat, rows_lon, levels)
 
 
 def control_kernel(
-    twice, corner_a, corner_b, vert_hbm, static_hbm, control, vert_loc, static_vert, sems
+    twice, cross, corner_a, corner_b, vert_hbm, static_hbm, control, vert_loc, static_vert, sems
 ):
     wait_all(fetch((vert_hbm, static_hbm), (vert_loc, static_vert), sems))
-    to_control(twice, corner_a, corner_b, vert_loc, static_vert, control)
+    to_control(twice, cross, corner_a, corner_b, vert_loc, static_vert, control)
 
 
 def final_kernel(
@@ -657,43 +692,53 @@
         cross, folded = sides(side_a, side_b)
         corner_b = lax.ppermute(folded, "lat", lat_outer)
         corner_a = lax.ppermute(cross, "lat", lat_inner)
+        powers = pltpu.VMEM((HALO, rows_lat, rows_lon + 8, levels), F32)
         smooth, twice = pl.pallas_call(
-            smooth_kernel,
+            near_kernel,
             out_shape=(tile, tile),
-            in_specs=[VMEM] * 4,
+            in_specs=[VMEM] * 2,
             out_specs=(VMEM,) * 2,
-            scratch_shapes=[pltpu.VMEM((HALO, rows_lat, rows_lon + 8, levels), F32)],
+            scratch_shapes=[powers],
             compiler_params=PARAMS,
-            name="smooth",
-        )(fields, lat_a, lat_b, cross)
-        return smooth, twice, corner_a, corner_b
-
-
-    smooth, twice, corner_a, corner_b = halo(fields, edge_a, edge_b)
+            name="near",
+        )(fields, lat_a)
+        smooth, twice = pl.pallas_call(
+            far_kernel,
+            out_shape=(tile, tile),
+            in_specs=[VMEM] * 3,
+            out_specs=(VMEM,) * 2,
+            scratch_shapes=[powers],
+            compiler_params=PARAMS,
+            name="far",
+        )(lat_b, smooth, twice)
+        return smooth, twice, cross, corner_a, corner_b
+
+
+    smooth, twice, cross, corner_a, corner_b = halo(fields, edge_a, edge_b)
     matrix_scratch = pltpu.VMEM(vert_loc.shape, F32)
     image, *outs = pl.pallas_call(
         middle_kernel,
         out_shape=(shape(8, total), tile, edge, edge),
-        in_specs=[VMEM] * 10,
+        in_specs=[VMEM] * 11,
         out_specs=(VMEM,) * 4,
         scratch_shapes=[tile_scratch, grad_scratch],
         compiler_params=PARAMS,
         name="middle",
-    )(smooth, corner_a, corner_b, feat, ivert, ens, *weights, squares)
+    )(smooth, cross, corner_a, corner_b, feat, ivert, ens, *weights, squares)
     early = pl.pallas_call(
         control_kernel,
         out_shape=tile,
-        in_specs=[VMEM] * 3 + [HBM] * 2,
+        in_specs=[VMEM] * 4 + [HBM] * 2,
         out_specs=VMEM,
         scratch_shapes=[matrix_scratch, matrix_scratch, DMA((2,))],
         compiler_params=PARAMS,
         name="control",
-    )(twice, corner_a, corner_b, *stay(vert_loc, static_vert))
-    smooth, twice, corner_a, corner_b = halo(*outs)
+    )(twice, cross, corner_a, corner_b, *stay(vert_loc, static_vert))
+    smooth, twice, cross, corner_a, corner_b = halo(*outs)
     send, late = pl.pallas_call(
         functools.partial(last_kernel, slots),
         out_shape=(shape(owners, LANES), tile),
-        in_specs=[VMEM] * 3 + [HBM] * 2 + [VMEM] * 7,
+        in_specs=[VMEM] * 4 + [HBM] * 2 + [VMEM] * 7,
         out_specs=(VMEM,) * 2,
         scratch_shapes=[
             tile_scratch,
@@ -706,6 +751,7 @@
         name="last",
     )(
         smooth,
+        cross,
         corner_a,
         corner_b,
         *stay(vert_loc, static_vert),

time: 69.3 us -> 69.8 us (level)
  Pallas kernels: 16.9 us -> 18.8 us
  starting transfers between devices: 18.7 us -> 17.5 us
    pallas_call x3 -> x5, Pallas kernels: 5.72 us -> 6.88 us  [the longest x2 3.93 us: halo(): pl.pallas_call(near_kernel, out_shape=(tile, tile), in_specs=[VMEM] * 2,...]
    ppermute x2, waiting for transfers between devices: 7.2 us -> 6.24 us  [halo(): side_b = lax.ppermute(edge_b, 'lon', lon_outer)]
    all_to_all x1, starting transfers between devices: 6.28 us -> 5.42 us  [exchange(): lax.all_to_all(blocks, ('lat', 'lon'), split_axis=0, concat_axis=0, tiled...]
  transfers between devices with their start and end apart: 13 -> 13, of which waited for: 5 -> 5; matrix products, arithmetic and copies ran while one was open for 0% -> 0% of each run, Pallas kernels for 9% -> 10%
where the time goes in v5:
time: 69.8 us; the launch traced here: 69.3 us
  Pallas kernels  18.8 us (27%)
  starting transfers between devices  17.5 us (25%)
  waiting for transfers between devices  17.1 us (24%)
  blocking collectives  14.3 us (20%)
  between operations  1.7 us (2%)
    all_to_all x1, blocking collectives, exchange(): lax.all_to_all(blocks, ('lat', 'lon'), split_axis=0, concat_axis=0, tiled...  14.3 us
    ppermute x2, waiting for transfers between devices, halo(): side_b = lax.ppermute(edge_b, 'lon', lon_outer)  6.24 us
    all_to_all x1, waiting for transfers between devices, exchange(): lax.all_to_all(blocks, ('lat', 'lon'), split_axis=0, concat_axis=0, tiled...  5.6 us
    all_to_all x1, starting transfers between devices, exchange(): lax.all_to_all(blocks, ('lat', 'lon'), split_axis=0, concat_axis=0, tiled...  5.42 us
    ppermute x2, waiting for transfers between devices, halo(): side_a = lax.ppermute(edge_a, 'lon', lon_inner)  5.23 us
    ppermute x2, starting transfers between devices, halo(): lat_a = lax.ppermute(fields, 'lat', lat_inner)  4.23 us
    pallas_call x2, Pallas kernels, halo(): pl.pallas_call(near_kernel, out_shape=(tile, tile), in_specs=[VMEM] * 2,...  3.93 us
    pallas_call x1, Pallas kernels, body(): pl.pallas_call(functools.partial(last_kernel, slots), out_shape=(shape(ow...  2.97 us
  transfers between devices with their start and end apart: 13, of which 5 were waited for; matrix products, arithmetic and copies ran while one was open for 0% of the time, Pallas kernels for 10%

profile of v5, /device:TPU:0, one launch (start us, length us, event | category | flops | bytes accessed | tf_op | source)
XLA Modules:
  0.0 69.3 jit_solution(14592920668155140306)
XLA Ops:
  0.6 0.0 copy-start
  0.6 0.0 copy-start.1
  1.3 1.5 %pack.1 = (f32[32,128]{1,0:T(8,128)S(1)}, s32[1,256]{1,0:T(1,128)}) custom-call(s32[1,256]{1,0:T(1,128)} %bitcast.18, s32[1,256]{1,0:T(1,128)} %bitcast.20, s32[1,256]{1,0:T(1,128)} %bitcast.21, s32[1,256]{1,0:T(1,128)} %bitcast.22, f32[4,256]{1,0:T(4,128)} %hweight_hbm.1, f32[1,256]{1,0:T(1,128)} %bitcast.23, s32[1]{0:T(128)S(6)} %copy.17.count), custom_call_target="tpu_custom_call" | custom-call | tf_op jit(solution)/shard_map/pack/pallas_call | solution.py:607
  2.9 14.3 %all_to_all.22 = f32[32,1,128]{2,1,0:T(1,128)S(1)} all-to-all(f32[32,1,128]{2,1,0:T(1,128)S(1)} %bitcast.17), channel_id=1, replica_groups=mesh['lat'=4,'lon'=8] {'lat','lon'}, dimensions={0} | all-to-all | bytes 32768 | tf_op jit(solution)/shard_map/all_to_all | solution.py:642
  17.2 2.4 %first.1 = (f32[8,512]{1,0:T(8,128)S(1)}, f32[128,512]{1,0:T(8,128)S(1)}, bf16[8,4,4,48,128]{4,3,2,1,0:T(8,128)(2,1)S(1)}, f32[768,512]{1,0:T(8,128)S(1)}, bf16[...) custom-call(f32[32,128]{1,0:T(8,128)S(1)} %bitcast.16, ...), custom_call_target="tpu_custom_call" | custom-call | tf_op jit(solution)/shard_map/first/pallas_call | solution.py:649
  19.6 0.1 collective-permute-start.1
  19.7 0.7 %collective-permute-start = (f32[9,4,48,128]{3,2,1,0:T(8,128)S(1)}, f32[9,4,48,128]{3,2,1,0:T(8,128)S(1)}, u32[]{:S(2)}, u32[]{:S(2)}) collective-permute-start(f32[9,4,48,128]{3,2,1,0:T(8,128)S(1)} %get-tuple-element.36.own), channel_id=1, source_target_pairs={{8,16},{16,8},{9,17},{17,9},{10,18},{18,10},{11,19},{19,11},{12,20... | collective-permute-start | bytes 2654216 | tf_op jit(solution)/shard_map/ppermute | solution.py:688
  20.4 0.7 collective-permute-start.2
  21.1 1.4 %collective-permute-start.3 = (f32[9,4,4,128]{3,2,1,0:T(4,128)S(1)}, f32[9,4,4,128]{3,2,1,0:T(4,128)S(1)}, u32[]{:S(2)}, u32[]{:S(2)}) collective-permute-start(f32[9,4,4,128]{3,2,1,0:T(4,128)S(1)} %get-tuple-element.41), channel_id=1, source_target_pairs={{1,2},{2,1},{3,4},{4,3},{5,6},{6,5},{7,0},{0,7},{9,10},{10,9},{11,... | collective-permute-start | bytes 221192 | tf_op jit(solution)/shard_map/ppermute | solution.py:690
  22.5 2.3 %collective-permute-done.2.part_a = f32[9,4,4,128]{3,2,1,0:T(4,128)S(1)} collective-permute-done((f32[9,4,4,128]{3,2,1,0:T(4,128)S(1)}, f32[9,4,4,128]{3,2,1,0:T(4,128)S(1)}, u32[]{:S(2)}, u32[]{:S(2)}) %collective-permute-start.2) | collective-permute-done | bytes 73760 | tf_op jit(solution)/shard_map/ppermute | solution.py:689
  24.8 3.5 %collective-permute-done.3.part_b = f32[9,4,4,128]{3,2,1,0:T(4,128)S(1)} collective-permute-done((f32[9,4,4,128]{3,2,1,0:T(4,128)S(1)}, f32[9,4,4,128]{3,2,1,0:T(4,128)S(1)}, u32[]{:S(2)}, u32[]{:S(2)}) %collective-permute-start.3) | collective-permute-done | bytes 73760 | tf_op jit(solution)/shard_map/ppermute | solution.py:690
  28.3 0.5 collective-permute-start.4
  28.8 0.7 collective-permute-start.5
  29.5 0.0 copy-done
  29.5 0.0 copy-done.1
  29.5 0.3 prepare.1.squares
  29.8 0.0 collective-permute-done.1.lat_a
  29.9 2.0 %near.2 = (f32[9,4,48,128]{3,2,1,0:T(8,128)S(1)}, f32[9,4,48,128]{3,2,1,0:T(8,128)S(1)}) custom-call(f32[9,4,48,128]{3,2,1,0:T(8,128)S(1)} %get-tuple-element.36.own, f32[9,4,48,128]{3,2,1,0:T(8,128)S(1)} %collective-permute-done.1.lat_a), custom_call_target="tpu_custom_call" | custom-call | tf_op jit(solution)/shard_map/near/pallas_call | solution.py:696
  31.8 0.0 collective-permute-done.lat_b
  31.8 0.7 %far.2 = (f32[9,4,48,128]{3,2,1,0:T(8,128)S(1)}, f32[9,4,48,128]{3,2,1,0:T(8,128)S(1)}) custom-call(f32[9,4,48,128]{3,2,1,0:T(8,128)S(1)} %collective-permute-done.lat_b, f32[9,4,48,128]{3,2,1,0:T(8,128)S(1)} %get-tuple-element.37.smooth_near, f32[9,4,48,128]{3,2,1,0:T(8,128)S(1)} %get-tuple-element.38.twice_near), custom_call_target="tpu_custom_call" | custom-call | tf_op jit(solution)/shard_map/far/pallas_call | solution.py:705
  32.6 0.0 collective-permute-done.5.corner_b
  32.6 0.0 collective-permute-done.4.corner_a
  32.6 2.4 %middle.1 = (f32[8,512]{1,0:T(8,128)S(1)}, f32[9,4,48,128]{3,2,1,0:T(8,128)S(1)}, f32[9,4,4,128]{3,2,1,0:T(4,128)S(1)}, f32[9,4,4,128]{3,2,1,0:T(4,128)S(1)}) custom-call(f32[9,4,48,128]{3,2,1,0:T(8,128)S(1)} %get-tuple-element.39.smooth, f32[9,4,8,128]{3,2,1,0:T(8,128)S(1)} %get-tuple-element.42.cross, ...), custom_call_target="tpu_custom_call" | custom-call | tf_op jit(solution)/shard_map/middle/pallas_call | solution.py:719
  35.0 4.2 %collective-permute-start.7 = (f32[9,4,48,128]{3,2,1,0:T(8,128)S(1)}, f32[9,4,48,128]{3,2,1,0:T(8,128)S(1)}, u32[]{:S(2)}, u32[]{:S(2)}) collective-permute-start(f32[9,4,48,128]{3,2,1,0:T(8,128)S(1)} %get-tuple-element.50.own), channel_id=1, source_target_pairs={{0,8},{8,0},{16,24},{24,16},{1,9},{9,1},{17,25},{25,17},{2,10},{10... | collective-permute-start | bytes 2654216 | tf_op jit(solution)/shard_map/ppermute | solution.py:691
  39.1 0.7 %collective-permute-start.6 = (f32[9,4,48,128]{3,2,1,0:T(8,128)S(1)}, f32[9,4,48,128]{3,2,1,0:T(8,128)S(1)}, u32[]{:S(2)}, u32[]{:S(2)}) collective-permute-start(f32[9,4,48,128]{3,2,1,0:T(8,128)S(1)} %get-tuple-element.50.own), channel_id=1, source_target_pairs={{8,16},{16,8},{9,17},{17,9},{10,18},{18,10},{11,19},{19,11},{12,20... | collective-permute-start | bytes 2654216 | tf_op jit(solution)/shard_map/ppermute | solution.py:688
  39.8 0.1 collective-permute-start.8
  39.9 1.5 %collective-permute-start.9 = (f32[9,4,4,128]{3,2,1,0:T(4,128)S(1)}, f32[9,4,4,128]{3,2,1,0:T(4,128)S(1)}, u32[]{:S(2)}, u32[]{:S(2)}) collective-permute-start(f32[9,4,4,128]{3,2,1,0:T(4,128)S(1)} %get-tuple-element.55), channel_id=1, source_target_pairs={{1,2},{2,1},{3,4},{4,3},{5,6},{6,5},{7,0},{0,7},{9,10},{10,9},{11,... | collective-permute-start | bytes 221192 | tf_op jit(solution)/shard_map/ppermute | solution.py:690
  41.4 2.9 %collective-permute-done.8.part_a = f32[9,4,4,128]{3,2,1,0:T(4,128)S(1)} collective-permute-done((f32[9,4,4,128]{3,2,1,0:T(4,128)S(1)}, f32[9,4,4,128]{3,2,1,0:T(4,128)S(1)}, u32[]{:S(2)}, u32[]{:S(2)}) %collective-permute-start.8) | collective-permute-done | bytes 73760 | tf_op jit(solution)/shard_map/ppermute | solution.py:689
  44.3 2.8 %collective-permute-done.9.part_b = f32[9,4,4,128]{3,2,1,0:T(4,128)S(1)} collective-permute-done((f32[9,4,4,128]{3,2,1,0:T(4,128)S(1)}, f32[9,4,4,128]{3,2,1,0:T(4,128)S(1)}, u32[]{:S(2)}, u32[]{:S(2)}) %collective-permute-start.9) | collective-permute-done | bytes 73760 | tf_op jit(solution)/shard_map/ppermute | solution.py:690
  47.1 0.8 %collective-permute-start.10 = (f32[9,4,8,128]{3,2,1,0:T(8,128)S(1)}, f32[9,4,8,128]{3,2,1,0:T(8,128)S(1)}, u32[]{:S(2)}, u32[]{:S(2)}) collective-permute-start(f32[9,4,8,128]{3,2,1,0:T(8,128)S(1)} %get-tuple-element.56.cross), channel_id=1, source_target_pairs={{0,8},{8,0},{16,24},{24,16},{1,9},{9,1},{17,25},{25,17},{2,10},{10... | collective-permute-start | bytes 442376 | tf_op jit(solution)/shard_map/ppermute | solution.py:694
  47.8 0.8 %collective-permute-start.11 = (f32[9,2,8,128]{3,2,1,0:T(8,128)S(1)}, f32[9,2,8,128]{3,2,1,0:T(8,128)S(1)}, u32[]{:S(2)}, u32[]{:S(2)}) collective-permute-start(f32[9,2,8,128]{3,2,1,0:T(8,128)S(1)} %get-tuple-element.57), channel_id=1, source_target_pairs={{8,16},{16,8},{9,17},{17,9},{10,18},{18,10},{11,19},{19,11},{12,20... | collective-permute-start | bytes 221192 | tf_op jit(solution)/shard_map/ppermute | solution.py:693
  48.7 0.0 collective-permute-done.7.lat_a
  48.7 2.0 %near.3 = (f32[9,4,48,128]{3,2,1,0:T(8,128)S(1)}, f32[9,4,48,128]{3,2,1,0:T(8,128)S(1)}) custom-call(f32[9,4,48,128]{3,2,1,0:T(8,128)S(1)} %get-tuple-element.50.own, f32[9,4,48,128]{3,2,1,0:T(8,128)S(1)} %collective-permute-done.7.lat_a), custom_call_target="tpu_custom_call" | custom-call | tf_op jit(solution)/shard_map/near/pallas_call | solution.py:696
  50.7 0.0 collective-permute-done.6.lat_b
  50.7 0.7 %far.3 = (f32[9,4,48,128]{3,2,1,0:T(8,128)S(1)}, f32[9,4,48,128]{3,2,1,0:T(8,128)S(1)}) custom-call(f32[9,4,48,128]{3,2,1,0:T(8,128)S(1)} %collective-permute-done.6.lat_b, f32[9,4,48,128]{3,2,1,0:T(8,128)S(1)} %get-tuple-element.51.smooth_near, f32[9,4,48,128]{3,2,1,0:T(8,128)S(1)} %get-tuple-element.52.twice_near), custom_call_target="tpu_custom_call" | custom-call | tf_op jit(solution)/shard_map/far/pallas_call | solution.py:705
  51.4 0.0 collective-permute-done.11.corner_b
  51.4 0.0 collective-permute-done.10.corner_a
  51.5 3.0 %last.1 = (f32[32,128]{1,0:T(8,128)}, f32[9,4,48,128]{3,2,1,0:T(8,128)S(1)}) custom-call(f32[9,4,48,128]{3,2,1,0:T(8,128)S(1)} %get-tuple-element.53.smooth, f32[9,4,8,128]{3,2,1,0:T(8,128)S(1)} %get-tuple-element.56.cross, f32[9,4,8,128]{3,2,1,0:T(8,128)S(1)} %collective-permute-done.10.corner_a, f32[9,2,8,128]{3,2,1,0:T(8,128)S(1)} %collective-permute-done.11.corner_b, ...), custom_call_target="tpu_custom_call" | custom-call | tf_op jit(solution)/shard_map/last/pallas_call | solution.py:738
  54.4 5.4 %all-to-all-start.1 = ((f32[32,1,128]{2,1,0:T(1,128)}), f32[32,1,128]{2,1,0:T(1,128)S(1)}, u32[]{:S(2)}, u32[]{:S(2)}) async-start(f32[32,1,128]{2,1,0:T(1,128)} %bitcast.10), calls=%async_computation.1 | async-start | bytes 32768 | tf_op jit(solution)/shard_map/all_to_all | solution.py:642
  59.9 1.5 %control.1.early = f32[9,4,48,128]{3,2,1,0:T(8,128)S(1)} custom-call(f32[9,4,48,128]{3,2,1,0:T(8,128)S(1)} %get-tuple-element.61.twice, f32[9,4,8,128]{3,2,1,0:T(8,128)S(1)} %get-tuple-element.42.cross, f32[9,4,8,128]{3,2,1,0:T(8,128)S(1)} %collective-permute-done.4.corner_a, f32[9,2,8,128]{3,2,1,0:T(8,128)S(1)} %collective-permute-done.5.corner_b, ...), custom_call_target="tpu_custom_call" | custom-call | tf_op jit(solution)/shard_map/control/pallas_call | solution.py:728
  61.3 5.6 %all-to-all-done.1 = f32[32,1,128]{2,1,0:T(1,128)S(1)} async-done(((f32[32,1,128]{2,1,0:T(1,128)}), f32[32,1,128]{2,1,0:T(1,128)S(1)}, u32[]{:S(2)}, u32[]{:S(2)}) %all-to-all-start.1) | async-done | bytes 16416 | tf_op jit(solution)/shard_map/all_to_all | solution.py:642
  66.9 2.2 %final.1 = (f32[4,48,128]{2,1,0:T(8,128)}, f32[8,4,48,128]{3,2,1,0:T(8,128)}, f32[1,256]{1,0:T(1,128)}) custom-call(f32[32,128]{1,0:T(8,128)S(1)} %bitcast.15, f32[9,4,48,128]{3,2,1,0:T(8,128)S(1)} %control.1.early, f32[9,4,48,128]{3,2,1,0:T(8,128)S(1)} %get-tuple-element.62.late, s32[1,256]{1,0:T(1,128)} %bitcast.19, s32[1,256]{1,0:T(1,128)} %get-tuple-element.63.lane_hbm), custom_call_target="tpu_custom_call" | custom-call | tf_op jit(solution)/shard_map/final/pallas_call | solution.py:767
  (2 shorter events, 0.1 us)
Async XLA Ops:
  0.6 28.9 %copy-start = (f32[128,128]{1,0:T(8,128)S(1)}, f32[128,128]{1,0:T(8,128)}, u32[]{:S(2)}) copy-start(f32[128,128]{1,0:T(8,128)} %vert_hbm.3) | copy-start | bytes 196612
  0.6 28.9 %copy-start.1 = (f32[128,128]{1,0:T(8,128)S(1)}, f32[128,128]{1,0:T(8,128)}, u32[]{:S(2)}) copy-start(f32[128,128]{1,0:T(8,128)} %static_hbm.3) | copy-start | bytes 196612
  19.6 10.3 %collective-permute-start.1 = (f32[9,4,48,128]{3,2,1,0:T(8,128)S(1)}, f32[9,4,48,128]{3,2,1,0:T(8,128)S(1)}, u32[]{:S(2)}, u32[]{:S(2)}) collective-permute-start(f32[9,4,48,128]{3,2,1,0:T(8,128)S(1)} %get-tuple-element.36.own), channel_id=1, source_target_pairs={{0,8},{8,0},{16,24},{24,16},{1,9},{9,1},{17,25},{25,17},{2,10},{10... | collective-permute-start | bytes 2654216 | tf_op jit(solution)/shard_map/ppermute | solution.py:691
  19.7 12.2 %collective-permute-start = (f32[9,4,48,128]{3,2,1,0:T(8,128)S(1)}, f32[9,4,48,128]{3,2,1,0:T(8,128)S(1)}, u32[]{:S(2)}, u32[]{:S(2)}) collective-permute-start(f32[9,4,48,128]{3,2,1,0:T(8,128)S(1)} %get-tuple-element.36.own), channel_id=1, source_target_pairs={{8,16},{16,8},{9,17},{17,9},{10,18},{18,10},{11,19},{19,11},{12,20... | collective-permute-start | bytes 2654216 | tf_op jit(solution)/shard_map/ppermute | solution.py:688
  20.4 4.4 %collective-permute-start.2 = (f32[9,4,4,128]{3,2,1,0:T(4,128)S(1)}, f32[9,4,4,128]{3,2,1,0:T(4,128)S(1)}, u32[]{:S(2)}, u32[]{:S(2)}) collective-permute-start(f32[9,4,4,128]{3,2,1,0:T(4,128)S(1)} %get-tuple-element.40), channel_id=1, source_target_pairs={{0,1},{1,0},{2,3},{3,2},{4,5},{5,4},{6,7},{7,6},{8,9},{9,8},{10,11... | collective-permute-start | bytes 221192 | tf_op jit(solution)/shard_map/ppermute | solution.py:689
  21.1 7.2 %collective-permute-start.3 = (f32[9,4,4,128]{3,2,1,0:T(4,128)S(1)}, f32[9,4,4,128]{3,2,1,0:T(4,128)S(1)}, u32[]{:S(2)}, u32[]{:S(2)}) collective-permute-start(f32[9,4,4,128]{3,2,1,0:T(4,128)S(1)} %get-tuple-element.41), channel_id=1, source_target_pairs={{1,2},{2,1},{3,4},{4,3},{5,6},{6,5},{7,0},{0,7},{9,10},{10,9},{11,... | collective-permute-start | bytes 221192 | tf_op jit(solution)/shard_map/ppermute | solution.py:690
  28.3 4.3 %collective-permute-start.4 = (f32[9,4,8,128]{3,2,1,0:T(8,128)S(1)}, f32[9,4,8,128]{3,2,1,0:T(8,128)S(1)}, u32[]{:S(2)}, u32[]{:S(2)}) collective-permute-start(f32[9,4,8,128]{3,2,1,0:T(8,128)S(1)} %get-tuple-element.42.cross), channel_id=1, source_target_pairs={{0,8},{8,0},{16,24},{24,16},{1,9},{9,1},{17,25},{25,17},{2,10},{10... | collective-permute-start | bytes 442376 | tf_op jit(solution)/shard_map/ppermute | solution.py:694
  28.8 3.7 %collective-permute-start.5 = (f32[9,2,8,128]{3,2,1,0:T(8,128)S(1)}, f32[9,2,8,128]{3,2,1,0:T(8,128)S(1)}, u32[]{:S(2)}, u32[]{:S(2)}) collective-permute-start(f32[9,2,8,128]{3,2,1,0:T(8,128)S(1)} %get-tuple-element.43), channel_id=1, source_target_pairs={{8,16},{16,8},{9,17},{17,9},{10,18},{18,10},{11,19},{19,11},{12,20... | collective-permute-start | bytes 221192 | tf_op jit(solution)/shard_map/ppermute | solution.py:693
  35.0 13.7 %collective-permute-start.7 = (f32[9,4,48,128]{3,2,1,0:T(8,128)S(1)}, f32[9,4,48,128]{3,2,1,0:T(8,128)S(1)}, u32[]{:S(2)}, u32[]{:S(2)}) collective-permute-start(f32[9,4,48,128]{3,2,1,0:T(8,128)S(1)} %get-tuple-element.50.own), channel_id=1, source_target_pairs={{0,8},{8,0},{16,24},{24,16},{1,9},{9,1},{17,25},{25,17},{2,10},{10... | collective-permute-start | bytes 2654216 | tf_op jit(solution)/shard_map/ppermute | solution.py:691
  39.1 11.5 %collective-permute-start.6 = (f32[9,4,48,128]{3,2,1,0:T(8,128)S(1)}, f32[9,4,48,128]{3,2,1,0:T(8,128)S(1)}, u32[]{:S(2)}, u32[]{:S(2)}) collective-permute-start(f32[9,4,48,128]{3,2,1,0:T(8,128)S(1)} %get-tuple-element.50.own), channel_id=1, source_target_pairs={{8,16},{16,8},{9,17},{17,9},{10,18},{18,10},{11,19},{19,11},{12,20... | collective-permute-start | bytes 2654216 | tf_op jit(solution)/shard_map/ppermute | solution.py:688
  39.8 4.4 %collective-permute-start.8 = (f32[9,4,4,128]{3,2,1,0:T(4,128)S(1)}, f32[9,4,4,128]{3,2,1,0:T(4,128)S(1)}, u32[]{:S(2)}, u32[]{:S(2)}) collective-permute-start(f32[9,4,4,128]{3,2,1,0:T(4,128)S(1)} %get-tuple-element.54), channel_id=1, source_target_pairs={{0,1},{1,0},{2,3},{3,2},{4,5},{5,4},{6,7},{7,6},{8,9},{9,8},{10,11... | collective-permute-start | bytes 221192 | tf_op jit(solution)/shard_map/ppermute | solution.py:689
  39.9 7.1 %collective-permute-start.9 = (f32[9,4,4,128]{3,2,1,0:T(4,128)S(1)}, f32[9,4,4,128]{3,2,1,0:T(4,128)S(1)}, u32[]{:S(2)}, u32[]{:S(2)}) collective-permute-start(f32[9,4,4,128]{3,2,1,0:T(4,128)S(1)} %get-tuple-element.55), channel_id=1, source_target_pairs={{1,2},{2,1},{3,4},{4,3},{5,6},{6,5},{7,0},{0,7},{9,10},{10,9},{11,... | collective-permute-start | bytes 221192 | tf_op jit(solution)/shard_map/ppermute | solution.py:690
  47.1 4.4 %collective-permute-start.10 = (f32[9,4,8,128]{3,2,1,0:T(8,128)S(1)}, f32[9,4,8,128]{3,2,1,0:T(8,128)S(1)}, u32[]{:S(2)}, u32[]{:S(2)}) collective-permute-start(f32[9,4,8,128]{3,2,1,0:T(8,128)S(1)} %get-tuple-element.56.cross), channel_id=1, source_target_pairs={{0,8},{8,0},{16,24},{24,16},{1,9},{9,1},{17,25},{25,17},{2,10},{10... | collective-permute-start | bytes 442376 | tf_op jit(solution)/shard_map/ppermute | solution.py:694
  47.8 3.6 %collective-permute-start.11 = (f32[9,2,8,128]{3,2,1,0:T(8,128)S(1)}, f32[9,2,8,128]{3,2,1,0:T(8,128)S(1)}, u32[]{:S(2)}, u32[]{:S(2)}) collective-permute-start(f32[9,2,8,128]{3,2,1,0:T(8,128)S(1)} %get-tuple-element.57), channel_id=1, source_target_pairs={{8,16},{16,8},{9,17},{17,9},{10,18},{18,10},{11,19},{19,11},{12,20... | collective-permute-start | bytes 221192 | tf_op jit(solution)/shard_map/ppermute | solution.py:693
  54.4 12.5 %all-to-all-start.1 = ((f32[32,1,128]{2,1,0:T(1,128)}), f32[32,1,128]{2,1,0:T(1,128)S(1)}, u32[]{:S(2)}, u32[]{:S(2)}) async-start(f32[32,1,128]{2,1,0:T(1,128)} %bitcast.10), calls=%async_computation.1 | async-start | bytes 32768 | tf_op jit(solution)/shard_map/all_to_all | solution.py:642

commit v6 on v5

--- a/solution.py
+++ b/solution.py
@@ -53,6 +53,16 @@
     return (value >= 0) & (value < length)
 
 
+def ens_shape(ens):
+    head, rest = ens
+    return (head.shape[0] + rest.shape[0],) + head.shape[1:]
+
+
+def member(ens, k):
+    head, rest = ens
+    return head.at[k] if k < head.shape[0] else rest.at[k - head.shape[0]]
+
+
 def fetch(sources, targets, sems):
     copies = [
         pltpu.make_async_copy(source, target, sems.at[n])
@@ -74,17 +84,18 @@
 
 def pack_kernel(
     slots, patches,
-    dest_hbm, patch_hbm, window_hbm, inst_hbm, hweight_hbm, innov_hbm, count,
-    send, lane_hbm,
+    dest_hbm, patch_hbm, window_hbm, inst_hbm, hweight_hbm, innov_hbm, count, ens_hbm,
+    send, lane_hbm, head,
     dest, patch, window, inst, hweight, innov, feat, lane, table, sems,
 ):
-    wait_all(
-        fetch(
-            (dest_hbm, patch_hbm, window_hbm, inst_hbm, hweight_hbm, innov_hbm),
-            (dest, patch, window, inst, hweight, innov),
-            sems,
-        )
-    )
+    copies = fetch(
+        (dest_hbm, patch_hbm, window_hbm, inst_hbm, hweight_hbm, innov_hbm),
+        (dest, patch, window, inst, hweight, innov),
+        sems,
+    )
+    head_copy = pltpu.make_async_copy(ens_hbm.at[pl.ds(0, head.shape[0])], head, sems.at[7])
+    head_copy.start()
+    wait_all(copies)
     owners = send.shape[0]
     rows = dest.shape[1]
     destination = dest[...]
@@ -113,6 +124,7 @@
         ((1,), (1,)),
     )
     lane_copy.wait()
+    head_copy.wait()
 
 
 def prepare_kernel(vert_loc, static_vert, squares):
@@ -146,7 +158,7 @@
 
 def adjoint_fields(amount, high_weights, low_weights, ivert, ens, ens_copies, grad, outs):
     fields, edge_a, edge_b = outs
-    members, windows, rows_lat, rows_lon, levels = ens.shape
+    members, windows, rows_lat, rows_lon, levels = ens_shape(ens)
     block = rows_lat * rows_lon
     high, low = halves(ivert[...] * amount)
     both = jnp.concatenate([high, low], axis=0)
@@ -162,12 +174,12 @@
         return grad[first : first + rows_lon]
 
     for k in range(members + 1):
-        if k < members and ens_copies:
+        if k < members and ens_copies and ens_copies[k] is not None:
             ens_copies[k].wait()
         for a in range(rows_lat):
-            total = part(0, a) if k == members else ens[k, 0, a].astype(F32) * part(0, a)
+            total = part(0, a) if k == members else member(ens, k)[0, a].astype(F32) * part(0, a)
             for t in range(1, windows):
-                term = part(t, a) if k == members else ens[k, t, a].astype(F32) * part(t, a)
+                term = part(t, a) if k == members else member(ens, k)[t, a].astype(F32) * part(t, a)
                 total = total + term
             fields[k, a] = total
             east = total[rows_lon - HALO :]
@@ -178,17 +190,18 @@
 
 def first_kernel(
     slots,
-    recv, inst_vert_hbm, inst_err_hbm, ens_hbm,
-    feat, ivert, ens, weights, high_weights, low_weights, fields, edge_a, edge_b,
+    recv, inst_vert_hbm, inst_err_hbm, ens_hbm, head,
+    feat, ivert, rest, weights, high_weights, low_weights, fields, edge_a, edge_b,
     inst_vert, inst_err, grad, sems,
 ):
-    members = ens.shape[0]
+    ens = (head, rest)
+    loaded, missing = head.shape[0], rest.shape[0]
     copies = fetch(
-        [inst_vert_hbm, inst_err_hbm] + [ens_hbm.at[k] for k in range(members)],
-        [inst_vert, inst_err] + [ens.at[k] for k in range(members)],
+        [inst_vert_hbm, inst_err_hbm] + [ens_hbm.at[loaded + k] for k in range(missing)],
+        [inst_vert, inst_err] + [rest.at[k] for k in range(missing)],
         sems,
     )
-    members, windows, rows_lat, rows_lon, _ = ens.shape
+    _, windows, rows_lat, rows_lon, _ = ens_shape(ens)
     owners = recv.shape[0]
     total = feat.shape[1]
     source = iota((owners, total), 1) - iota((owners, total), 0) * slots
@@ -212,7 +225,8 @@
     feat[7:8] = rinv
     fill_weights(feat, weights, high_weights, low_weights, windows, rows_lat, rows_lon)
     outs = (fields, edge_a, edge_b)
-    adjoint_fields(feat[6:7], high_weights, low_weights, ivert, ens, copies[2:], grad, outs)
+    copies = [None] * loaded + copies[2:]
+    adjoint_fields(feat[6:7], high_weights, low_weights, ivert, ens, copies, grad, outs)
 
 
 def ring_step(value):
@@ -369,7 +383,7 @@
 
 
 def observe(smooth, cross, corner_a, corner_b, mixed, squares, ivert, weights, ens):
-    members, windows, rows_lat, rows_lon, levels = ens.shape
+    members, windows, rows_lat, rows_lon, levels = ens_shape(ens)
     block = rows_lat * rows_lon
     shape = (rows_lat, rows_lon, levels)
     for k in range(members + 1):
@@ -386,7 +400,7 @@
         for a in range(rows_lat):
             total = mixed[members, a]
             for k in range(members):
-                total = total + ens[k, t, a].astype(F32) * mixed[k, a]
+                total = total + member(ens, k)[t, a].astype(F32) * mixed[k, a]
             lines.append(total)
         increment = jnp.stack(lines).reshape(block, levels)
         high, low = halves(increment)
@@ -397,10 +411,11 @@
 
 
 def middle_kernel(
-    smooth, cross, corner_a, corner_b, feat, ivert, ens, weights, high_weights, low_weights, squares,
+    smooth, cross, corner_a, corner_b, feat, ivert, head, rest, weights, high_weights, low_weights, squares,
     image, fields, edge_a, edge_b,
     mixed, grad,
 ):
+    ens = (head, rest)
     seen = observe(smooth, cross, corner_a, corner_b, mixed, squares, ivert, weights, ens)
     scaled = seen * feat[7:8]
     image[...] = jnp.zeros_like(image)
@@ -413,11 +428,12 @@
 def last_kernel(
     slots,
     smooth, cross, corner_a, corner_b, vert_hbm, static_hbm,
-    feat, ivert, ens, weights, squares, image, twice,
+    feat, ivert, head, rest, weights, squares, image, twice,
     send, late,
     mixed, terms, vert_loc, static_vert, sems,
 ):
     matrices = fetch((vert_hbm, static_hbm), (vert_loc, static_vert), sems)
+    ens = (head, rest)
     second = observe(smooth, cross, corner_a, corner_b, mixed, squares, ivert, weights, ens)
     wait_all(matrices)
     to_control(twice, cross, corner_a, corner_b, vert_loc, static_vert, late)
@@ -532,8 +548,9 @@
     near = step + step_next * ((1.0 - step) + beta)
     far = -step_next * step
     stores = []
+    near, far = jnp.sum(near), jnp.sum(far)
     for k in range(count):
-        result[k] = near[None] * early[k] + far[None] * late[k]
+        result[k] = near * early[k] + far * late[k]
         target = member_hbm.at[k] if k < count - 1 else static_hbm
         stores.append(pltpu.make_async_copy(result.at[k], target, out_sems.at[k]))
         stores[k].start()
@@ -604,11 +621,16 @@
 
     dest = line(obs_dest)
     row_scratch = pltpu.VMEM((1, rows), jnp.int32)
-    send, lane = pl.pallas_call(
+    early_members = members // 2
+    send, lane, head = pl.pallas_call(
         functools.partial(pack_kernel, slots, patches),
-        out_shape=(shape(owners, LANES), pltpu.HBM((1, rows), jnp.int32)),
-        in_specs=[HBM] * 6 + [SMEM],
-        out_specs=(VMEM, HBM),
+        out_shape=(
+            shape(owners, LANES),
+            pltpu.HBM((1, rows), jnp.int32),
+            jax.ShapeDtypeStruct((early_members,) + ensemble.shape[1:], ensemble.dtype),
+        ),
+        in_specs=[HBM] * 6 + [SMEM, HBM],
+        out_specs=(VMEM, HBM, VMEM),
         scratch_shapes=[row_scratch] * 4
         + [
             pltpu.VMEM(obs_hweight.shape, F32),
@@ -616,7 +638,7 @@
             pltpu.VMEM((8, rows), F32),
             row_scratch,
             pltpu.VMEM((LANES, rows), F32),
-            DMA((7,)),
+            DMA((8,)),
         ],
         compiler_params=PARAMS,
         name="pack",
@@ -630,6 +652,7 @@
             line(innovation),
         ),
         obs_count,
+        *stay(ensemble),
     )
     squares = pl.pallas_call(
         prepare_kernel,
@@ -646,12 +669,12 @@
     tile_scratch = pltpu.VMEM(tile.shape, F32)
     grad_scratch = pltpu.VMEM((cells, levels), F32)
 
-    feat, ivert, ens, *weights, fields, edge_a, edge_b = pl.pallas_call(
+    feat, ivert, rest, *weights, fields, edge_a, edge_b = pl.pallas_call(
         functools.partial(first_kernel, slots),
         out_shape=(
             shape(8, total),
             shape(levels, total),
-            jax.ShapeDtypeStruct(ensemble.shape, ensemble.dtype),
+            jax.ShapeDtypeStruct((members - early_members,) + ensemble.shape[1:], ensemble.dtype),
             shape(cells, total),
             jax.ShapeDtypeStruct((cells, total), BF16),
             jax.ShapeDtypeStruct((cells, total), BF16),
@@ -659,17 +682,17 @@
             edge,
             edge,
         ),
-        in_specs=[VMEM, HBM, HBM, HBM],
+        in_specs=[VMEM, HBM, HBM, HBM, VMEM],
         out_specs=(VMEM,) * 9,
         scratch_shapes=[
             pltpu.VMEM(inst_vert.shape, F32),
             pltpu.VMEM((1, inst_err.shape[0]), F32),
             grad_scratch,
-            DMA((2 + members,)),
+            DMA((2 + members - early_members,)),
         ],
         compiler_params=PARAMS,
         name="first",
-    )(recv, *stay(inst_vert, inst_err.reshape(1, -1), ensemble))
+    )(recv, *stay(inst_vert, inst_err.reshape(1, -1), ensemble), head)
 
     def sides(part_a, part_b):
         return pl.pallas_call(
@@ -719,12 +742,12 @@
     image, *outs = pl.pallas_call(
         middle_kernel,
         out_shape=(shape(8, total), tile, edge, edge),
-        in_specs=[VMEM] * 11,
+        in_specs=[VMEM] * 12,
         out_specs=(VMEM,) * 4,
         scratch_shapes=[tile_scratch, grad_scratch],
         compiler_params=PARAMS,
         name="middle",
-    )(smooth, cross, corner_a, corner_b, feat, ivert, ens, *weights, squares)
+    )(smooth, cross, corner_a, corner_b, feat, ivert, head, rest, *weights, squares)
     early = pl.pallas_call(
         control_kernel,
         out_shape=tile,
@@ -738,7 +761,7 @@
     send, late = pl.pallas_call(
         functools.partial(last_kernel, slots),
         out_shape=(shape(owners, LANES), tile),
-        in_specs=[VMEM] * 4 + [HBM] * 2 + [VMEM] * 7,
+        in_specs=[VMEM] * 4 + [HBM] * 2 + [VMEM] * 8,
         out_specs=(VMEM,) * 2,
         scratch_shapes=[
             tile_scratch,
@@ -757,7 +780,8 @@
         *stay(vert_loc, static_vert),
         feat,
         ivert,
-        ens,
+        head,
+        rest,
         weights[0],
         squares,
         image,

time: 69.8 us -> 69.6 us (level)
  transfers between devices with their start and end apart: 13 -> 13, of which waited for: 5 -> 5; matrix products, arithmetic and copies ran while one was open for 0% -> 0% of each run, Pallas kernels for 10% -> 11%
where the time goes in v6:
time: 69.6 us; the launch traced here: 69.2 us
  Pallas kernels  18.6 us (27%)
  starting transfers between devices  17.5 us (25%)
  waiting for transfers between devices  17.1 us (25%)
  blocking collectives  14.3 us (21%)
  between operations  1.67 us (2%)
    all_to_all x1, blocking collectives, exchange(): lax.all_to_all(blocks, ('lat', 'lon'), split_axis=0, concat_axis=0, tiled...  14.3 us
    ppermute x2, waiting for transfers between devices, halo(): side_b = lax.ppermute(edge_b, 'lon', lon_outer)  6.24 us
    all_to_all x1, waiting for transfers between devices, exchange(): lax.all_to_all(blocks, ('lat', 'lon'), split_axis=0, concat_axis=0, tiled...  5.6 us
    all_to_all x1, starting transfers between devices, exchange(): lax.all_to_all(blocks, ('lat', 'lon'), split_axis=0, concat_axis=0, tiled...  5.42 us
    ppermute x2, waiting for transfers between devices, halo(): side_a = lax.ppermute(edge_a, 'lon', lon_inner)  5.22 us
    ppermute x2, starting transfers between devices, halo(): lat_a = lax.ppermute(fields, 'lat', lat_inner)  4.23 us
    pallas_call x2, Pallas kernels, halo(): pl.pallas_call(near_kernel, out_shape=(tile, tile), in_specs=[VMEM] * 2,...  3.93 us
    pallas_call x1, Pallas kernels, body(): pl.pallas_call(functools.partial(last_kernel, slots), out_shape=(shape(ow...  2.97 us
  transfers between devices with their start and end apart: 13, of which 5 were waited for; matrix products, arithmetic and copies ran while one was open for 0% of the time, Pallas kernels for 11%

profile of v6, /device:TPU:0, one launch (start us, length us, event | category | flops | bytes accessed | tf_op | source)
XLA Modules:
  0.0 69.2 jit_solution(17667061438303693273)
XLA Ops:
  1.3 1.5 %pack.1 = (f32[32,128]{1,0:T(8,128)S(1)}, s32[1,256]{1,0:T(1,128)}, bf16[4,4,4,48,128]{4,3,2,1,0:T(8,128)(2,1)S(1)}) custom-call(s32[1,256]{1,0:T(1,128)} %bitcast.18, s32[1,256]{1,0:T(1,128)} %bitcast.20, s32[1,256]{1,0:T(1,128)} %bitcast.21, s32[1,256]{1,0:T(1,128)} %bitcast.22, f32[4,256]{1,0:T(4,128)} %hweight_hbm.1, f32[1,256]{1,0:T(1,128)} %bitcast.23, ...), custom_call_target="tpu_custom_call" | custom-call | tf_op jit(solution)/shard_map/pack/pallas_call | solution.py:625
  2.8 0.0 copy-start
  2.8 0.0 copy-start.1
  2.9 14.3 %all_to_all.22 = f32[32,1,128]{2,1,0:T(1,128)S(1)} all-to-all(f32[32,1,128]{2,1,0:T(1,128)S(1)} %bitcast.17), channel_id=1, replica_groups=mesh['lat'=4,'lon'=8] {'lat','lon'}, dimensions={0} | all-to-all | bytes 32768 | tf_op jit(solution)/shard_map/all_to_all | solution.py:665
  17.1 2.2 %first.1 = (f32[8,512]{1,0:T(8,128)S(1)}, f32[128,512]{1,0:T(8,128)S(1)}, bf16[4,4,4,48,128]{4,3,2,1,0:T(8,128)(2,1)S(1)}, f32[768,512]{1,0:T(8,128)S(1)}, bf16[...) custom-call(f32[32,128]{1,0:T(8,128)S(1)} %bitcast.16, ...), custom_call_target="tpu_custom_call" | custom-call | tf_op jit(solution)/shard_map/first/pallas_call | solution.py:672
  19.4 0.1 collective-permute-start.1
  19.5 0.7 %collective-permute-start = (f32[9,4,48,128]{3,2,1,0:T(8,128)S(1)}, f32[9,4,48,128]{3,2,1,0:T(8,128)S(1)}, u32[]{:S(2)}, u32[]{:S(2)}) collective-permute-start(f32[9,4,48,128]{3,2,1,0:T(8,128)S(1)} %get-tuple-element.38.own), channel_id=1, source_target_pairs={{8,16},{16,8},{9,17},{17,9},{10,18},{18,10},{11,19},{19,11},{12,20... | collective-permute-start | bytes 2654216 | tf_op jit(solution)/shard_map/ppermute | solution.py:711
  20.2 0.7 collective-permute-start.2
  20.9 1.4 %collective-permute-start.3 = (f32[9,4,4,128]{3,2,1,0:T(4,128)S(1)}, f32[9,4,4,128]{3,2,1,0:T(4,128)S(1)}, u32[]{:S(2)}, u32[]{:S(2)}) collective-permute-start(f32[9,4,4,128]{3,2,1,0:T(4,128)S(1)} %get-tuple-element.43), channel_id=1, source_target_pairs={{1,2},{2,1},{3,4},{4,3},{5,6},{6,5},{7,0},{0,7},{9,10},{10,9},{11,... | collective-permute-start | bytes 221192 | tf_op jit(solution)/shard_map/ppermute | solution.py:713
  22.3 2.3 %collective-permute-done.2.part_a = f32[9,4,4,128]{3,2,1,0:T(4,128)S(1)} collective-permute-done((f32[9,4,4,128]{3,2,1,0:T(4,128)S(1)}, f32[9,4,4,128]{3,2,1,0:T(4,128)S(1)}, u32[]{:S(2)}, u32[]{:S(2)}) %collective-permute-start.2) | collective-permute-done | bytes 73760 | tf_op jit(solution)/shard_map/ppermute | solution.py:712
  24.6 3.5 %collective-permute-done.3.part_b = f32[9,4,4,128]{3,2,1,0:T(4,128)S(1)} collective-permute-done((f32[9,4,4,128]{3,2,1,0:T(4,128)S(1)}, f32[9,4,4,128]{3,2,1,0:T(4,128)S(1)}, u32[]{:S(2)}, u32[]{:S(2)}) %collective-permute-start.3) | collective-permute-done | bytes 73760 | tf_op jit(solution)/shard_map/ppermute | solution.py:713
  28.1 0.5 collective-permute-start.4
  28.6 0.7 collective-permute-start.5
  29.3 0.0 copy-done
  29.3 0.0 copy-done.1
  29.3 0.3 prepare.1.squares
  29.7 0.0 collective-permute-done.1.lat_a
  29.7 2.0 %near.2 = (f32[9,4,48,128]{3,2,1,0:T(8,128)S(1)}, f32[9,4,48,128]{3,2,1,0:T(8,128)S(1)}) custom-call(f32[9,4,48,128]{3,2,1,0:T(8,128)S(1)} %get-tuple-element.38.own, f32[9,4,48,128]{3,2,1,0:T(8,128)S(1)} %collective-permute-done.1.lat_a), custom_call_target="tpu_custom_call" | custom-call | tf_op jit(solution)/shard_map/near/pallas_call | solution.py:719
  31.6 0.0 collective-permute-done.lat_b
  31.6 0.7 %far.2 = (f32[9,4,48,128]{3,2,1,0:T(8,128)S(1)}, f32[9,4,48,128]{3,2,1,0:T(8,128)S(1)}) custom-call(f32[9,4,48,128]{3,2,1,0:T(8,128)S(1)} %collective-permute-done.lat_b, f32[9,4,48,128]{3,2,1,0:T(8,128)S(1)} %get-tuple-element.39.smooth_near, f32[9,4,48,128]{3,2,1,0:T(8,128)S(1)} %get-tuple-element.40.twice_near), custom_call_target="tpu_custom_call" | custom-call | tf_op jit(solution)/shard_map/far/pallas_call | solution.py:728
  32.4 0.0 collective-permute-done.5.corner_b
  32.4 0.0 collective-permute-done.4.corner_a
  32.4 2.4 %middle.1 = (f32[8,512]{1,0:T(8,128)S(1)}, f32[9,4,48,128]{3,2,1,0:T(8,128)S(1)}, f32[9,4,4,128]{3,2,1,0:T(4,128)S(1)}, f32[9,4,4,128]{3,2,1,0:T(4,128)S(1)}) custom-call(f32[9,4,48,128]{3,2,1,0:T(8,128)S(1)} %get-tuple-element.41.smooth, f32[9,4,8,128]{3,2,1,0:T(8,128)S(1)} %get-tuple-element.44.cross, ...), custom_call_target="tpu_custom_call" | custom-call | tf_op jit(solution)/shard_map/middle/pallas_call | solution.py:742
  34.8 4.2 %collective-permute-start.7 = (f32[9,4,48,128]{3,2,1,0:T(8,128)S(1)}, f32[9,4,48,128]{3,2,1,0:T(8,128)S(1)}, u32[]{:S(2)}, u32[]{:S(2)}) collective-permute-start(f32[9,4,48,128]{3,2,1,0:T(8,128)S(1)} %get-tuple-element.52.own), channel_id=1, source_target_pairs={{0,8},{8,0},{16,24},{24,16},{1,9},{9,1},{17,25},{25,17},{2,10},{10... | collective-permute-start | bytes 2654216 | tf_op jit(solution)/shard_map/ppermute | solution.py:714
  38.9 0.7 %collective-permute-start.6 = (f32[9,4,48,128]{3,2,1,0:T(8,128)S(1)}, f32[9,4,48,128]{3,2,1,0:T(8,128)S(1)}, u32[]{:S(2)}, u32[]{:S(2)}) collective-permute-start(f32[9,4,48,128]{3,2,1,0:T(8,128)S(1)} %get-tuple-element.52.own), channel_id=1, source_target_pairs={{8,16},{16,8},{9,17},{17,9},{10,18},{18,10},{11,19},{19,11},{12,20... | collective-permute-start | bytes 2654216 | tf_op jit(solution)/shard_map/ppermute | solution.py:711
  39.7 0.1 collective-permute-start.8
  39.7 1.5 %collective-permute-start.9 = (f32[9,4,4,128]{3,2,1,0:T(4,128)S(1)}, f32[9,4,4,128]{3,2,1,0:T(4,128)S(1)}, u32[]{:S(2)}, u32[]{:S(2)}) collective-permute-start(f32[9,4,4,128]{3,2,1,0:T(4,128)S(1)} %get-tuple-element.57), channel_id=1, source_target_pairs={{1,2},{2,1},{3,4},{4,3},{5,6},{6,5},{7,0},{0,7},{9,10},{10,9},{11,... | collective-permute-start | bytes 221192 | tf_op jit(solution)/shard_map/ppermute | solution.py:713
  41.2 2.9 %collective-permute-done.8.part_a = f32[9,4,4,128]{3,2,1,0:T(4,128)S(1)} collective-permute-done((f32[9,4,4,128]{3,2,1,0:T(4,128)S(1)}, f32[9,4,4,128]{3,2,1,0:T(4,128)S(1)}, u32[]{:S(2)}, u32[]{:S(2)}) %collective-permute-start.8) | collective-permute-done | bytes 73760 | tf_op jit(solution)/shard_map/ppermute | solution.py:712
  44.1 2.8 %collective-permute-done.9.part_b = f32[9,4,4,128]{3,2,1,0:T(4,128)S(1)} collective-permute-done((f32[9,4,4,128]{3,2,1,0:T(4,128)S(1)}, f32[9,4,4,128]{3,2,1,0:T(4,128)S(1)}, u32[]{:S(2)}, u32[]{:S(2)}) %collective-permute-start.9) | collective-permute-done | bytes 73760 | tf_op jit(solution)/shard_map/ppermute | solution.py:713
  46.9 0.8 %collective-permute-start.10 = (f32[9,4,8,128]{3,2,1,0:T(8,128)S(1)}, f32[9,4,8,128]{3,2,1,0:T(8,128)S(1)}, u32[]{:S(2)}, u32[]{:S(2)}) collective-permute-start(f32[9,4,8,128]{3,2,1,0:T(8,128)S(1)} %get-tuple-element.58.cross), channel_id=1, source_target_pairs={{0,8},{8,0},{16,24},{24,16},{1,9},{9,1},{17,25},{25,17},{2,10},{10... | collective-permute-start | bytes 442376 | tf_op jit(solution)/shard_map/ppermute | solution.py:717
  47.7 0.8 %collective-permute-start.11 = (f32[9,2,8,128]{3,2,1,0:T(8,128)S(1)}, f32[9,2,8,128]{3,2,1,0:T(8,128)S(1)}, u32[]{:S(2)}, u32[]{:S(2)}) collective-permute-start(f32[9,2,8,128]{3,2,1,0:T(8,128)S(1)} %get-tuple-element.59), channel_id=1, source_target_pairs={{8,16},{16,8},{9,17},{17,9},{10,18},{18,10},{11,19},{19,11},{12,20... | collective-permute-start | bytes 221192 | tf_op jit(solution)/shard_map/ppermute | solution.py:716
  48.5 0.0 collective-permute-done.7.lat_a
  48.5 2.0 %near.3 = (f32[9,4,48,128]{3,2,1,0:T(8,128)S(1)}, f32[9,4,48,128]{3,2,1,0:T(8,128)S(1)}) custom-call(f32[9,4,48,128]{3,2,1,0:T(8,128)S(1)} %get-tuple-element.52.own, f32[9,4,48,128]{3,2,1,0:T(8,128)S(1)} %collective-permute-done.7.lat_a), custom_call_target="tpu_custom_call" | custom-call | tf_op jit(solution)/shard_map/near/pallas_call | solution.py:719
  50.5 0.0 collective-permute-done.6.lat_b
  50.5 0.7 %far.3 = (f32[9,4,48,128]{3,2,1,0:T(8,128)S(1)}, f32[9,4,48,128]{3,2,1,0:T(8,128)S(1)}) custom-call(f32[9,4,48,128]{3,2,1,0:T(8,128)S(1)} %collective-permute-done.6.lat_b, f32[9,4,48,128]{3,2,1,0:T(8,128)S(1)} %get-tuple-element.53.smooth_near, f32[9,4,48,128]{3,2,1,0:T(8,128)S(1)} %get-tuple-element.54.twice_near), custom_call_target="tpu_custom_call" | custom-call | tf_op jit(solution)/shard_map/far/pallas_call | solution.py:728
  51.2 0.0 collective-permute-done.11.corner_b
  51.3 0.0 collective-permute-done.10.corner_a
  51.3 3.0 %last.1 = (f32[32,128]{1,0:T(8,128)}, f32[9,4,48,128]{3,2,1,0:T(8,128)S(1)}) custom-call(f32[9,4,48,128]{3,2,1,0:T(8,128)S(1)} %get-tuple-element.55.smooth, f32[9,4,8,128]{3,2,1,0:T(8,128)S(1)} %get-tuple-element.58.cross, f32[9,4,8,128]{3,2,1,0:T(8,128)S(1)} %collective-permute-done.10.corner_a, f32[9,2,8,128]{3,2,1,0:T(8,128)S(1)} %collective-permute-done.11.corner_b, ...), custom_call_target="tpu_custom_call" | custom-call | tf_op jit(solution)/shard_map/last/pallas_call | solution.py:761
  54.2 5.4 %all-to-all-start.1 = ((f32[32,1,128]{2,1,0:T(1,128)}), f32[32,1,128]{2,1,0:T(1,128)S(1)}, u32[]{:S(2)}, u32[]{:S(2)}) async-start(f32[32,1,128]{2,1,0:T(1,128)} %bitcast.10), calls=%async_computation.1 | async-start | bytes 32768 | tf_op jit(solution)/shard_map/all_to_all | solution.py:665
  59.7 1.5 %control.1.early = f32[9,4,48,128]{3,2,1,0:T(8,128)S(1)} custom-call(f32[9,4,48,128]{3,2,1,0:T(8,128)S(1)} %get-tuple-element.63.twice, f32[9,4,8,128]{3,2,1,0:T(8,128)S(1)} %get-tuple-element.44.cross, f32[9,4,8,128]{3,2,1,0:T(8,128)S(1)} %collective-permute-done.4.corner_a, f32[9,2,8,128]{3,2,1,0:T(8,128)S(1)} %collective-permute-done.5.corner_b, ...), custom_call_target="tpu_custom_call" | custom-call | tf_op jit(solution)/shard_map/control/pallas_call | solution.py:751
  61.1 5.6 %all-to-all-done.1 = f32[32,1,128]{2,1,0:T(1,128)S(1)} async-done(((f32[32,1,128]{2,1,0:T(1,128)}), f32[32,1,128]{2,1,0:T(1,128)S(1)}, u32[]{:S(2)}, u32[]{:S(2)}) %all-to-all-start.1) | async-done | bytes 16416 | tf_op jit(solution)/shard_map/all_to_all | solution.py:665
  66.7 2.2 %final.1 = (f32[4,48,128]{2,1,0:T(8,128)}, f32[8,4,48,128]{3,2,1,0:T(8,128)}, f32[1,256]{1,0:T(1,128)}) custom-call(f32[32,128]{1,0:T(8,128)S(1)} %bitcast.15, f32[9,4,48,128]{3,2,1,0:T(8,128)S(1)} %control.1.early, f32[9,4,48,128]{3,2,1,0:T(8,128)S(1)} %get-tuple-element.64.late, s32[1,256]{1,0:T(1,128)} %bitcast.19, s32[1,256]{1,0:T(1,128)} %get-tuple-element.65.lane_hbm), custom_call_target="tpu_custom_call" | custom-call | tf_op jit(solution)/shard_map/final/pallas_call | solution.py:791
  (2 shorter events, 0.1 us)
Async XLA Ops:
  2.8 26.5 %copy-start = (f32[128,128]{1,0:T(8,128)S(1)}, f32[128,128]{1,0:T(8,128)}, u32[]{:S(2)}) copy-start(f32[128,128]{1,0:T(8,128)} %vert_hbm.3) | copy-start | bytes 196612
  2.8 26.5 %copy-start.1 = (f32[128,128]{1,0:T(8,128)S(1)}, f32[128,128]{1,0:T(8,128)}, u32[]{:S(2)}) copy-start(f32[128,128]{1,0:T(8,128)} %static_hbm.3) | copy-start | bytes 196612
  19.4 10.3 %collective-permute-start.1 = (f32[9,4,48,128]{3,2,1,0:T(8,128)S(1)}, f32[9,4,48,128]{3,2,1,0:T(8,128)S(1)}, u32[]{:S(2)}, u32[]{:S(2)}) collective-permute-start(f32[9,4,48,128]{3,2,1,0:T(8,128)S(1)} %get-tuple-element.38.own), channel_id=1, source_target_pairs={{0,8},{8,0},{16,24},{24,16},{1,9},{9,1},{17,25},{25,17},{2,10},{10... | collective-permute-start | bytes 2654216 | tf_op jit(solution)/shard_map/ppermute | solution.py:714
  19.5 12.2 %collective-permute-start = (f32[9,4,48,128]{3,2,1,0:T(8,128)S(1)}, f32[9,4,48,128]{3,2,1,0:T(8,128)S(1)}, u32[]{:S(2)}, u32[]{:S(2)}) collective-permute-start(f32[9,4,48,128]{3,2,1,0:T(8,128)S(1)} %get-tuple-element.38.own), channel_id=1, source_target_pairs={{8,16},{16,8},{9,17},{17,9},{10,18},{18,10},{11,19},{19,11},{12,20... | collective-permute-start | bytes 2654216 | tf_op jit(solution)/shard_map/ppermute | solution.py:711
  20.2 4.4 %collective-permute-start.2 = (f32[9,4,4,128]{3,2,1,0:T(4,128)S(1)}, f32[9,4,4,128]{3,2,1,0:T(4,128)S(1)}, u32[]{:S(2)}, u32[]{:S(2)}) collective-permute-start(f32[9,4,4,128]{3,2,1,0:T(4,128)S(1)} %get-tuple-element.42), channel_id=1, source_target_pairs={{0,1},{1,0},{2,3},{3,2},{4,5},{5,4},{6,7},{7,6},{8,9},{9,8},{10,11... | collective-permute-start | bytes 221192 | tf_op jit(solution)/shard_map/ppermute | solution.py:712
  20.9 7.2 %collective-permute-start.3 = (f32[9,4,4,128]{3,2,1,0:T(4,128)S(1)}, f32[9,4,4,128]{3,2,1,0:T(4,128)S(1)}, u32[]{:S(2)}, u32[]{:S(2)}) collective-permute-start(f32[9,4,4,128]{3,2,1,0:T(4,128)S(1)} %get-tuple-element.43), channel_id=1, source_target_pairs={{1,2},{2,1},{3,4},{4,3},{5,6},{6,5},{7,0},{0,7},{9,10},{10,9},{11,... | collective-permute-start | bytes 221192 | tf_op jit(solution)/shard_map/ppermute | solution.py:713
  28.1 4.3 %collective-permute-start.4 = (f32[9,4,8,128]{3,2,1,0:T(8,128)S(1)}, f32[9,4,8,128]{3,2,1,0:T(8,128)S(1)}, u32[]{:S(2)}, u32[]{:S(2)}) collective-permute-start(f32[9,4,8,128]{3,2,1,0:T(8,128)S(1)} %get-tuple-element.44.cross), channel_id=1, source_target_pairs={{0,8},{8,0},{16,24},{24,16},{1,9},{9,1},{17,25},{25,17},{2,10},{10... | collective-permute-start | bytes 442376 | tf_op jit(solution)/shard_map/ppermute | solution.py:717
  28.6 3.7 %collective-permute-start.5 = (f32[9,2,8,128]{3,2,1,0:T(8,128)S(1)}, f32[9,2,8,128]{3,2,1,0:T(8,128)S(1)}, u32[]{:S(2)}, u32[]{:S(2)}) collective-permute-start(f32[9,2,8,128]{3,2,1,0:T(8,128)S(1)} %get-tuple-element.45), channel_id=1, source_target_pairs={{8,16},{16,8},{9,17},{17,9},{10,18},{18,10},{11,19},{19,11},{12,20... | collective-permute-start | bytes 221192 | tf_op jit(solution)/shard_map/ppermute | solution.py:716
  34.8 13.7 %collective-permute-start.7 = (f32[9,4,48,128]{3,2,1,0:T(8,128)S(1)}, f32[9,4,48,128]{3,2,1,0:T(8,128)S(1)}, u32[]{:S(2)}, u32[]{:S(2)}) collective-permute-start(f32[9,4,48,128]{3,2,1,0:T(8,128)S(1)} %get-tuple-element.52.own), channel_id=1, source_target_pairs={{0,8},{8,0},{16,24},{24,16},{1,9},{9,1},{17,25},{25,17},{2,10},{10... | collective-permute-start | bytes 2654216 | tf_op jit(solution)/shard_map/ppermute | solution.py:714
  38.9 11.5 %collective-permute-start.6 = (f32[9,4,48,128]{3,2,1,0:T(8,128)S(1)}, f32[9,4,48,128]{3,2,1,0:T(8,128)S(1)}, u32[]{:S(2)}, u32[]{:S(2)}) collective-permute-start(f32[9,4,48,128]{3,2,1,0:T(8,128)S(1)} %get-tuple-element.52.own), channel_id=1, source_target_pairs={{8,16},{16,8},{9,17},{17,9},{10,18},{18,10},{11,19},{19,11},{12,20... | collective-permute-start | bytes 2654216 | tf_op jit(solution)/shard_map/ppermute | solution.py:711
  39.7 4.4 %collective-permute-start.8 = (f32[9,4,4,128]{3,2,1,0:T(4,128)S(1)}, f32[9,4,4,128]{3,2,1,0:T(4,128)S(1)}, u32[]{:S(2)}, u32[]{:S(2)}) collective-permute-start(f32[9,4,4,128]{3,2,1,0:T(4,128)S(1)} %get-tuple-element.56), channel_id=1, source_target_pairs={{0,1},{1,0},{2,3},{3,2},{4,5},{5,4},{6,7},{7,6},{8,9},{9,8},{10,11... | collective-permute-start | bytes 221192 | tf_op jit(solution)/shard_map/ppermute | solution.py:712
  39.7 7.1 %collective-permute-start.9 = (f32[9,4,4,128]{3,2,1,0:T(4,128)S(1)}, f32[9,4,4,128]{3,2,1,0:T(4,128)S(1)}, u32[]{:S(2)}, u32[]{:S(2)}) collective-permute-start(f32[9,4,4,128]{3,2,1,0:T(4,128)S(1)} %get-tuple-element.57), channel_id=1, source_target_pairs={{1,2},{2,1},{3,4},{4,3},{5,6},{6,5},{7,0},{0,7},{9,10},{10,9},{11,... | collective-permute-start | bytes 221192 | tf_op jit(solution)/shard_map/ppermute | solution.py:713
  46.9 4.4 %collective-permute-start.10 = (f32[9,4,8,128]{3,2,1,0:T(8,128)S(1)}, f32[9,4,8,128]{3,2,1,0:T(8,128)S(1)}, u32[]{:S(2)}, u32[]{:S(2)}) collective-permute-start(f32[9,4,8,128]{3,2,1,0:T(8,128)S(1)} %get-tuple-element.58.cross), channel_id=1, source_target_pairs={{0,8},{8,0},{16,24},{24,16},{1,9},{9,1},{17,25},{25,17},{2,10},{10... | collective-permute-start | bytes 442376 | tf_op jit(solution)/shard_map/ppermute | solution.py:717
  47.7 3.6 %collective-permute-start.11 = (f32[9,2,8,128]{3,2,1,0:T(8,128)S(1)}, f32[9,2,8,128]{3,2,1,0:T(8,128)S(1)}, u32[]{:S(2)}, u32[]{:S(2)}) collective-permute-start(f32[9,2,8,128]{3,2,1,0:T(8,128)S(1)} %get-tuple-element.59), channel_id=1, source_target_pairs={{8,16},{16,8},{9,17},{17,9},{10,18},{18,10},{11,19},{19,11},{12,20... | collective-permute-start | bytes 221192 | tf_op jit(solution)/shard_map/ppermute | solution.py:716
  54.2 12.5 %all-to-all-start.1 = ((f32[32,1,128]{2,1,0:T(1,128)}), f32[32,1,128]{2,1,0:T(1,128)S(1)}, u32[]{:S(2)}, u32[]{:S(2)}) async-start(f32[32,1,128]{2,1,0:T(1,128)} %bitcast.10), calls=%async_computation.1 | async-start | bytes 32768 | tf_op jit(solution)/shard_map/all_to_all | solution.py:665

commit v7 on v6

--- a/solution.py
+++ b/solution.py
@@ -218,9 +218,10 @@
     wait_all(copies[:2])
     instruments = inst_vert.shape[0]
     onehot = (iota((instruments, total), 0) == feat[1:2].astype(jnp.int32)).astype(F32)
-    ivert[...] = dot(inst_vert[...].T, onehot)
+    onehot = jnp.concatenate([onehot.astype(BF16)] * 3, axis=0)
+    ivert[...] = short_dot(jnp.concatenate(thirds(inst_vert[...].T), axis=1), onehot)
     inverse = jnp.broadcast_to(1.0 / (inst_err[...] * inst_err[...]), (8, instruments))
-    rinv = dot(inverse, onehot)[0:1]
+    rinv = short_dot(jnp.concatenate(thirds(inverse), axis=1), onehot)[0:1]
     feat[6:7] = feat[6:7] * rinv
     feat[7:8] = rinv
     fill_weights(feat, weights, high_weights, low_weights, windows, rows_lat, rows_lon)

time: 69.6 us -> 69.4 us (level)
  no operation moved by 1% of the time
where the time goes in v7:
time: 69.4 us; the launch traced here: 69 us
  Pallas kernels  18.5 us (27%)
  starting transfers between devices  17.5 us (25%)
  waiting for transfers between devices  17.1 us (25%)
  blocking collectives  14.3 us (21%)
  between operations  1.67 us (2%)
    all_to_all x1, blocking collectives, exchange(): lax.all_to_all(blocks, ('lat', 'lon'), split_axis=0, concat_axis=0, tiled...  14.3 us
    ppermute x2, waiting for transfers between devices, halo(): side_b = lax.ppermute(edge_b, 'lon', lon_outer)  6.23 us
    all_to_all x1, waiting for transfers between devices, exchange(): lax.all_to_all(blocks, ('lat', 'lon'), split_axis=0, concat_axis=0, tiled...  5.6 us
    all_to_all x1, starting transfers between devices, exchange(): lax.all_to_all(blocks, ('lat', 'lon'), split_axis=0, concat_axis=0, tiled...  5.42 us
    ppermute x2, waiting for transfers between devices, halo(): side_a = lax.ppermute(edge_a, 'lon', lon_inner)  5.22 us
    ppermute x2, starting transfers between devices, halo(): lat_a = lax.ppermute(fields, 'lat', lat_inner)  4.23 us
    pallas_call x2, Pallas kernels, halo(): pl.pallas_call(near_kernel, out_shape=(tile, tile), in_specs=[VMEM] * 2,...  3.93 us
    pallas_call x1, Pallas kernels, body(): pl.pallas_call(functools.partial(last_kernel, slots), out_shape=(shape(ow...  2.97 us
  transfers between devices with their start and end apart: 13, of which 5 were waited for; matrix products, arithmetic and copies ran while one was open for 0% of the time, Pallas kernels for 11%

profile of v7, /device:TPU:0, one launch (start us, length us, event | category | flops | bytes accessed | tf_op | source)
XLA Modules:
  0.0 69.0 jit_solution(5785695486334192352)
XLA Ops:
  1.3 1.5 %pack.1 = (f32[32,128]{1,0:T(8,128)S(1)}, s32[1,256]{1,0:T(1,128)}, bf16[4,4,4,48,128]{4,3,2,1,0:T(8,128)(2,1)S(1)}) custom-call(s32[1,256]{1,0:T(1,128)} %bitcast.18, s32[1,256]{1,0:T(1,128)} %bitcast.20, s32[1,256]{1,0:T(1,128)} %bitcast.21, s32[1,256]{1,0:T(1,128)} %bitcast.22, f32[4,256]{1,0:T(4,128)} %hweight_hbm.1, f32[1,256]{1,0:T(1,128)} %bitcast.23, ...), custom_call_target="tpu_custom_call" | custom-call | tf_op jit(solution)/shard_map/pack/pallas_call | solution.py:626
  2.8 0.0 copy-start
  2.8 0.0 copy-start.1
  2.9 14.3 %all_to_all.22 = f32[32,1,128]{2,1,0:T(1,128)S(1)} all-to-all(f32[32,1,128]{2,1,0:T(1,128)S(1)} %bitcast.17), channel_id=1, replica_groups=mesh['lat'=4,'lon'=8] {'lat','lon'}, dimensions={0} | all-to-all | bytes 32768 | tf_op jit(solution)/shard_map/all_to_all | solution.py:666
  17.1 2.1 %first.1 = (f32[8,512]{1,0:T(8,128)S(1)}, f32[128,512]{1,0:T(8,128)S(1)}, bf16[4,4,4,48,128]{4,3,2,1,0:T(8,128)(2,1)S(1)}, f32[768,512]{1,0:T(8,128)S(1)}, bf16[...) custom-call(f32[32,128]{1,0:T(8,128)S(1)} %bitcast.16, ...), custom_call_target="tpu_custom_call" | custom-call | tf_op jit(solution)/shard_map/first/pallas_call | solution.py:673
  19.3 0.1 collective-permute-start.1
  19.3 0.7 %collective-permute-start = (f32[9,4,48,128]{3,2,1,0:T(8,128)S(1)}, f32[9,4,48,128]{3,2,1,0:T(8,128)S(1)}, u32[]{:S(2)}, u32[]{:S(2)}) collective-permute-start(f32[9,4,48,128]{3,2,1,0:T(8,128)S(1)} %get-tuple-element.38.own), channel_id=1, source_target_pairs={{8,16},{16,8},{9,17},{17,9},{10,18},{18,10},{11,19},{19,11},{12,20... | collective-permute-start | bytes 2654216 | tf_op jit(solution)/shard_map/ppermute | solution.py:712
  20.1 0.7 collective-permute-start.2
  20.7 1.4 %collective-permute-start.3 = (f32[9,4,4,128]{3,2,1,0:T(4,128)S(1)}, f32[9,4,4,128]{3,2,1,0:T(4,128)S(1)}, u32[]{:S(2)}, u32[]{:S(2)}) collective-permute-start(f32[9,4,4,128]{3,2,1,0:T(4,128)S(1)} %get-tuple-element.43), channel_id=1, source_target_pairs={{1,2},{2,1},{3,4},{4,3},{5,6},{6,5},{7,0},{0,7},{9,10},{10,9},{11,... | collective-permute-start | bytes 221192 | tf_op jit(solution)/shard_map/ppermute | solution.py:714
  22.1 2.3 %collective-permute-done.2.part_a = f32[9,4,4,128]{3,2,1,0:T(4,128)S(1)} collective-permute-done((f32[9,4,4,128]{3,2,1,0:T(4,128)S(1)}, f32[9,4,4,128]{3,2,1,0:T(4,128)S(1)}, u32[]{:S(2)}, u32[]{:S(2)}) %collective-permute-start.2) | collective-permute-done | bytes 73760 | tf_op jit(solution)/shard_map/ppermute | solution.py:713
  24.5 3.5 %collective-permute-done.3.part_b = f32[9,4,4,128]{3,2,1,0:T(4,128)S(1)} collective-permute-done((f32[9,4,4,128]{3,2,1,0:T(4,128)S(1)}, f32[9,4,4,128]{3,2,1,0:T(4,128)S(1)}, u32[]{:S(2)}, u32[]{:S(2)}) %collective-permute-start.3) | collective-permute-done | bytes 73760 | tf_op jit(solution)/shard_map/ppermute | solution.py:714
  28.0 0.5 collective-permute-start.4
  28.5 0.7 collective-permute-start.5
  29.2 0.0 copy-done
  29.2 0.0 copy-done.1
  29.2 0.3 prepare.1.squares
  29.5 0.0 collective-permute-done.1.lat_a
  29.5 2.0 %near.2 = (f32[9,4,48,128]{3,2,1,0:T(8,128)S(1)}, f32[9,4,48,128]{3,2,1,0:T(8,128)S(1)}) custom-call(f32[9,4,48,128]{3,2,1,0:T(8,128)S(1)} %get-tuple-element.38.own, f32[9,4,48,128]{3,2,1,0:T(8,128)S(1)} %collective-permute-done.1.lat_a), custom_call_target="tpu_custom_call" | custom-call | tf_op jit(solution)/shard_map/near/pallas_call | solution.py:720
  31.5 0.0 collective-permute-done.lat_b
  31.5 0.7 %far.2 = (f32[9,4,48,128]{3,2,1,0:T(8,128)S(1)}, f32[9,4,48,128]{3,2,1,0:T(8,128)S(1)}) custom-call(f32[9,4,48,128]{3,2,1,0:T(8,128)S(1)} %collective-permute-done.lat_b, f32[9,4,48,128]{3,2,1,0:T(8,128)S(1)} %get-tuple-element.39.smooth_near, f32[9,4,48,128]{3,2,1,0:T(8,128)S(1)} %get-tuple-element.40.twice_near), custom_call_target="tpu_custom_call" | custom-call | tf_op jit(solution)/shard_map/far/pallas_call | solution.py:729
  32.3 0.0 collective-permute-done.5.corner_b
  32.3 0.0 collective-permute-done.4.corner_a
  32.3 2.4 %middle.1 = (f32[8,512]{1,0:T(8,128)S(1)}, f32[9,4,48,128]{3,2,1,0:T(8,128)S(1)}, f32[9,4,4,128]{3,2,1,0:T(4,128)S(1)}, f32[9,4,4,128]{3,2,1,0:T(4,128)S(1)}) custom-call(f32[9,4,48,128]{3,2,1,0:T(8,128)S(1)} %get-tuple-element.41.smooth, f32[9,4,8,128]{3,2,1,0:T(8,128)S(1)} %get-tuple-element.44.cross, ...), custom_call_target="tpu_custom_call" | custom-call | tf_op jit(solution)/shard_map/middle/pallas_call | solution.py:743
  34.6 4.2 %collective-permute-start.7 = (f32[9,4,48,128]{3,2,1,0:T(8,128)S(1)}, f32[9,4,48,128]{3,2,1,0:T(8,128)S(1)}, u32[]{:S(2)}, u32[]{:S(2)}) collective-permute-start(f32[9,4,48,128]{3,2,1,0:T(8,128)S(1)} %get-tuple-element.52.own), channel_id=1, source_target_pairs={{0,8},{8,0},{16,24},{24,16},{1,9},{9,1},{17,25},{25,17},{2,10},{10... | collective-permute-start | bytes 2654216 | tf_op jit(solution)/shard_map/ppermute | solution.py:715
  38.8 0.7 %collective-permute-start.6 = (f32[9,4,48,128]{3,2,1,0:T(8,128)S(1)}, f32[9,4,48,128]{3,2,1,0:T(8,128)S(1)}, u32[]{:S(2)}, u32[]{:S(2)}) collective-permute-start(f32[9,4,48,128]{3,2,1,0:T(8,128)S(1)} %get-tuple-element.52.own), channel_id=1, source_target_pairs={{8,16},{16,8},{9,17},{17,9},{10,18},{18,10},{11,19},{19,11},{12,20... | collective-permute-start | bytes 2654216 | tf_op jit(solution)/shard_map/ppermute | solution.py:712
  39.5 0.1 collective-permute-start.8
  39.6 1.5 %collective-permute-start.9 = (f32[9,4,4,128]{3,2,1,0:T(4,128)S(1)}, f32[9,4,4,128]{3,2,1,0:T(4,128)S(1)}, u32[]{:S(2)}, u32[]{:S(2)}) collective-permute-start(f32[9,4,4,128]{3,2,1,0:T(4,128)S(1)} %get-tuple-element.57), channel_id=1, source_target_pairs={{1,2},{2,1},{3,4},{4,3},{5,6},{6,5},{7,0},{0,7},{9,10},{10,9},{11,... | collective-permute-start | bytes 221192 | tf_op jit(solution)/shard_map/ppermute | solution.py:714
  41.1 2.9 %collective-permute-done.8.part_a = f32[9,4,4,128]{3,2,1,0:T(4,128)S(1)} collective-permute-done((f32[9,4,4,128]{3,2,1,0:T(4,128)S(1)}, f32[9,4,4,128]{3,2,1,0:T(4,128)S(1)}, u32[]{:S(2)}, u32[]{:S(2)}) %collective-permute-start.8) | collective-permute-done | bytes 73760 | tf_op jit(solution)/shard_map/ppermute | solution.py:713
  43.9 2.8 %collective-permute-done.9.part_b = f32[9,4,4,128]{3,2,1,0:T(4,128)S(1)} collective-permute-done((f32[9,4,4,128]{3,2,1,0:T(4,128)S(1)}, f32[9,4,4,128]{3,2,1,0:T(4,128)S(1)}, u32[]{:S(2)}, u32[]{:S(2)}) %collective-permute-start.9) | collective-permute-done | bytes 73760 | tf_op jit(solution)/shard_map/ppermute | solution.py:714
  46.8 0.8 %collective-permute-start.10 = (f32[9,4,8,128]{3,2,1,0:T(8,128)S(1)}, f32[9,4,8,128]{3,2,1,0:T(8,128)S(1)}, u32[]{:S(2)}, u32[]{:S(2)}) collective-permute-start(f32[9,4,8,128]{3,2,1,0:T(8,128)S(1)} %get-tuple-element.58.cross), channel_id=1, source_target_pairs={{0,8},{8,0},{16,24},{24,16},{1,9},{9,1},{17,25},{25,17},{2,10},{10... | collective-permute-start | bytes 442376 | tf_op jit(solution)/shard_map/ppermute | solution.py:718
  47.5 0.8 %collective-permute-start.11 = (f32[9,2,8,128]{3,2,1,0:T(8,128)S(1)}, f32[9,2,8,128]{3,2,1,0:T(8,128)S(1)}, u32[]{:S(2)}, u32[]{:S(2)}) collective-permute-start(f32[9,2,8,128]{3,2,1,0:T(8,128)S(1)} %get-tuple-element.59), channel_id=1, source_target_pairs={{8,16},{16,8},{9,17},{17,9},{10,18},{18,10},{11,19},{19,11},{12,20... | collective-permute-start | bytes 221192 | tf_op jit(solution)/shard_map/ppermute | solution.py:717
  48.4 0.0 collective-permute-done.7.lat_a
  48.4 2.0 %near.3 = (f32[9,4,48,128]{3,2,1,0:T(8,128)S(1)}, f32[9,4,48,128]{3,2,1,0:T(8,128)S(1)}) custom-call(f32[9,4,48,128]{3,2,1,0:T(8,128)S(1)} %get-tuple-element.52.own, f32[9,4,48,128]{3,2,1,0:T(8,128)S(1)} %collective-permute-done.7.lat_a), custom_call_target="tpu_custom_call" | custom-call | tf_op jit(solution)/shard_map/near/pallas_call | solution.py:720
  50.4 0.0 collective-permute-done.6.lat_b
  50.4 0.7 %far.3 = (f32[9,4,48,128]{3,2,1,0:T(8,128)S(1)}, f32[9,4,48,128]{3,2,1,0:T(8,128)S(1)}) custom-call(f32[9,4,48,128]{3,2,1,0:T(8,128)S(1)} %collective-permute-done.6.lat_b, f32[9,4,48,128]{3,2,1,0:T(8,128)S(1)} %get-tuple-element.53.smooth_near, f32[9,4,48,128]{3,2,1,0:T(8,128)S(1)} %get-tuple-element.54.twice_near), custom_call_target="tpu_custom_call" | custom-call | tf_op jit(solution)/shard_map/far/pallas_call | solution.py:729
  51.1 0.0 collective-permute-done.11.corner_b
  51.1 0.0 collective-permute-done.10.corner_a
  51.1 3.0 %last.1 = (f32[32,128]{1,0:T(8,128)}, f32[9,4,48,128]{3,2,1,0:T(8,128)S(1)}) custom-call(f32[9,4,48,128]{3,2,1,0:T(8,128)S(1)} %get-tuple-element.55.smooth, f32[9,4,8,128]{3,2,1,0:T(8,128)S(1)} %get-tuple-element.58.cross, f32[9,4,8,128]{3,2,1,0:T(8,128)S(1)} %collective-permute-done.10.corner_a, f32[9,2,8,128]{3,2,1,0:T(8,128)S(1)} %collective-permute-done.11.corner_b, ...), custom_call_target="tpu_custom_call" | custom-call | tf_op jit(solution)/shard_map/last/pallas_call | solution.py:762
  54.1 5.4 %all-to-all-start.1 = ((f32[32,1,128]{2,1,0:T(1,128)}), f32[32,1,128]{2,1,0:T(1,128)S(1)}, u32[]{:S(2)}, u32[]{:S(2)}) async-start(f32[32,1,128]{2,1,0:T(1,128)} %bitcast.10), calls=%async_computation.1 | async-start | bytes 32768 | tf_op jit(solution)/shard_map/all_to_all | solution.py:666
  59.5 1.5 %control.1.early = f32[9,4,48,128]{3,2,1,0:T(8,128)S(1)} custom-call(f32[9,4,48,128]{3,2,1,0:T(8,128)S(1)} %get-tuple-element.63.twice, f32[9,4,8,128]{3,2,1,0:T(8,128)S(1)} %get-tuple-element.44.cross, f32[9,4,8,128]{3,2,1,0:T(8,128)S(1)} %collective-permute-done.4.corner_a, f32[9,2,8,128]{3,2,1,0:T(8,128)S(1)} %collective-permute-done.5.corner_b, ...), custom_call_target="tpu_custom_call" | custom-call | tf_op jit(solution)/shard_map/control/pallas_call | solution.py:752
  61.0 5.6 %all-to-all-done.1 = f32[32,1,128]{2,1,0:T(1,128)S(1)} async-done(((f32[32,1,128]{2,1,0:T(1,128)}), f32[32,1,128]{2,1,0:T(1,128)S(1)}, u32[]{:S(2)}, u32[]{:S(2)}) %all-to-all-start.1) | async-done | bytes 16416 | tf_op jit(solution)/shard_map/all_to_all | solution.py:666
  66.6 2.2 %final.1 = (f32[4,48,128]{2,1,0:T(8,128)}, f32[8,4,48,128]{3,2,1,0:T(8,128)}, f32[1,256]{1,0:T(1,128)}) custom-call(f32[32,128]{1,0:T(8,128)S(1)} %bitcast.15, f32[9,4,48,128]{3,2,1,0:T(8,128)S(1)} %control.1.early, f32[9,4,48,128]{3,2,1,0:T(8,128)S(1)} %get-tuple-element.64.late, s32[1,256]{1,0:T(1,128)} %bitcast.19, s32[1,256]{1,0:T(1,128)} %get-tuple-element.65.lane_hbm), custom_call_target="tpu_custom_call" | custom-call | tf_op jit(solution)/shard_map/final/pallas_call | solution.py:792
  (2 shorter events, 0.1 us)
Async XLA Ops:
  2.8 26.3 %copy-start = (f32[128,128]{1,0:T(8,128)S(1)}, f32[128,128]{1,0:T(8,128)}, u32[]{:S(2)}) copy-start(f32[128,128]{1,0:T(8,128)} %vert_hbm.3) | copy-start | bytes 196612
  2.8 26.3 %copy-start.1 = (f32[128,128]{1,0:T(8,128)S(1)}, f32[128,128]{1,0:T(8,128)}, u32[]{:S(2)}) copy-start(f32[128,128]{1,0:T(8,128)} %static_hbm.3) | copy-start | bytes 196612
  19.3 10.3 %collective-permute-start.1 = (f32[9,4,48,128]{3,2,1,0:T(8,128)S(1)}, f32[9,4,48,128]{3,2,1,0:T(8,128)S(1)}, u32[]{:S(2)}, u32[]{:S(2)}) collective-permute-start(f32[9,4,48,128]{3,2,1,0:T(8,128)S(1)} %get-tuple-element.38.own), channel_id=1, source_target_pairs={{0,8},{8,0},{16,24},{24,16},{1,9},{9,1},{17,25},{25,17},{2,10},{10... | collective-permute-start | bytes 2654216 | tf_op jit(solution)/shard_map/ppermute | solution.py:715
  19.3 12.2 %collective-permute-start = (f32[9,4,48,128]{3,2,1,0:T(8,128)S(1)}, f32[9,4,48,128]{3,2,1,0:T(8,128)S(1)}, u32[]{:S(2)}, u32[]{:S(2)}) collective-permute-start(f32[9,4,48,128]{3,2,1,0:T(8,128)S(1)} %get-tuple-element.38.own), channel_id=1, source_target_pairs={{8,16},{16,8},{9,17},{17,9},{10,18},{18,10},{11,19},{19,11},{12,20... | collective-permute-start | bytes 2654216 | tf_op jit(solution)/shard_map/ppermute | solution.py:712
  20.1 4.4 %collective-permute-start.2 = (f32[9,4,4,128]{3,2,1,0:T(4,128)S(1)}, f32[9,4,4,128]{3,2,1,0:T(4,128)S(1)}, u32[]{:S(2)}, u32[]{:S(2)}) collective-permute-start(f32[9,4,4,128]{3,2,1,0:T(4,128)S(1)} %get-tuple-element.42), channel_id=1, source_target_pairs={{0,1},{1,0},{2,3},{3,2},{4,5},{5,4},{6,7},{7,6},{8,9},{9,8},{10,11... | collective-permute-start | bytes 221192 | tf_op jit(solution)/shard_map/ppermute | solution.py:713
  20.7 7.2 %collective-permute-start.3 = (f32[9,4,4,128]{3,2,1,0:T(4,128)S(1)}, f32[9,4,4,128]{3,2,1,0:T(4,128)S(1)}, u32[]{:S(2)}, u32[]{:S(2)}) collective-permute-start(f32[9,4,4,128]{3,2,1,0:T(4,128)S(1)} %get-tuple-element.43), channel_id=1, source_target_pairs={{1,2},{2,1},{3,4},{4,3},{5,6},{6,5},{7,0},{0,7},{9,10},{10,9},{11,... | collective-permute-start | bytes 221192 | tf_op jit(solution)/shard_map/ppermute | solution.py:714
  28.0 4.3 %collective-permute-start.4 = (f32[9,4,8,128]{3,2,1,0:T(8,128)S(1)}, f32[9,4,8,128]{3,2,1,0:T(8,128)S(1)}, u32[]{:S(2)}, u32[]{:S(2)}) collective-permute-start(f32[9,4,8,128]{3,2,1,0:T(8,128)S(1)} %get-tuple-element.44.cross), channel_id=1, source_target_pairs={{0,8},{8,0},{16,24},{24,16},{1,9},{9,1},{17,25},{25,17},{2,10},{10... | collective-permute-start | bytes 442376 | tf_op jit(solution)/shard_map/ppermute | solution.py:718
  28.5 3.7 %collective-permute-start.5 = (f32[9,2,8,128]{3,2,1,0:T(8,128)S(1)}, f32[9,2,8,128]{3,2,1,0:T(8,128)S(1)}, u32[]{:S(2)}, u32[]{:S(2)}) collective-permute-start(f32[9,2,8,128]{3,2,1,0:T(8,128)S(1)} %get-tuple-element.45), channel_id=1, source_target_pairs={{8,16},{16,8},{9,17},{17,9},{10,18},{18,10},{11,19},{19,11},{12,20... | collective-permute-start | bytes 221192 | tf_op jit(solution)/shard_map/ppermute | solution.py:717
  34.6 13.7 %collective-permute-start.7 = (f32[9,4,48,128]{3,2,1,0:T(8,128)S(1)}, f32[9,4,48,128]{3,2,1,0:T(8,128)S(1)}, u32[]{:S(2)}, u32[]{:S(2)}) collective-permute-start(f32[9,4,48,128]{3,2,1,0:T(8,128)S(1)} %get-tuple-element.52.own), channel_id=1, source_target_pairs={{0,8},{8,0},{16,24},{24,16},{1,9},{9,1},{17,25},{25,17},{2,10},{10... | collective-permute-start | bytes 2654216 | tf_op jit(solution)/shard_map/ppermute | solution.py:715
  38.8 11.6 %collective-permute-start.6 = (f32[9,4,48,128]{3,2,1,0:T(8,128)S(1)}, f32[9,4,48,128]{3,2,1,0:T(8,128)S(1)}, u32[]{:S(2)}, u32[]{:S(2)}) collective-permute-start(f32[9,4,48,128]{3,2,1,0:T(8,128)S(1)} %get-tuple-element.52.own), channel_id=1, source_target_pairs={{8,16},{16,8},{9,17},{17,9},{10,18},{18,10},{11,19},{19,11},{12,20... | collective-permute-start | bytes 2654216 | tf_op jit(solution)/shard_map/ppermute | solution.py:712
  39.5 4.4 %collective-permute-start.8 = (f32[9,4,4,128]{3,2,1,0:T(4,128)S(1)}, f32[9,4,4,128]{3,2,1,0:T(4,128)S(1)}, u32[]{:S(2)}, u32[]{:S(2)}) collective-permute-start(f32[9,4,4,128]{3,2,1,0:T(4,128)S(1)} %get-tuple-element.56), channel_id=1, source_target_pairs={{0,1},{1,0},{2,3},{3,2},{4,5},{5,4},{6,7},{7,6},{8,9},{9,8},{10,11... | collective-permute-start | bytes 221192 | tf_op jit(solution)/shard_map/ppermute | solution.py:713
  39.6 7.1 %collective-permute-start.9 = (f32[9,4,4,128]{3,2,1,0:T(4,128)S(1)}, f32[9,4,4,128]{3,2,1,0:T(4,128)S(1)}, u32[]{:S(2)}, u32[]{:S(2)}) collective-permute-start(f32[9,4,4,128]{3,2,1,0:T(4,128)S(1)} %get-tuple-element.57), channel_id=1, source_target_pairs={{1,2},{2,1},{3,4},{4,3},{5,6},{6,5},{7,0},{0,7},{9,10},{10,9},{11,... | collective-permute-start | bytes 221192 | tf_op jit(solution)/shard_map/ppermute | solution.py:714
  46.8 4.4 %collective-permute-start.10 = (f32[9,4,8,128]{3,2,1,0:T(8,128)S(1)}, f32[9,4,8,128]{3,2,1,0:T(8,128)S(1)}, u32[]{:S(2)}, u32[]{:S(2)}) collective-permute-start(f32[9,4,8,128]{3,2,1,0:T(8,128)S(1)} %get-tuple-element.58.cross), channel_id=1, source_target_pairs={{0,8},{8,0},{16,24},{24,16},{1,9},{9,1},{17,25},{25,17},{2,10},{10... | collective-permute-start | bytes 442376 | tf_op jit(solution)/shard_map/ppermute | solution.py:718
  47.5 3.6 %collective-permute-start.11 = (f32[9,2,8,128]{3,2,1,0:T(8,128)S(1)}, f32[9,2,8,128]{3,2,1,0:T(8,128)S(1)}, u32[]{:S(2)}, u32[]{:S(2)}) collective-permute-start(f32[9,2,8,128]{3,2,1,0:T(8,128)S(1)} %get-tuple-element.59), channel_id=1, source_target_pairs={{8,16},{16,8},{9,17},{17,9},{10,18},{18,10},{11,19},{19,11},{12,20... | collective-permute-start | bytes 221192 | tf_op jit(solution)/shard_map/ppermute | solution.py:717
  54.1 12.5 %all-to-all-start.1 = ((f32[32,1,128]{2,1,0:T(1,128)}), f32[32,1,128]{2,1,0:T(1,128)S(1)}, u32[]{:S(2)}, u32[]{:S(2)}) async-start(f32[32,1,128]{2,1,0:T(1,128)} %bitcast.10), calls=%async_computation.1 | async-start | bytes 32768 | tf_op jit(solution)/shard_map/all_to_all | solution.py:666
